TPU v7x, 256 devices: a whole 4x4x8 slice. The times are simulated.
256 devices in a mesh: seq: 64 (over x, z_lo, y, core), tensor: 4 (over z_hi).
Axes of the slice: x: 4, y: 4, z: 8 (z_hi: 4, z_lo: 2; z = z_hi * 2 + z_lo), core: 2. Of those that a mesh axis runs over, the one named last changes fastest.
Arguments:
- q_tok: bfloat16 [32768, 1536], P('seq', 'tensor'), may hold values from -24 to 24
- k_tok: bfloat16 [32768, 1536], P('seq', 'tensor'), may hold values from -6 to 6
- v_tok: bfloat16 [32768, 1536], P('seq', 'tensor'), may hold values from -16 to 16
- ref_hidden: bfloat16 [2048, 3072], P('seq', 'tensor'), may hold values from -16 to 16
- ref_wk: bfloat16 [3072, 1536], P('tensor'), may hold values from -0.109375 to 0.109375
- ref_wv: bfloat16 [3072, 1536], P('tensor'), may hold values from -0.109375 to 0.109375
- key_gain: float32 [128], replicated, may hold values from 1 to 2
Outputs:
- attended: bfloat16 [32768, 1536], P('seq', 'tensor')
All inputs are finite; a program needn't handle non-finite values.
Results may differ from a plain program's by a relative error of at most 0.022.
Values may be sent and summed in bfloat16 or wider, within the bound.
No kernel may reach another device: no remote copies, remote signals or barrier semaphores. Data moves between devices by JAX's collectives and lax.ppermute only.
A program may use at most 128 MiB of HBM per device.

v0:
```python
import jax
import jax.numpy as jnp
from jax import lax
from jax.sharding import PartitionSpec as P

HD = 128
VIEW_LEN = 4096


EPSILON = 1e-06


def from_partner(block, axis, apart):
    count = lax.axis_size(axis)
    route = []
    for low in range(count):
        high = low | 1 << apart
        if high != low and high < count:
            route += [(low, high), (high, low)]
    return lax.ppermute(block, axis, route)


def attend(carried, queries, key_rows, values):
    running_max, running_sum, weighted = carried
    head_count = queries.shape[1] // HD
    factor = HD ** (-0.5)
    new_maxes, new_sums, new_weighted = ([], [], [])
    for head_index in range(head_count):
        col_start = head_index * HD
        col_stop = col_start + HD
        scores = (
            jnp.einsum(
                "qd,kd->qk",
                queries[:, col_start:col_stop],
                key_rows[:, col_start:col_stop],
                preferred_element_type=jnp.float32,
            )
            * factor
        )
        raised = jnp.maximum(running_max[head_index], jnp.max(scores, axis=1))
        rescale = jnp.exp(running_max[head_index] - raised)
        weights = jnp.exp(scores - raised[:, None])
        new_sums.append(running_sum[head_index] * rescale + jnp.sum(weights, axis=1))
        product = jnp.dot(
            weights.astype(jnp.bfloat16),
            values[:, col_start:col_stop],
            preferred_element_type=jnp.float32,
        )
        new_weighted.append(weighted[:, col_start:col_stop] * rescale[:, None] + product)
        new_maxes.append(raised)
    return (jnp.stack(new_maxes), jnp.stack(new_sums), jnp.concatenate(new_weighted, axis=1))


def reference_pair(ref_hidden, ref_wk, ref_wv, key_gain):
    k_partial = jnp.dot(ref_hidden, ref_wk, preferred_element_type=jnp.float32)
    v_partial = jnp.dot(ref_hidden, ref_wv, preferred_element_type=jnp.float32)
    row_count = ref_hidden.shape[0]
    groups = lax.axis_size("tensor")
    group_width = k_partial.shape[1] // groups
    stacked = jnp.stack(
        (
            k_partial.reshape(row_count, groups, group_width),
            v_partial.reshape(row_count, groups, group_width),
        ),
        axis=2,
    ).reshape(row_count, 2 * groups * group_width)
    summed = lax.psum_scatter(
        stacked.astype(jnp.bfloat16), "tensor", scatter_dimension=1, tiled=True
    ).astype(jnp.float32)
    raw_keys = summed[:, :group_width].reshape(row_count, group_width // HD, HD)
    normed = (
        raw_keys
        * lax.rsqrt(jnp.mean(raw_keys * raw_keys, axis=2, keepdims=True) + EPSILON)
        * key_gain
    )
    return (
        normed.reshape(row_count, group_width).astype(jnp.bfloat16),
        summed[:, group_width:].astype(jnp.bfloat16),
    )


def per_device(q_tok, k_tok, v_tok, ref_hidden, ref_wk, ref_wv, key_gain):
    ref_keys, ref_vals = reference_pair(ref_hidden, ref_wk, ref_wv, key_gain)
    query_rows = q_tok.shape[0]
    heads_here = q_tok.shape[1] // HD
    group_size = VIEW_LEN // query_rows
    view_bits = group_size.bit_length() - 1
    initial = (
        jnp.full((heads_here, query_rows), -jnp.inf, jnp.float32),
        jnp.zeros((heads_here, query_rows), jnp.float32),
        jnp.zeros(q_tok.shape, jnp.float32),
    )
    view_keys, view_vals = (k_tok, v_tok)
    for bit_index in range(view_bits):
        other_keys, other_vals = from_partner((view_keys, view_vals), "seq", bit_index)
        view_keys = jnp.concatenate((view_keys, other_keys), axis=0)
        view_vals = jnp.concatenate((view_vals, other_vals), axis=0)
    carried = attend(initial, q_tok, view_keys, view_vals)
    carried = attend(
        carried,
        q_tok,
        lax.all_gather(ref_keys, "seq", axis=0, tiled=True),
        lax.all_gather(ref_vals, "seq", axis=0, tiled=True),
    )
    running_max, running_sum, weighted = carried
    spread = jnp.repeat(running_sum.T, HD, axis=1)
    return (weighted / spread).astype(jnp.bfloat16)


def solution(mesh):
    placed = (
        P("seq", "tensor"),
        P("seq", "tensor"),
        P("seq", "tensor"),
        P("seq", "tensor"),
        P("tensor", None),
        P("tensor", None),
        P(),
    )
    return jax.shard_map(
        per_device, mesh=mesh, in_specs=placed, out_specs=P("seq", "tensor"), check_vma=False
    )
```

profile of v0, /device:TPU:1, one launch (start us, length us, event | category | flops | bytes accessed | tf_op | source)
XLA Modules:
  0.0 341.4 jit_solution(11778259846070906958)
XLA Ops:
  6.6 1.6 copy-done
  9.6 2.2 convolution_convert_fusion
  13.2 27.0 %reduce-scatter.2.cloned.1.call-done = bf16[32,768]{1,0:T(8,128)(2,1)} async-done(((bf16[32,3072]{1,0:T(8,128)(2,1)}), bf16[32,768]{1,0:T(8,128)(2,1)}) %reduce-scatter.2.cloned.1.call-update) | async-done | bytes 49168 | tf_op jit(solution)/shard_map/reduce_scatter | solution.py:67
  41.3 1.4 fusion.83
  42.7 3.0 collective-permute-start
  45.7 1.3 collective-permute-done
  49.1 16.9 %collective-permute-done.1 = bf16[1024,384]{1,0:T(8,128)(2,1)S(1)} collective-permute-done((bf16[1024,384]{1,0:T(8,128)(2,1)S(1)}, bf16[1024,384]{1,0:T(8,128)(2,1)S(1)}, u32[]{:S(2)}, u32[]{:S(2)}) %collective-permute-start.1) | collective-permute-done | bytes 786464 | tf_op jit(solution)/shard_map/ppermute | solution.py:20
  67.3 3.8 %collective-permute-start.2 = (bf16[2048,384]{1,0:T(8,128)(2,1)}, bf16[2048,384]{1,0:T(8,128)(2,1)}, u32[]{:S(2)}, u32[]{:S(2)}) collective-permute-start(bf16[2048,384]{1,0:T(8,128)(2,1)} %pad_maximum_fusion), channel_id=1, source_target_pairs={{0,16},{16,0},{4,20},{20,4},{8,24},{24,8},{12,28},{28,12},{32,48},... | collective-permute-start | bytes 4718600 | tf_op jit(solution)/shard_map/ppermute | solution.py:20
  76.2 45.3 %collective-permute-done.4 = bf16[1024,384]{1,0:T(8,128)(2,1)S(1)} collective-permute-done((bf16[1024,384]{1,0:T(8,128)(2,1)}, bf16[1024,384]{1,0:T(8,128)(2,1)S(1)}, u32[]{:S(2)}, u32[]{:S(2)}) %collective-permute-start.4) | collective-permute-done | bytes 786464 | tf_op jit(solution)/shard_map/ppermute | solution.py:20
  121.7 3.4 collective-permute-start.5
  127.0 2.7 constant_dynamic-update-slice_fusion
  129.7 2.6 multiply_reduce_fusion
  135.6 1.5 fusion.4
  138.2 1.5 fusion.2
  139.6 18.5 %collective-permute-done.5 = bf16[2048,384]{1,0:T(8,128)(2,1)S(1)} collective-permute-done((bf16[2048,384]{1,0:T(8,128)(2,1)S(1)}, bf16[2048,384]{1,0:T(8,128)(2,1)S(1)}, u32[]{:S(2)}, u32[]{:S(2)}) %collective-permute-start.5) | collective-permute-done | bytes 1572896 | tf_op jit(solution)/shard_map/ppermute | solution.py:20
  158.4 1.6 copy-done.17
  160.0 1.4 fusion
  161.5 50.6 %all-gather.3.cloned.1.call-done = bf16[2048,384]{1,0:T(8,128)(2,1)} async-done(((bf16[32,384]{1,0:T(8,128)(2,1)}), bf16[2048,384]{1,0:T(8,128)(2,1)}) %all-gather.3.cloned.1.call-update) | async-done | bytes 1572880 | tf_op jit(solution)/shard_map/all_gather | solution.py:102
  212.1 1.9 multiply_reduce_fusion.3
  219.2 98.7 %all-gather.5.cloned.1.call-done = bf16[2048,384]{1,0:T(8,128)(2,1)} async-done(((bf16[32,384]{1,0:T(8,128)(2,1)}), bf16[2048,384]{1,0:T(8,128)(2,1)}) %all-gather.5.cloned.1.call-update) | async-done | bytes 1572880 | tf_op jit(solution)/shard_map/all_gather | solution.py:103
  318.0 3.3 fusion.18
  321.3 5.3 %fusion.54 = f32[512,128]{0,1:T(8,128)S(1)} fusion(f32[512,128]{0,1:T(8,128)S(1)} %fusion.18, f32[4096,512]{1,0:T(8,128)} %copy-done.4, f32[512]{0:T(512)S(1)} %get-tuple-element.14, bf16[4096,384]{1,0:T(8,128)(2,1)} %copy-done.17, f32[512]{0:T(512)S(1)} %get-tuple-element.9, f32[512]{0:T(512)S(1)} %get-tuple-element.13), kind=kOutput, calls=%fused_computation.48 | convolution fusion | flops 543358976 | bytes 9967616 | tf_op jit(solution)/shard_map/dot_general | solution.py:44
  328.5 1.6 fusion.45
  332.2 1.6 fusion.36
  (101 shorter events, 29.3 us)
Async XLA Ops:
  6.5 6.6 %copy-start.19 = (f32[128]{0:T(128)S(1)}, f32[128]{0:T(128)}, u32[]{:S(2)}) copy-start(f32[128]{0:T(128)} %param.13) | copy-start | bytes 1540
  6.5 36.2 %copy-start.11 = (bf16[512,384]{1,0:T(8,128)(2,1)S(1)}, bf16[512,384]{1,0:T(8,128)(2,1)}, u32[]{:S(2)}) copy-start(bf16[512,384]{1,0:T(8,128)(2,1)} %param.8) | copy-start | bytes 1179652
  6.5 41.9 %copy-start.12 = (bf16[512,384]{1,0:T(8,128)(2,1)S(1)}, bf16[512,384]{1,0:T(8,128)(2,1)}, u32[]{:S(2)}) copy-start(bf16[512,384]{1,0:T(8,128)(2,1)} %param.9) | copy-start | bytes 1179652
  6.5 33.7 %reduce-scatter.2.cloned.1.call-start = ((), (), s32[]{:S(2)}) async-start(), calls=%async_computation.1 | async-start | bytes 245760 | tf_op jit(solution)/shard_map/reduce_scatter | solution.py:67
  13.1 199.0 %all-gather.3.cloned.1.call-start = ((), (), s32[]{:S(2)}) async-start(), calls=%async_computation.2 | async-start | bytes 1597440 | tf_op jit(solution)/shard_map/all_gather | solution.py:102
  40.2 33.8 %copy-start.15 = (bf16[32,768]{1,0:T(8,128)(2,1)S(1)}, bf16[32,768]{1,0:T(8,128)(2,1)}, u32[]{:S(2)}) copy-start(bf16[32,768]{1,0:T(8,128)(2,1)} %reduce-scatter.2.cloned.1.call-done) | copy-start | bytes 147460
  42.7 275.3 %all-gather.5.cloned.1.call-start = ((), (), s32[]{:S(2)}) async-start(), calls=%async_computation.3 | async-start | bytes 1597440 | tf_op jit(solution)/shard_map/all_gather | solution.py:103
  42.7 4.3 %collective-permute-start = (bf16[512,384]{1,0:T(8,128)(2,1)S(1)}, bf16[512,384]{1,0:T(8,128)(2,1)S(1)}, u32[]{:S(2)}, u32[]{:S(2)}) collective-permute-start(bf16[512,384]{1,0:T(8,128)(2,1)S(1)} %copy-done.11), channel_id=1, source_target_pairs={{0,4},{4,0},{8,12},{12,8},{16,20},{20,16},{24,28},{28,24},{32,36},... | collective-permute-start | bytes 1179656 | tf_op jit(solution)/shard_map/ppermute | solution.py:20
  47.1 18.8 %collective-permute-start.1 = (bf16[1024,384]{1,0:T(8,128)(2,1)S(1)}, bf16[1024,384]{1,0:T(8,128)(2,1)S(1)}, u32[]{:S(2)}, u32[]{:S(2)}) collective-permute-start(bf16[1024,384]{1,0:T(8,128)(2,1)S(1)} %pad_maximum_fusion.2), channel_id=1, source_target_pairs={{0,8},{8,0},{4,12},{12,4},{16,24},{24,16},{20,28},{28,20},{32,40},... | collective-permute-start | bytes 2359304 | tf_op jit(solution)/shard_map/ppermute | solution.py:20
  48.4 22.6 %collective-permute-start.3 = (bf16[512,384]{1,0:T(8,128)(2,1)S(1)}, bf16[512,384]{1,0:T(8,128)(2,1)S(1)}, u32[]{:S(2)}, u32[]{:S(2)}) collective-permute-start(bf16[512,384]{1,0:T(8,128)(2,1)S(1)} %copy-done.12), channel_id=1, source_target_pairs={{0,4},{4,0},{8,12},{12,8},{16,20},{20,16},{24,28},{28,24},{32,36},... | collective-permute-start | bytes 1179656 | tf_op jit(solution)/shard_map/ppermute | solution.py:20
  67.3 59.7 %collective-permute-start.2 = (bf16[2048,384]{1,0:T(8,128)(2,1)}, bf16[2048,384]{1,0:T(8,128)(2,1)}, u32[]{:S(2)}, u32[]{:S(2)}) collective-permute-start(bf16[2048,384]{1,0:T(8,128)(2,1)} %pad_maximum_fusion), channel_id=1, source_target_pairs={{0,16},{16,0},{4,20},{20,4},{8,24},{24,8},{12,28},{28,12},{32,48},... | collective-permute-start | bytes 4718600 | tf_op jit(solution)/shard_map/ppermute | solution.py:20
  72.1 49.4 %collective-permute-start.4 = (bf16[1024,384]{1,0:T(8,128)(2,1)}, bf16[1024,384]{1,0:T(8,128)(2,1)S(1)}, u32[]{:S(2)}, u32[]{:S(2)}) collective-permute-start(bf16[1024,384]{1,0:T(8,128)(2,1)} %pad_maximum_fusion.3), channel_id=1, source_target_pairs={{0,8},{8,0},{4,12},{12,4},{16,24},{24,16},{20,28},{28,20},{32,40},... | collective-permute-start | bytes 2359304 | tf_op jit(solution)/shard_map/ppermute | solution.py:20
  76.2 53.5 %copy-start.13 = (bf16[512,384]{1,0:T(8,128)(2,1)S(1)}, bf16[512,384]{1,0:T(8,128)(2,1)}, u32[]{:S(2)}) copy-start(bf16[512,384]{1,0:T(8,128)(2,1)} %param.7) | copy-start | bytes 1179652
  121.7 36.4 %collective-permute-start.5 = (bf16[2048,384]{1,0:T(8,128)(2,1)S(1)}, bf16[2048,384]{1,0:T(8,128)(2,1)S(1)}, u32[]{:S(2)}, u32[]{:S(2)}) collective-permute-start(bf16[2048,384]{1,0:T(8,128)(2,1)S(1)} %pad_maximum_fusion.1), channel_id=1, source_target_pairs={{0,16},{16,0},{4,20},{20,4},{8,24},{24,8},{12,28},{28,12},{32,48},... | collective-permute-start | bytes 4718600 | tf_op jit(solution)/shard_map/ppermute | solution.py:20
  133.7 4.5 %copy-start.3 = (f32[4096,512]{1,0:T(8,128)}, f32[4096,512]{1,0:T(8,128)S(1)}, u32[]{:S(2)}) copy-start(f32[4096,512]{1,0:T(8,128)S(1)} %get-tuple-element.19) | copy-start | bytes 25165828
  134.9 25.1 %copy-start.2 = (f32[4096,512]{1,0:T(8,128)}, f32[4096,512]{1,0:T(8,128)S(1)}, u32[]{:S(2)}) copy-start(f32[4096,512]{1,0:T(8,128)S(1)} %get-tuple-element.23) | copy-start | bytes 25165828
  138.2 19.9 %copy-start.16 = (bf16[4096,384]{1,0:T(8,128)(2,1)S(1)}, bf16[4096,384]{1,0:T(8,128)(2,1)}, u32[]{:S(2)}) copy-start(bf16[4096,384]{1,0:T(8,128)(2,1)} %constant_dynamic-update-slice_fusion.5) | copy-start | bytes 9437188
  317.9 8.7 %copy-start.20 = (bf16[2048,384]{1,0:T(8,128)(2,1)S(1)}, bf16[2048,384]{1,0:T(8,128)(2,1)}, u32[]{:S(2)}) copy-start(bf16[2048,384]{1,0:T(8,128)(2,1)} %all-gather.5.cloned.1.call-done) | copy-start | bytes 4718596
  318.0 9.6 %slice-start.2 = ((s8[8388608]{0:T(1024)(128)(4,1)}), s8[4194304]{0:T(1024)(128)(4,1)S(1)}, s32[]{:S(2)}) async-start(s8[8388608]{0:T(1024)(128)(4,1)} %bitcast.27), calls=%async_computation.6 | async-start | bytes 8388608
  321.3 5.4 %copy-start.8 = (f32[2048,512]{1,0:T(8,128)S(1)}, f32[2048,512]{1,0:T(8,128)}, u32[]{:S(2)}) copy-start(f32[2048,512]{1,0:T(8,128)} %copy-done.7) | copy-start | bytes 12582916
  321.3 6.3 %slice-start.3 = ((s8[8388608]{0:T(1024)(128)(4,1)}), s8[4194304]{0:T(1024)(128)(4,1)S(1)}, s32[]{:S(2)}) async-start(s8[8388608]{0:T(1024)(128)(4,1)} %bitcast.27), calls=%async_computation.7 | async-start | bytes 8388608
  321.3 7.2 %copy-start.18 = (bf16[4096,384]{1,0:T(8,128)(2,1)S(1)}, bf16[4096,384]{1,0:T(8,128)(2,1)}, u32[]{:S(2)}) copy-start(bf16[4096,384]{1,0:T(8,128)(2,1)} %copy-done.17) | copy-start | bytes 9437188
  326.7 5.0 %slice-start = ((s8[8388608]{0:T(1024)(128)(4,1)}), s8[4194304]{0:T(1024)(128)(4,1)S(1)}, s32[]{:S(2)}) async-start(s8[8388608]{0:T(1024)(128)(4,1)} %bitcast.25), calls=%async_computation.4 | async-start | bytes 8388608
  328.5 3.7 %slice-start.1 = ((s8[8388608]{0:T(1024)(128)(4,1)}), s8[4194304]{0:T(1024)(128)(4,1)S(1)}, s32[]{:S(2)}) async-start(s8[8388608]{0:T(1024)(128)(4,1)} %bitcast.25), calls=%async_computation.5 | async-start | bytes 8388608
  (10 other events, 24.0 us)
Sparse Core Ops, SparseCore 0:
  13.2 26.9 reduce-scatter.1
  42.8 169.2 all-gather.2
  214.1 103.7 all-gather.4
where the time goes:
time: 342 us; the launch traced here: 341 us
  waiting for transfers between devices  258 us (75%)
  matrix products  25.5 us (7%)
  local copies, waits for them, and re-layouts  19.2 us (6%)
  between operations  13.5 us (4%)
  starting transfers between devices  12.5 us (4%)
  other arithmetic  12.3 us (4%)
    all_gather x1, waiting for transfers between devices, per_device(): lax.all_gather(ref_vals, 'seq', axis=0, tiled=True)  98.7 us
    ppermute x6, waiting for transfers between devices, from_partner(): return lax.ppermute(block, axis, route)  82 us
    all_gather x1, waiting for transfers between devices, per_device(): lax.all_gather(ref_keys, 'seq', axis=0, tiled=True)  50.6 us
    reduce_scatter x1, waiting for transfers between devices, reference_pair(): lax.psum_scatter(stacked.astype(jnp.bfloat16), 'tensor', scatter_dimensio...  27 us
    dot_general x6, matrix products, attend(): jnp.dot(weights.astype(jnp.bfloat16), values[:, col_start:col_stop], pref...  13.6 us
    unnamed x56, local copies, waits for them, and re-layouts  13.5 us
    ppermute x6, starting transfers between devices, from_partner(): return lax.ppermute(block, axis, route)  12.4 us
    dot_general x6, matrix products, attend(): jnp.einsum('qd,kd->qk', queries[:, col_start:col_stop], key_rows[:, col_s...  8.46 us
  transfers between devices with their start and end apart: 9, of which 7 were waited for; matrix products, arithmetic and copies ran while one was open for 8% of the time, Pallas kernels for 0%

commit v1 on v0

v1 whole, which is shorter than its diff:
```python
import functools

import jax
import jax.numpy as jnp
from jax import lax
from jax.experimental import pallas as pl
from jax.experimental.pallas import tpu as pltpu
from jax.sharding import Mesh
from jax.sharding import PartitionSpec as P

HD = 128
HEADS_HERE = 3
WIDTH = HEADS_HERE * HD
EPSILON = 1e-06
FACTOR = HD**-0.5 * 1.4426950408889634
SEQ = ("x", "w", "y", "core")


def ring(count, shift):
    return [(i, (i + shift) % count) for i in range(count)]


def project_kernel(me_ref, hidden, wk, wv, own, first, second, third):
    step = pl.program_id(0)
    rows = hidden[...]
    k_part = jnp.dot(rows, wk[...], preferred_element_type=jnp.float32)
    v_part = jnp.dot(rows, wv[...], preferred_element_type=jnp.float32)

    @pl.when(step == 3)
    def _():
        own[:, :WIDTH] = k_part
        own[:, WIDTH:] = v_part

    for index, out in ((0, second), (1, first), (2, third)):

        @pl.when(step == index)
        def _():
            out[:, :WIDTH] = k_part.astype(jnp.bfloat16)
            out[:, WIDTH:] = v_part.astype(jnp.bfloat16)


def project(me, hidden, wk, wv):
    rows, depth = hidden.shape
    ahead = (2, 1, 3, 0)

    def group(step, me_ref):
        shift = jnp.where(step == 0, 2, jnp.where(step == 1, 1, jnp.where(step == 2, 3, 0)))
        return (0, lax.rem(me_ref[0] + shift, 4))

    del ahead
    whole = lambda step, me_ref: (0, 0)
    sent = jax.ShapeDtypeStruct((rows, 2 * WIDTH), jnp.bfloat16)
    return pl.pallas_call(
        project_kernel,
        out_shape=(jax.ShapeDtypeStruct((rows, 2 * WIDTH), jnp.float32), sent, sent, sent),
        grid_spec=pltpu.PrefetchScalarGridSpec(
            num_scalar_prefetch=1,
            grid=(4,),
            in_specs=[
                pl.BlockSpec((rows, depth), whole),
                pl.BlockSpec((depth, WIDTH), group),
                pl.BlockSpec((depth, WIDTH), group),
            ],
            out_specs=[pl.BlockSpec((rows, 2 * WIDTH), whole)] * 4,
        ),
        compiler_params=pltpu.CompilerParams(vmem_limit_bytes=32 << 20),
        cost_estimate=pl.CostEstimate(
            flops=2 * rows * depth * 8 * WIDTH, bytes_accessed=2 * depth * 8 * WIDTH, transcendentals=0
        ),
        name="project",
    )(me, hidden, wk, wv)


def norm_kernel(own, a, b, c, gain, out):
    total = (
        own[...]
        + a[...].astype(jnp.float32)
        + b[...].astype(jnp.float32)
        + c[...].astype(jnp.float32)
    )
    for head in range(HEADS_HERE):
        cols = slice(head * HD, (head + 1) * HD)
        raw = total[:, cols]
        scale = lax.rsqrt(jnp.mean(raw * raw, axis=1, keepdims=True) + EPSILON)
        out[:, cols] = (raw * scale * gain[...]).astype(jnp.bfloat16)
    out[:, WIDTH:] = total[:, WIDTH:].astype(jnp.bfloat16)


def norm(own, a, b, c, gain):
    rows = own.shape[0]
    return pl.pallas_call(
        norm_kernel,
        out_shape=jax.ShapeDtypeStruct((rows, 2 * WIDTH), jnp.bfloat16),
        cost_estimate=pl.CostEstimate(flops=10 * own.size, bytes_accessed=12 * own.size, transcendentals=128),
        name="norm",
    )(own, a, b, c, gain)


def attend_block(q, kv, acc, top, total, fresh):
    for head in range(HEADS_HERE):
        cols = slice(head * HD, (head + 1) * HD)
        vals = slice(WIDTH + head * HD, WIDTH + (head + 1) * HD)
        scores = lax.dot_general(
            q[:, cols], kv[:, cols], (((1,), (1,)), ((), ())), preferred_element_type=jnp.float32
        )
        high = jnp.max(scores, axis=1, keepdims=True) * FACTOR
        if fresh:
            raised = high
        else:
            old = top[:, head : head + 1]
            raised = jnp.maximum(old, high)
        weights = jnp.exp2(scores * FACTOR - raised)
        row_sum = jnp.sum(weights, axis=1, keepdims=True)
        mixed = jnp.dot(
            weights.astype(jnp.bfloat16), kv[:, vals], preferred_element_type=jnp.float32
        )
        if fresh:
            total[:, head : head + 1] = row_sum
            acc[:, cols] = mixed
        else:
            rescale = jnp.exp2(old - raised)
            total[:, head : head + 1] = total[:, head : head + 1] * rescale + row_sum
            acc[:, cols] = acc[:, cols] * rescale + mixed
        top[:, head : head + 1] = raised


def view_kernel(q, kv, acc, top, total):
    first = pl.program_id(0) == 0

    @pl.when(first)
    def _():
        attend_block(q, kv, acc, top, total, True)

    @pl.when(jnp.logical_not(first))
    def _():
        attend_block(q, kv, acc, top, total, False)


def attend_cost(rows, keys):
    pairs = rows * keys * HEADS_HERE
    return pl.CostEstimate(
        flops=4 * HD * pairs, bytes_accessed=4 * keys * WIDTH + 8 * rows * WIDTH, transcendentals=pairs
    )


def attend_view(q, kv, chunk=1024):
    rows = q.shape[0]
    whole = lambda i: (0, 0)
    return pl.pallas_call(
        view_kernel,
        out_shape=(
            jax.ShapeDtypeStruct((rows, WIDTH), jnp.float32),
            jax.ShapeDtypeStruct((rows, HD), jnp.float32),
            jax.ShapeDtypeStruct((rows, HD), jnp.float32),
        ),
        grid=(kv.shape[0] // chunk,),
        in_specs=[pl.BlockSpec((rows, WIDTH), whole), pl.BlockSpec((chunk, 2 * WIDTH), lambda i: (i, 0))],
        out_specs=[
            pl.BlockSpec((rows, WIDTH), whole),
            pl.BlockSpec((rows, HD), whole),
            pl.BlockSpec((rows, HD), whole),
        ],
        compiler_params=pltpu.CompilerParams(vmem_limit_bytes=48 << 20),
        cost_estimate=attend_cost(rows, kv.shape[0]),
        name="attend_view",
    )(q, kv)


def more_kernel(count, last, q, *refs):
    pieces, (acc_in, top_in, total_in), rest = refs[:count], refs[count : count + 3], refs[count + 3 :]
    if last:
        out, acc, top, total = rest
    else:
        acc, top, total = rest
    acc[...] = acc_in[...]
    top[...] = top_in[...]
    total[...] = total_in[...]
    for piece in pieces:
        attend_block(q, piece, acc, top, total, False)
    if last:
        for head in range(HEADS_HERE):
            cols = slice(head * HD, (head + 1) * HD)
            out[:, cols] = (acc[:, cols] / total[:, head : head + 1]).astype(jnp.bfloat16)


def attend_more(q, pieces, carried, last):
    rows = q.shape[0]
    state = [
        jax.ShapeDtypeStruct((rows, WIDTH), jnp.float32),
        jax.ShapeDtypeStruct((rows, HD), jnp.float32),
        jax.ShapeDtypeStruct((rows, HD), jnp.float32),
    ]
    vmem = pl.BlockSpec(memory_space=pltpu.VMEM)
    if last:
        out_shape, scratch = (
            jax.ShapeDtypeStruct((rows, WIDTH), jnp.bfloat16),
            [pltpu.VMEM(s.shape, s.dtype) for s in state],
        )
        out_specs = vmem
    else:
        out_shape, scratch, out_specs = tuple(state), [], (vmem,) * 3
    return pl.pallas_call(
        functools.partial(more_kernel, len(pieces), last),
        out_shape=out_shape,
        in_specs=[vmem] * (4 + len(pieces)),
        out_specs=out_specs,
        scratch_shapes=scratch,
        compiler_params=pltpu.CompilerParams(vmem_limit_bytes=48 << 20),
        cost_estimate=attend_cost(rows, sum(p.shape[0] for p in pieces)),
        name="attend_last" if last else "attend_more",
    )(q, *pieces, *carried)


def per_device(q_tok, k_tok, v_tok, ref_hidden, ref_wk, ref_wv, key_gain):
    view = lax.all_gather(jnp.concatenate((k_tok, v_tok), axis=1), ("y", "core"), axis=0, tiled=True)

    me = lax.axis_index("tensor").astype(jnp.int32).reshape(1)
    own, *sent = project(me, ref_hidden, ref_wk, ref_wv)
    arrived = [lax.ppermute(block, "tensor", ring(4, shift)) for shift, block in zip((1, 2, 3), sent)]
    block = norm(own, *arrived, key_gain.reshape(1, HD))
    block = jnp.concatenate((block, lax.ppermute(block, "w", ring(2, 1))), axis=0)
    block = jnp.concatenate([block] + [lax.ppermute(block, "y", ring(4, s)) for s in (1, 3, 2)], axis=0)
    pieces = [block] + [lax.ppermute(block, "x", ring(4, s)) for s in (1, 3, 2)]
    others = [lax.ppermute(piece, "core", ring(2, 1)) for piece in pieces]

    carried = attend_view(q_tok, view)
    carried = attend_more(q_tok, pieces, carried, False)
    return attend_more(q_tok, others, carried, True)


def solution(mesh):
    fine = Mesh(
        mesh.devices.reshape(4, 2, 4, 2, 4),
        ("x", "w", "y", "core", "tensor"),
    )
    placed = (
        P(SEQ, "tensor"),
        P(SEQ, "tensor"),
        P(SEQ, "tensor"),
        P(SEQ, "tensor"),
        P("tensor", None),
        P("tensor", None),
        P(),
    )
    return jax.shard_map(
        per_device, mesh=fine, in_specs=placed, out_specs=P(SEQ, "tensor"), check_vma=False
    )
```

time: 342 us -> 107 us (0.31)
  waiting for transfers between devices: 258 us -> 19 us
  Pallas kernels: 0 us -> 31.7 us
  matrix products: 25.5 us -> 0 us
  starting transfers between devices: 12.5 us -> 35 us
  local copies, waits for them, and re-layouts: 19.2 us -> 4.58 us
  other arithmetic: 12.3 us -> 3.01 us
    all_gather x2 -> x1, waiting for transfers between devices: 149 us -> 0.01 us  [per_device(): lax.all_gather(jnp.concatenate((k_tok, v_tok), axis=1), ('y', 'core'), ax...]
    ppermute x6 -> x14, waiting for transfers between devices: 82 us -> 19 us  [the longest x3 8.24 us: per_device(): lax.ppermute(block, 'y', ring(4, s))]
    pallas_call x0 -> x5, Pallas kernels: none -> 31.7 us  [the longest x1 15.9 us: attend_view(): pl.pallas_call(view_kernel, out_shape=(jax.ShapeDtypeStruct((rows, WIDTH)...]
    reduce_scatter x1 -> x0, waiting for transfers between devices: 27 us -> none  [reference_pair(): lax.psum_scatter(stacked.astype(jnp.bfloat16), 'tensor', scatter_dimensio...]
    dot_general x14 -> x0, matrix products: 25.5 us -> none  [the longest x6 13.6 us: attend(): jnp.dot(weights.astype(jnp.bfloat16), values[:, col_start:col_stop], pref...]
    ppermute x6 -> x14, starting transfers between devices: 12.4 us -> 35 us  [the longest x4 15.5 us: per_device(): others = [lax.ppermute(piece, 'core', ring(2, 1)) for piece in pieces]]
    unnamed x56 -> x20, local copies, waits for them, and re-layouts: 13.5 us -> 4.57 us
    reduce_sum x7 -> x0, other arithmetic: 6.95 us -> none  [the longest x6 6.84 us: attend(): jnp.sum(weights, axis=1)]
  transfers between devices with their start and end apart: 9 -> 15, of which waited for: 7 -> 6; matrix products, arithmetic and copies ran while one was open for 8% -> 2% of each run, Pallas kernels for 0% -> 23%
where the time goes in v1:
time: 107 us
  starting transfers between devices  35 us (33%)
  Pallas kernels  31.7 us (30%)
  waiting for transfers between devices  19 us (18%)
  between operations  13.5 us (13%)
  local copies, waits for them, and re-layouts  4.58 us (4%)
  other arithmetic  3.01 us (3%)
    pallas_call x1, Pallas kernels, attend_view(): pl.pallas_call(view_kernel, out_shape=(jax.ShapeDtypeStruct((rows, WIDTH)...  15.9 us
    ppermute x4, starting transfers between devices, per_device(): others = [lax.ppermute(piece, 'core', ring(2, 1)) for piece in pieces]  15.5 us
    pallas_call x2, Pallas kernels, attend_more(): pl.pallas_call(functools.partial(more_kernel, len(pieces), last), out_sha...  12.4 us
    ppermute x3, starting transfers between devices, per_device(): lax.ppermute(block, 'tensor', ring(4, shift))  11.3 us
    ppermute x3, waiting for transfers between devices, per_device(): lax.ppermute(block, 'y', ring(4, s))  8.24 us
    ppermute x3, waiting for transfers between devices, per_device(): pieces = [block] + [lax.ppermute(block, 'x', ring(4, s)) for s in (1, 3, 2)]  4.84 us
    unnamed x20, local copies, waits for them, and re-layouts  4.57 us
    ppermute x3, starting transfers between devices, per_device(): lax.ppermute(block, 'y', ring(4, s))  4.38 us
  transfers between devices with their start and end apart: 15, of which 6 were waited for; matrix products, arithmetic and copies ran while one was open for 2% of the time, Pallas kernels for 23%

profile of v1, /device:TPU:1, one launch (start us, length us, event | category | flops | bytes accessed | tf_op | source)
XLA Modules:
  0.0 106.8 jit_solution(1271429876712147851)
XLA Ops:
  6.5 2.2 %pad_maximum_fusion = bf16[512,768]{1,0:T(8,128)(2,1)} fusion(bf16[512,384]{1,0:T(8,128)(2,1)} %param.9, bf16[512,384]{1,0:T(8,128)(2,1)} %param.8), kind=kLoop, calls=%fused_computation | loop fusion | flops 1572864 | bytes 1572864 | tf_op jit(solution)/shard_map/concatenate | solution.py:215
  8.8 1.7 %copy-done.1 = bf16[768,1536]{1,0:T(8,128)(2,1)S(1)} copy-done((bf16[768,1536]{1,0:T(8,128)(2,1)S(1)}, bf16[768,1536]{1,0:T(8,128)(2,1)}, u32[]{:S(2)}) %copy-start.1) | copy-done | bytes 2359320
  11.3 1.8 %project.1 = (f32[32,768]{1,0:T(8,128)S(1)}, bf16[32,768]{1,0:T(8,128)(2,1)S(1)}, bf16[32,768]{1,0:T(8,128)(2,1)S(1)}, bf16[32,768]{1,0:T(8,128)(2,1)S(1)}) custom-call(s32[1]{0:T(128)} %bitcast.me_ref, bf16[32,768]{1,0:T(8,128)(2,1)S(1)} %copy-done.4, bf16[768,1536]{1,0:T(8,128)(2,1)S(1)} %copy-done, bf16[768,1536]{1,0:T(8,128)(2,1)S(1)} %copy-done.1), custom_call_target="tpu_custom_call" | custom-call | flops 150994944 | bytes 4718592 | tf_op jit(solution)/shard_map/project/pallas_call | solution.py:53
  13.7 3.8 %collective-permute-start = (bf16[32,768]{1,0:T(8,128)(2,1)S(1)}, bf16[32,768]{1,0:T(8,128)(2,1)S(1)}, u32[]{:S(2)}, u32[]{:S(2)}) collective-permute-start(bf16[32,768]{1,0:T(8,128)(2,1)S(1)} %get-tuple-element.16), channel_id=1, source_target_pairs={{0,1},{1,2},{2,3},{3,0},{4,5},{5,6},{6,7},{7,4},{8,9},{9,10},{10,1... | collective-permute-start | bytes 147464 | tf_op jit(solution)/shard_map/ppermute | solution.py:219
  17.5 5.1 %collective-permute-start.1 = (bf16[32,768]{1,0:T(8,128)(2,1)S(1)}, bf16[32,768]{1,0:T(8,128)(2,1)S(1)}, u32[]{:S(2)}, u32[]{:S(2)}) collective-permute-start(bf16[32,768]{1,0:T(8,128)(2,1)S(1)} %get-tuple-element.17), channel_id=1, source_target_pairs={{0,2},{1,3},{2,0},{3,1},{4,6},{5,7},{6,4},{7,5},{8,10},{9,11},{10,... | collective-permute-start | bytes 147464 | tf_op jit(solution)/shard_map/ppermute | solution.py:219
  22.6 2.4 %collective-permute-start.2 = (bf16[32,768]{1,0:T(8,128)(2,1)S(1)}, bf16[32,768]{1,0:T(8,128)(2,1)S(1)}, u32[]{:S(2)}, u32[]{:S(2)}) collective-permute-start(bf16[32,768]{1,0:T(8,128)(2,1)S(1)} %get-tuple-element.18), channel_id=1, source_target_pairs={{0,3},{1,0},{2,1},{3,2},{4,7},{5,4},{6,5},{7,6},{8,11},{9,8},{10,9... | collective-permute-start | bytes 147464 | tf_op jit(solution)/shard_map/ppermute | solution.py:219
  25.0 3.2 %collective-permute-done.2.c = bf16[32,768]{1,0:T(8,128)(2,1)S(1)} collective-permute-done((bf16[32,768]{1,0:T(8,128)(2,1)S(1)}, bf16[32,768]{1,0:T(8,128)(2,1)S(1)}, u32[]{:S(2)}, u32[]{:S(2)}) %collective-permute-start.2) | collective-permute-done | bytes 49184 | tf_op jit(solution)/shard_map/ppermute | solution.py:219
  28.8 1.7 %norm.1 = bf16[32,768]{1,0:T(8,128)(2,1)} custom-call(f32[32,768]{1,0:T(8,128)} %copy-done.3, bf16[32,768]{1,0:T(8,128)(2,1)} %copy-done.5, bf16[32,768]{1,0:T(8,128)(2,1)} %copy-done.6, bf16[32,768]{1,0:T(8,128)(2,1)} %copy-done.7, f32[1,128]{1,0:T(1,128)} %bitcast.2), custom_call_target="tpu_custom_call" | custom-call | flops 245760 | bytes 294912 | tf_op jit(solution)/shard_map/norm/pallas_call | solution.py:91
  30.5 0.8 constant_dynamic-update-slice_fusion.4
  31.3 2.7 %collective-permute-done.3 = bf16[32,768]{1,0:T(8,128)(2,1)S(1)} collective-permute-done((bf16[32,768]{1,0:T(8,128)(2,1)}, bf16[32,768]{1,0:T(8,128)(2,1)S(1)}, u32[]{:S(2)}, u32[]{:S(2)}) %collective-permute-start.3) | collective-permute-done | bytes 49184 | tf_op jit(solution)/shard_map/ppermute | solution.py:221
  34.0 0.8 pad_maximum_fusion.1
  34.8 1.3 %collective-permute-start.4 = (bf16[64,768]{1,0:T(8,128)(2,1)S(1)}, bf16[64,768]{1,0:T(8,128)(2,1)S(1)}, u32[]{:S(2)}, u32[]{:S(2)}) collective-permute-start(bf16[64,768]{1,0:T(8,128)(2,1)S(1)} %pad_maximum_fusion.1), channel_id=1, source_target_pairs={{0,8},{8,16},{16,24},{24,0},{1,9},{9,17},{17,25},{25,1},{2,10},{10... | collective-permute-start | bytes 294920 | tf_op jit(solution)/shard_map/ppermute | solution.py:222
  36.1 1.5 %collective-permute-start.5 = (bf16[64,768]{1,0:T(8,128)(2,1)S(1)}, bf16[64,768]{1,0:T(8,128)(2,1)S(1)}, u32[]{:S(2)}, u32[]{:S(2)}) collective-permute-start(bf16[64,768]{1,0:T(8,128)(2,1)S(1)} %pad_maximum_fusion.1), channel_id=1, source_target_pairs={{0,24},{8,0},{16,8},{24,16},{1,25},{9,1},{17,9},{25,17},{2,26},{10... | collective-permute-start | bytes 294920 | tf_op jit(solution)/shard_map/ppermute | solution.py:222
  37.6 1.6 %collective-permute-start.6 = (bf16[64,768]{1,0:T(8,128)(2,1)S(1)}, bf16[64,768]{1,0:T(8,128)(2,1)S(1)}, u32[]{:S(2)}, u32[]{:S(2)}) collective-permute-start(bf16[64,768]{1,0:T(8,128)(2,1)S(1)} %pad_maximum_fusion.1), channel_id=1, source_target_pairs={{0,16},{8,24},{16,0},{24,8},{1,17},{9,25},{17,1},{25,9},{2,18},{10... | collective-permute-start | bytes 294920 | tf_op jit(solution)/shard_map/ppermute | solution.py:222
  39.2 3.0 %collective-permute-done.4 = bf16[64,768]{1,0:T(8,128)(2,1)S(1)} collective-permute-done((bf16[64,768]{1,0:T(8,128)(2,1)S(1)}, bf16[64,768]{1,0:T(8,128)(2,1)S(1)}, u32[]{:S(2)}, u32[]{:S(2)}) %collective-permute-start.4) | collective-permute-done | bytes 98336 | tf_op jit(solution)/shard_map/ppermute | solution.py:222
  42.3 5.2 %collective-permute-done.6 = bf16[64,768]{1,0:T(8,128)(2,1)S(1)} collective-permute-done((bf16[64,768]{1,0:T(8,128)(2,1)S(1)}, bf16[64,768]{1,0:T(8,128)(2,1)S(1)}, u32[]{:S(2)}, u32[]{:S(2)}) %collective-permute-start.6) | collective-permute-done | bytes 98336 | tf_op jit(solution)/shard_map/ppermute | solution.py:222
  47.5 2.7 %collective-permute-start.10 = (bf16[256,768]{1,0:T(8,128)(2,1)S(1)}, bf16[256,768]{1,0:T(8,128)(2,1)S(1)}, u32[]{:S(2)}, u32[]{:S(2)}) collective-permute-start(bf16[256,768]{1,0:T(8,128)(2,1)S(1)} %constant_dynamic-update-slice_fusion.refs_0_), channel_id=1, source_target_pairs={{0,192},{64,0},{128,64},{192,128},{1,193},{65,1},{129,65},{193,129... | collective-permute-start | bytes 1179656 | tf_op jit(solution)/shard_map/ppermute | solution.py:223
  51.3 3.8 %collective-permute-start.7 = (bf16[256,768]{1,0:T(8,128)(2,1)S(1)}, bf16[256,768]{1,0:T(8,128)(2,1)S(1)}, u32[]{:S(2)}, u32[]{:S(2)}) collective-permute-start(bf16[256,768]{1,0:T(8,128)(2,1)S(1)} %constant_dynamic-update-slice_fusion.refs_0_), channel_id=1, source_target_pairs={{0,4},{4,0},{1,5},{5,1},{2,6},{6,2},{3,7},{7,3},{8,12},{12,8},{9,1... | collective-permute-start | bytes 1179656 | tf_op jit(solution)/shard_map/ppermute | solution.py:224
  55.1 1.6 %collective-permute-done.10.refs_2_ = bf16[256,768]{1,0:T(8,128)(2,1)S(1)} collective-permute-done((bf16[256,768]{1,0:T(8,128)(2,1)S(1)}, bf16[256,768]{1,0:T(8,128)(2,1)S(1)}, u32[]{:S(2)}, u32[]{:S(2)}) %collective-permute-start.10) | collective-permute-done | bytes 393248 | tf_op jit(solution)/shard_map/ppermute | solution.py:223
  56.7 11.2 %collective-permute-start.11 = (bf16[256,768]{1,0:T(8,128)(2,1)S(1)}, bf16[256,768]{1,0:T(8,128)(2,1)S(1)}, u32[]{:S(2)}, u32[]{:S(2)}) collective-permute-start(bf16[256,768]{1,0:T(8,128)(2,1)S(1)} %collective-permute-done.10.refs_2_), channel_id=1, source_target_pairs={{0,4},{4,0},{1,5},{5,1},{2,6},{6,2},{3,7},{7,3},{8,12},{12,8},{9,1... | collective-permute-start | bytes 1179656 | tf_op jit(solution)/shard_map/ppermute | solution.py:224
  68.0 3.2 %collective-permute-done.8.refs_1_ = bf16[256,768]{1,0:T(8,128)(2,1)S(1)} collective-permute-done((bf16[256,768]{1,0:T(8,128)(2,1)S(1)}, bf16[256,768]{1,0:T(8,128)(2,1)S(1)}, u32[]{:S(2)}, u32[]{:S(2)}) %collective-permute-start.8) | collective-permute-done | bytes 393248 | tf_op jit(solution)/shard_map/ppermute | solution.py:223
  71.7 15.9 %attend_view.1 = (f32[512,384]{1,0:T(8,128)S(1)}, f32[512,128]{1,0:T(8,128)S(1)}, f32[512,128]{1,0:T(8,128)S(1)}) custom-call(bf16[512,384]{1,0:T(8,128)(2,1)S(1)} %copy-done.2, bf16[4096,768]{1,0:T(8,128)(2,1)} %all-gather.2.cloned.1.call-done.kv), custom_call_target="tpu_custom_call" | custom-call | flops 3221225472 | bytes 7864320 | tf_op jit(solution)/shard_map/attend_view/pallas_call | solution.py:149
  87.6 5.7 %attend_more.1 = (f32[512,384]{1,0:T(8,128)S(1)}, f32[512,128]{1,0:T(8,128)S(1)}, f32[512,128]{1,0:T(8,128)S(1)}) custom-call(bf16[512,384]{1,0:T(8,128)(2,1)S(1)} %copy-done.2, bf16[256,768]{1,0:T(8,128)(2,1)S(1)} %constant_dynamic-update-slice_fusion.refs_0_, bf16[256,768]{1,0:T(8,128)(2,1)S(1)} %collective-permute-done.8.refs_1_, ...), custom_call_target="tpu_custom_call" | custom-call | flops 805306368 | bytes 3145728 | tf_op jit(solution)/shard_map/attend_more/pallas_call | solution.py:202
  93.3 6.7 %attend_last.1 = bf16[512,384]{1,0:T(8,128)(2,1)} custom-call(bf16[512,384]{1,0:T(8,128)(2,1)S(1)} %copy-done.2, bf16[256,768]{1,0:T(8,128)(2,1)S(1)} %collective-permute-done.7.refs_0_, bf16[256,768]{1,0:T(8,128)(2,1)S(1)} %collective-permute-done.9.refs_1_, bf16[256,768]{1,0:T(8,128)(2,1)S(1)} %collective-permute-done.11.refs_2_, ...), custom_call_target="tpu_custom_call" | custom-call | flops 805306368 | bytes 3145728 | tf_op jit(solution)/shard_map/attend_last/pallas_call | solution.py:202
  (35 shorter events, 3.8 us)
Async XLA Ops:
  6.5 2.2 %copy-start = (bf16[768,1536]{1,0:T(8,128)(2,1)S(1)}, bf16[768,1536]{1,0:T(8,128)(2,1)}, u32[]{:S(2)}) copy-start(bf16[768,1536]{1,0:T(8,128)(2,1)} %wk.1) | copy-start | bytes 7077892
  6.5 65.1 %all-gather.2.cloned.1.call-start = ((), (), s32[]{:S(2)}) async-start(), calls=%async_computation | async-start | bytes 7077888 | tf_op jit(solution)/shard_map/all_gather | solution.py:215
  8.8 1.7 %copy-start.1 = (bf16[768,1536]{1,0:T(8,128)(2,1)S(1)}, bf16[768,1536]{1,0:T(8,128)(2,1)}, u32[]{:S(2)}) copy-start(bf16[768,1536]{1,0:T(8,128)(2,1)} %wv.1) | copy-start | bytes 7077892
  10.5 0.8 copy-start.4
  11.3 60.4 %copy-start.2 = (bf16[512,384]{1,0:T(8,128)(2,1)S(1)}, bf16[512,384]{1,0:T(8,128)(2,1)}, u32[]{:S(2)}) copy-start(bf16[512,384]{1,0:T(8,128)(2,1)} %q.5) | copy-start | bytes 1179652
  13.0 0.6 copy-start.3
  13.7 11.3 %collective-permute-start = (bf16[32,768]{1,0:T(8,128)(2,1)S(1)}, bf16[32,768]{1,0:T(8,128)(2,1)S(1)}, u32[]{:S(2)}, u32[]{:S(2)}) collective-permute-start(bf16[32,768]{1,0:T(8,128)(2,1)S(1)} %get-tuple-element.16), channel_id=1, source_target_pairs={{0,1},{1,2},{2,3},{3,0},{4,5},{5,6},{6,7},{7,4},{8,9},{9,10},{10,1... | collective-permute-start | bytes 147464 | tf_op jit(solution)/shard_map/ppermute | solution.py:219
  17.5 7.5 %collective-permute-start.1 = (bf16[32,768]{1,0:T(8,128)(2,1)S(1)}, bf16[32,768]{1,0:T(8,128)(2,1)S(1)}, u32[]{:S(2)}, u32[]{:S(2)}) collective-permute-start(bf16[32,768]{1,0:T(8,128)(2,1)S(1)} %get-tuple-element.17), channel_id=1, source_target_pairs={{0,2},{1,3},{2,0},{3,1},{4,6},{5,7},{6,4},{7,5},{8,10},{9,11},{10,... | collective-permute-start | bytes 147464 | tf_op jit(solution)/shard_map/ppermute | solution.py:219
  22.6 5.6 %collective-permute-start.2 = (bf16[32,768]{1,0:T(8,128)(2,1)S(1)}, bf16[32,768]{1,0:T(8,128)(2,1)S(1)}, u32[]{:S(2)}, u32[]{:S(2)}) collective-permute-start(bf16[32,768]{1,0:T(8,128)(2,1)S(1)} %get-tuple-element.18), channel_id=1, source_target_pairs={{0,3},{1,0},{2,1},{3,2},{4,7},{5,4},{6,5},{7,6},{8,11},{9,8},{10,9... | collective-permute-start | bytes 147464 | tf_op jit(solution)/shard_map/ppermute | solution.py:219
  25.0 3.2 %copy-start.5 = (bf16[32,768]{1,0:T(8,128)(2,1)}, bf16[32,768]{1,0:T(8,128)(2,1)S(1)}, u32[]{:S(2)}) copy-start(bf16[32,768]{1,0:T(8,128)(2,1)S(1)} %collective-permute-done.a) | copy-start | bytes 147460
  25.0 3.2 %copy-start.6 = (bf16[32,768]{1,0:T(8,128)(2,1)}, bf16[32,768]{1,0:T(8,128)(2,1)S(1)}, u32[]{:S(2)}) copy-start(bf16[32,768]{1,0:T(8,128)(2,1)S(1)} %collective-permute-done.1.b) | copy-start | bytes 147460
  28.2 0.6 copy-start.7
  30.5 3.6 %collective-permute-start.3 = (bf16[32,768]{1,0:T(8,128)(2,1)}, bf16[32,768]{1,0:T(8,128)(2,1)S(1)}, u32[]{:S(2)}, u32[]{:S(2)}) collective-permute-start(bf16[32,768]{1,0:T(8,128)(2,1)} %norm.1), channel_id=1, source_target_pairs={{0,32},{32,0},{1,33},{33,1},{2,34},{34,2},{3,35},{35,3},{4,36},{36... | collective-permute-start | bytes 147464 | tf_op jit(solution)/shard_map/ppermute | solution.py:221
  34.8 7.4 %collective-permute-start.4 = (bf16[64,768]{1,0:T(8,128)(2,1)S(1)}, bf16[64,768]{1,0:T(8,128)(2,1)S(1)}, u32[]{:S(2)}, u32[]{:S(2)}) collective-permute-start(bf16[64,768]{1,0:T(8,128)(2,1)S(1)} %pad_maximum_fusion.1), channel_id=1, source_target_pairs={{0,8},{8,16},{16,24},{24,0},{1,9},{9,17},{17,25},{25,1},{2,10},{10... | collective-permute-start | bytes 294920 | tf_op jit(solution)/shard_map/ppermute | solution.py:222
  36.1 6.1 %collective-permute-start.5 = (bf16[64,768]{1,0:T(8,128)(2,1)S(1)}, bf16[64,768]{1,0:T(8,128)(2,1)S(1)}, u32[]{:S(2)}, u32[]{:S(2)}) collective-permute-start(bf16[64,768]{1,0:T(8,128)(2,1)S(1)} %pad_maximum_fusion.1), channel_id=1, source_target_pairs={{0,24},{8,0},{16,8},{24,16},{1,25},{9,1},{17,9},{25,17},{2,26},{10... | collective-permute-start | bytes 294920 | tf_op jit(solution)/shard_map/ppermute | solution.py:222
  37.6 9.8 %collective-permute-start.6 = (bf16[64,768]{1,0:T(8,128)(2,1)S(1)}, bf16[64,768]{1,0:T(8,128)(2,1)S(1)}, u32[]{:S(2)}, u32[]{:S(2)}) collective-permute-start(bf16[64,768]{1,0:T(8,128)(2,1)S(1)} %pad_maximum_fusion.1), channel_id=1, source_target_pairs={{0,16},{8,24},{16,0},{24,8},{1,17},{9,25},{17,1},{25,9},{2,18},{10... | collective-permute-start | bytes 294920 | tf_op jit(solution)/shard_map/ppermute | solution.py:222
  47.5 9.2 %collective-permute-start.10 = (bf16[256,768]{1,0:T(8,128)(2,1)S(1)}, bf16[256,768]{1,0:T(8,128)(2,1)S(1)}, u32[]{:S(2)}, u32[]{:S(2)}) collective-permute-start(bf16[256,768]{1,0:T(8,128)(2,1)S(1)} %constant_dynamic-update-slice_fusion.refs_0_), channel_id=1, source_target_pairs={{0,192},{64,0},{128,64},{192,128},{1,193},{65,1},{129,65},{193,129... | collective-permute-start | bytes 1179656 | tf_op jit(solution)/shard_map/ppermute | solution.py:223
  50.2 17.8 %collective-permute-start.12 = (bf16[256,768]{1,0:T(8,128)(2,1)S(1)}, bf16[256,768]{1,0:T(8,128)(2,1)S(1)}, u32[]{:S(2)}, u32[]{:S(2)}) collective-permute-start(bf16[256,768]{1,0:T(8,128)(2,1)S(1)} %constant_dynamic-update-slice_fusion.refs_0_), channel_id=1, source_target_pairs={{0,128},{64,192},{128,0},{192,64},{1,129},{65,193},{129,1},{193,65... | collective-permute-start | bytes 1179656 | tf_op jit(solution)/shard_map/ppermute | solution.py:223
  50.6 20.6 %collective-permute-start.8 = (bf16[256,768]{1,0:T(8,128)(2,1)S(1)}, bf16[256,768]{1,0:T(8,128)(2,1)S(1)}, u32[]{:S(2)}, u32[]{:S(2)}) collective-permute-start(bf16[256,768]{1,0:T(8,128)(2,1)S(1)} %constant_dynamic-update-slice_fusion.refs_0_), channel_id=1, source_target_pairs={{0,64},{64,128},{128,192},{192,0},{1,65},{65,129},{129,193},{193,1... | collective-permute-start | bytes 1179656 | tf_op jit(solution)/shard_map/ppermute | solution.py:223
  51.3 41.9 %collective-permute-start.7 = (bf16[256,768]{1,0:T(8,128)(2,1)S(1)}, bf16[256,768]{1,0:T(8,128)(2,1)S(1)}, u32[]{:S(2)}, u32[]{:S(2)}) collective-permute-start(bf16[256,768]{1,0:T(8,128)(2,1)S(1)} %constant_dynamic-update-slice_fusion.refs_0_), channel_id=1, source_target_pairs={{0,4},{4,0},{1,5},{5,1},{2,6},{6,2},{3,7},{7,3},{8,12},{12,8},{9,1... | collective-permute-start | bytes 1179656 | tf_op jit(solution)/shard_map/ppermute | solution.py:224
  56.7 36.5 %collective-permute-start.11 = (bf16[256,768]{1,0:T(8,128)(2,1)S(1)}, bf16[256,768]{1,0:T(8,128)(2,1)S(1)}, u32[]{:S(2)}, u32[]{:S(2)}) collective-permute-start(bf16[256,768]{1,0:T(8,128)(2,1)S(1)} %collective-permute-done.10.refs_2_), channel_id=1, source_target_pairs={{0,4},{4,0},{1,5},{5,1},{2,6},{6,2},{3,7},{7,3},{8,12},{12,8},{9,1... | collective-permute-start | bytes 1179656 | tf_op jit(solution)/shard_map/ppermute | solution.py:224
  68.0 25.3 %collective-permute-start.13 = (bf16[256,768]{1,0:T(8,128)(2,1)S(1)}, bf16[256,768]{1,0:T(8,128)(2,1)S(1)}, u32[]{:S(2)}, u32[]{:S(2)}) collective-permute-start(bf16[256,768]{1,0:T(8,128)(2,1)S(1)} %collective-permute-done.12.refs_3_), channel_id=1, source_target_pairs={{0,4},{4,0},{1,5},{5,1},{2,6},{6,2},{3,7},{7,3},{8,12},{12,8},{9,1... | collective-permute-start | bytes 1179656 | tf_op jit(solution)/shard_map/ppermute | solution.py:224
  71.2 22.1 %collective-permute-start.9 = (bf16[256,768]{1,0:T(8,128)(2,1)S(1)}, bf16[256,768]{1,0:T(8,128)(2,1)S(1)}, u32[]{:S(2)}, u32[]{:S(2)}) collective-permute-start(bf16[256,768]{1,0:T(8,128)(2,1)S(1)} %collective-permute-done.8.refs_1_), channel_id=1, source_target_pairs={{0,4},{4,0},{1,5},{5,1},{2,6},{6,2},{3,7},{7,3},{8,12},{12,8},{9,1... | collective-permute-start | bytes 1179656 | tf_op jit(solution)/shard_map/ppermute | solution.py:224
Sparse Core Ops, SparseCore 0:
  9.2 51.9 all-gather.1

commit v2 on v1

v2 whole, which is shorter than its diff:
```python
import functools

import jax
import jax.numpy as jnp
from jax import lax
from jax.experimental import pallas as pl
from jax.experimental.pallas import tpu as pltpu
from jax.sharding import Mesh
from jax.sharding import PartitionSpec as P

HD = 128
HEADS_HERE = 3
WIDTH = HEADS_HERE * HD
EPSILON = 1e-06
FACTOR = HD**-0.5 * 1.4426950408889634
SEQ = ("x", "w", "y", "core")


def ring(count, shift):
    return [(i, (i + shift) % count) for i in range(count)]


def project_kernel(me_ref, hidden, wk, wv, own, first, second, third):
    step = pl.program_id(0)
    rows = hidden[...]
    k_part = jnp.dot(rows, wk[...], preferred_element_type=jnp.float32)
    v_part = jnp.dot(rows, wv[...], preferred_element_type=jnp.float32)

    @pl.when(step == 3)
    def _():
        own[:, :WIDTH] = k_part
        own[:, WIDTH:] = v_part

    for index, out in ((0, second), (1, first), (2, third)):

        @pl.when(step == index)
        def _():
            out[:, :WIDTH] = k_part.astype(jnp.bfloat16)
            out[:, WIDTH:] = v_part.astype(jnp.bfloat16)


def project(me, hidden, wk, wv):
    rows, depth = hidden.shape
    def group(step, me_ref):
        shift = jnp.where(step == 0, 2, jnp.where(step == 1, 1, jnp.where(step == 2, 3, 0)))
        return (0, lax.rem(me_ref[0] + shift, 4))

    whole = lambda step, me_ref: (0, 0)
    sent = jax.ShapeDtypeStruct((rows, 2 * WIDTH), jnp.bfloat16)
    return pl.pallas_call(
        project_kernel,
        out_shape=(jax.ShapeDtypeStruct((rows, 2 * WIDTH), jnp.float32), sent, sent, sent),
        grid_spec=pltpu.PrefetchScalarGridSpec(
            num_scalar_prefetch=1,
            grid=(4,),
            in_specs=[
                pl.BlockSpec((rows, depth), whole),
                pl.BlockSpec((depth, WIDTH), group),
                pl.BlockSpec((depth, WIDTH), group),
            ],
            out_specs=[pl.BlockSpec((rows, 2 * WIDTH), whole)] * 4,
        ),
        compiler_params=pltpu.CompilerParams(vmem_limit_bytes=8 << 20),
        cost_estimate=pl.CostEstimate(
            flops=2 * rows * depth * 8 * WIDTH, bytes_accessed=2 * depth * 8 * WIDTH, transcendentals=0
        ),
        name="project",
    )(me, hidden, wk, wv)


def norm_kernel(own, a, b, c, gain, out):
    total = (
        own[...]
        + a[...].astype(jnp.float32)
        + b[...].astype(jnp.float32)
        + c[...].astype(jnp.float32)
    )
    for head in range(HEADS_HERE):
        cols = slice(head * HD, (head + 1) * HD)
        raw = total[:, cols]
        scale = lax.rsqrt(jnp.mean(raw * raw, axis=1, keepdims=True) + EPSILON)
        out[:, cols] = (raw * scale * gain[...]).astype(jnp.bfloat16)
    out[:, WIDTH:] = total[:, WIDTH:].astype(jnp.bfloat16)


def norm(own, a, b, c, gain):
    rows = own.shape[0]
    return pl.pallas_call(
        norm_kernel,
        out_shape=jax.ShapeDtypeStruct((rows, 2 * WIDTH), jnp.bfloat16),
        compiler_params=pltpu.CompilerParams(vmem_limit_bytes=2 << 20),
        cost_estimate=pl.CostEstimate(flops=10 * own.size, bytes_accessed=12 * own.size, transcendentals=128),
        name="norm",
    )(own, a, b, c, gain)


def attend_kernel(moves, keys, chunk, block, fresh, q, *refs):
    operands = 1 + max(move[0] for move in moves)
    pieces, refs = refs[:operands], refs[operands:]
    if not fresh:
        carried, refs = refs[0], refs[1:]
    out, held, sems = refs
    copies = []
    for index, (operand, source, count, row, col, width) in enumerate(moves):
        copy = pltpu.make_async_copy(
            pieces[operand].at[pl.ds(source, count), :],
            held.at[pl.ds(row, count), pl.ds(col, width)],
            sems.at[index],
        )
        copy.start()
        copies.append((row, copy))
    ones = jnp.ones((chunk, HD), jnp.bfloat16)
    rows = q.shape[0]
    state = {}
    for base in range(0, keys, chunk):
        for begin, copy in copies:
            if base <= begin < base + chunk:
                copy.wait()
        for low in range(0, rows, block):
            here = slice(low, low + block)
            for head in range(HEADS_HERE):
                cols = slice(head * HD, (head + 1) * HD)
                vals = slice(WIDTH + head * HD, WIDTH + (head + 1) * HD)
                top_at = slice(WIDTH + head, WIDTH + head + 1)
                sum_at = slice(WIDTH + HEADS_HERE + head, WIDTH + HEADS_HERE + head + 1)
                if base:
                    old = state[low, head]
                elif fresh:
                    old = None
                else:
                    old = (carried[here, top_at], carried[here, sum_at], carried[here, cols])
                scores = lax.dot_general(
                    q[here, cols],
                    held[base : base + chunk, cols],
                    (((1,), (1,)), ((), ())),
                    preferred_element_type=jnp.float32,
                )
                raised = jnp.max(scores, axis=1, keepdims=True) * FACTOR
                if old is not None:
                    raised = jnp.maximum(raised, old[0])
                weights = jnp.exp2(scores * FACTOR - raised).astype(jnp.bfloat16)
                mixed = jnp.dot(
                    weights,
                    jnp.concatenate((held[base : base + chunk, vals], ones), axis=1),
                    preferred_element_type=jnp.float32,
                )
                acc, total = mixed[:, :HD], mixed[:, HD:]
                if old is not None:
                    rescale = jnp.exp2(old[0] - raised)
                    acc = old[2] * rescale + acc
                    total = old[1] * rescale + total
                state[low, head] = (raised, total, acc)
                if base + chunk >= keys:
                    out[here, cols] = acc
                    out[here, top_at] = raised
                    out[here, sum_at] = total[:, :1]


def attend(q, pieces, moves, carried=None, chunk=1024, block=256):
    rows = q.shape[0]
    keys = max(move[2] + move[3] for move in moves)
    chunk = min(chunk, keys)
    vmem, anywhere = pl.BlockSpec(memory_space=pltpu.VMEM), pl.BlockSpec(memory_space=pl.ANY)
    carried = () if carried is None else (carried,)
    pairs = rows * keys * HEADS_HERE
    return pl.pallas_call(
        functools.partial(attend_kernel, moves, keys, chunk, block, not carried),
        out_shape=jax.ShapeDtypeStruct((rows, WIDTH + HD), jnp.float32),
        in_specs=[vmem] + [anywhere] * len(pieces) + [vmem] * len(carried),
        out_specs=vmem,
        scratch_shapes=[
            pltpu.VMEM((keys, 2 * WIDTH), jnp.bfloat16),
            pltpu.SemaphoreType.DMA((len(moves),)),
        ],
        compiler_params=pltpu.CompilerParams(vmem_limit_bytes=20 << 20),
        cost_estimate=pl.CostEstimate(
            flops=4 * HD * pairs,
            bytes_accessed=4 * keys * WIDTH + 8 * rows * WIDTH,
            transcendentals=pairs,
        ),
        name="attend_more" if carried else "attend_view",
    )(q, *pieces, *carried)


def join_kernel(a, b, out):
    for head in range(HEADS_HERE):
        cols = slice(head * HD, (head + 1) * HD)
        top_at = slice(WIDTH + head, WIDTH + head + 1)
        sum_at = slice(WIDTH + HEADS_HERE + head, WIDTH + HEADS_HERE + head + 1)
        top_a, top_b = a[:, top_at], b[:, top_at]
        top = jnp.maximum(top_a, top_b)
        scale_a, scale_b = jnp.exp2(top_a - top), jnp.exp2(top_b - top)
        total = a[:, sum_at] * scale_a + b[:, sum_at] * scale_b
        out[:, cols] = ((a[:, cols] * scale_a + b[:, cols] * scale_b) / total).astype(jnp.bfloat16)


def join(a, b):
    return pl.pallas_call(
        join_kernel,
        out_shape=jax.ShapeDtypeStruct((a.shape[0], WIDTH), jnp.bfloat16),
        compiler_params=pltpu.CompilerParams(vmem_limit_bytes=8 << 20),
        cost_estimate=pl.CostEstimate(flops=6 * a.size, bytes_accessed=10 * a.size, transcendentals=6 * a.shape[0]),
        name="join",
    )(a, b)


def hop(block, axis, shift):
    return lax.ppermute(block, axis, ring(2 if axis in ("w", "core") else 4, shift))


def per_device(q_tok, k_tok, v_tok, ref_hidden, ref_wk, ref_wv, key_gain):
    rows = q_tok.shape[0]
    q_peer = hop(q_tok, "core", 1)
    k_back, v_ahead = hop(k_tok, "y", 1), hop(v_tok, "y", 3)
    k_ahead, v_back = hop(k_tok, "y", 3), hop(v_tok, "y", 1)
    ref_hidden, q_peer = lax.optimization_barrier((ref_hidden, q_peer))
    ref_wk, ref_wv = [pltpu.with_memory_space_constraint(w, pltpu.HBM) for w in (ref_wk, ref_wv)]

    me = lax.axis_index("tensor").astype(jnp.int32).reshape(1)
    own, *sent = project(me, ref_hidden, ref_wk, ref_wv)
    arrived = [hop(block, "tensor", shift) for shift, block in zip((1, 2, 3), sent)]
    arrived, k_back, v_ahead = lax.optimization_barrier((arrived, k_back, v_ahead))
    opposite = [hop(k_back, "y", 1), hop(v_ahead, "y", 3)]

    block = norm(own, *arrived, key_gain.reshape(1, HD))
    paired = hop(block, "w", 1)
    paired, k_ahead, v_back = lax.optimization_barrier((paired, k_ahead, v_back))
    block = jnp.concatenate((block, paired), axis=0)
    pieces = [block] + [hop(block, "x", s) for s in (1, 3, 2)]
    pieces, opposite = lax.optimization_barrier((pieces, opposite))
    block = jnp.concatenate(pieces, axis=0)
    pieces = [block] + [hop(block, "y", s) for s in (1, 3, 2)]

    view = [k_tok, v_tok, k_back, v_back, k_ahead, v_ahead] + opposite
    moves = [(i, 0, rows, i // 2 * rows, i % 2 * WIDTH, WIDTH) for i in range(8)]
    at_peer = attend(q_peer, view, moves)
    at_own = attend(q_tok, view, moves)
    pieces, at_peer, at_own = lax.optimization_barrier((pieces, at_peer, at_own))
    size = block.shape[0]
    moves = [(i, 0, size, i * size, 0, 2 * WIDTH) for i in range(4)]
    at_peer = attend(q_peer, pieces, moves, at_peer)
    from_peer = hop(at_peer, "core", 1)
    return join(attend(q_tok, pieces, moves, at_own), from_peer)


def solution(mesh):
    fine = Mesh(
        mesh.devices.reshape(4, 2, 4, 2, 4),
        ("x", "w", "y", "core", "tensor"),
    )
    placed = (
        P(SEQ, "tensor"),
        P(SEQ, "tensor"),
        P(SEQ, "tensor"),
        P(SEQ, "tensor"),
        P("tensor", None),
        P("tensor", None),
        P(),
    )
    return jax.shard_map(
        per_device, mesh=fine, in_specs=placed, out_specs=P(SEQ, "tensor"), check_vma=False
    )
```

time: 107 us -> 72.2 us (0.67)
  between operations: 13.5 us -> 0.16 us
  Pallas kernels: 31.7 us -> 23.9 us
  starting transfers between devices: 35 us -> 29 us
  local copies, waits for them, and re-layouts: 4.58 us -> 0.85 us
  other arithmetic: 3.01 us -> 0.01 us
    pallas_call x3 -> x5, Pallas kernels: 28.3 us -> 20.1 us  [the longest x4 18.2 us: attend(): pl.pallas_call(functools.partial(attend_kernel, moves, keys, chunk, block...]
    ppermute x14 -> x18, starting transfers between devices: 35 us -> 29 us  [hop(): lax.ppermute(block, axis, ring(2 if axis in ('w', 'core') else 4, shift))]
    unnamed x20 -> x13, local copies, waits for them, and re-layouts: 4.57 us -> 0.84 us
    concatenate x2 -> x1, other arithmetic: 3.01 us -> 0.01 us  [per_device(): block = jnp.concatenate((block, paired), axis=0)]
    pallas_call x1, Pallas kernels: 1.77 us -> 3.69 us  [project(): pl.pallas_call(project_kernel, out_shape=(jax.ShapeDtypeStruct((rows, 2 *...]
    pallas_call x1, Pallas kernels: 1.68 us -> 0.11 us  [norm(): pl.pallas_call(norm_kernel, out_shape=jax.ShapeDtypeStruct((rows, 2 * WID...]
    ppermute x14 -> x18, waiting for transfers between devices: 19 us -> 18 us  [hop(): lax.ppermute(block, axis, ring(2 if axis in ('w', 'core') else 4, shift))]
  transfers between devices with their start and end apart: 15 -> 18, of which waited for: 6 -> 8; matrix products, arithmetic and copies ran while one was open for 2% -> 0% of each run, Pallas kernels for 23% -> 25%
where the time goes in v2:
time: 72.2 us; the launch traced here: 72 us
  starting transfers between devices  29 us (40%)
  Pallas kernels  23.9 us (33%)
  waiting for transfers between devices  18 us (25%)
  local copies, waits for them, and re-layouts  0.85 us (1%)
    ppermute x18, starting transfers between devices, hop(): lax.ppermute(block, axis, ring(2 if axis in ('w', 'core') else 4, shift))  29 us
    pallas_call x4, Pallas kernels, attend(): pl.pallas_call(functools.partial(attend_kernel, moves, keys, chunk, block...  18.2 us
    ppermute x18, waiting for transfers between devices, hop(): lax.ppermute(block, axis, ring(2 if axis in ('w', 'core') else 4, shift))  18 us
    pallas_call x1, Pallas kernels, project(): pl.pallas_call(project_kernel, out_shape=(jax.ShapeDtypeStruct((rows, 2 *...  3.69 us
    pallas_call x1, Pallas kernels, join(): pl.pallas_call(join_kernel, out_shape=jax.ShapeDtypeStruct((a.shape[0], W...  1.96 us
  transfers between devices with their start and end apart: 18, of which 8 were waited for; matrix products, arithmetic and copies ran while one was open for 0% of the time, Pallas kernels for 25%

profile of v2, /device:TPU:1, one launch (start us, length us, event | category | flops | bytes accessed | tf_op | source)
XLA Modules:
  0.0 72.0 jit_solution(9847060762390005715)
XLA Ops:
  0.0 3.2 %collective-permute-start = (bf16[512,384]{1,0:T(8,128)(2,1)}, bf16[512,384]{1,0:T(8,128)(2,1)S(1)}, u32[]{:S(2)}, u32[]{:S(2)}) collective-permute-start(bf16[512,384]{1,0:T(8,128)(2,1)} %q.3), channel_id=1, source_target_pairs={{0,4},{4,0},{1,5},{5,1},{2,6},{6,2},{3,7},{7,3},{8,12},{12,8},{9,1... | collective-permute-start | bytes 1179656 | tf_op jit(solution)/shard_map/ppermute | solution.py:208
  3.2 2.7 %collective-permute-start.5 = (bf16[512,384]{1,0:T(8,128)(2,1)}, bf16[512,384]{1,0:T(8,128)(2,1)S(1)}, u32[]{:S(2)}, u32[]{:S(2)}) collective-permute-start(bf16[512,384]{1,0:T(8,128)(2,1)} %refs_1_.3), channel_id=1, source_target_pairs={{0,24},{8,0},{16,8},{24,16},{1,25},{9,1},{17,9},{25,17},{2,26},{10... | collective-permute-start | bytes 1179656 | tf_op jit(solution)/shard_map/ppermute | solution.py:208
  6.0 1.4 %collective-permute-start.8 = (bf16[512,384]{1,0:T(8,128)(2,1)}, bf16[512,384]{1,0:T(8,128)(2,1)S(1)}, u32[]{:S(2)}, u32[]{:S(2)}) collective-permute-start(bf16[512,384]{1,0:T(8,128)(2,1)} %refs_1_.3), channel_id=1, source_target_pairs={{0,8},{8,16},{16,24},{24,0},{1,9},{9,17},{17,25},{25,1},{2,10},{10... | collective-permute-start | bytes 1179656 | tf_op jit(solution)/shard_map/ppermute | solution.py:208
  7.4 0.8 %copy-done.1 = bf16[32,768]{1,0:T(8,128)(2,1)S(1)} copy-done((bf16[32,768]{1,0:T(8,128)(2,1)S(1)}, bf16[32,768]{1,0:T(8,128)(2,1)}, u32[]{:S(2)}) %copy-start.1) | copy-done | bytes 49176
  8.2 3.7 %project.1 = (f32[32,768]{1,0:T(8,128)S(1)}, bf16[32,768]{1,0:T(8,128)(2,1)S(1)}, bf16[32,768]{1,0:T(8,128)(2,1)S(1)}, bf16[32,768]{1,0:T(8,128)(2,1)S(1)}) custom-call(s32[1]{0:T(128)} %bitcast.me_ref, bf16[32,768]{1,0:T(8,128)(2,1)S(1)} %copy-done.1, bf16[768,1536]{1,0:T(8,128)(2,1)} %wk.1, bf16[768,1536]{1,0:T(8,128)(2,1)} %wv.1), custom_call_target="tpu_custom_call" | custom-call | flops 150994944 | bytes 4718592 | tf_op jit(solution)/shard_map/project/pallas_call | solution.py:50
  11.9 1.4 %collective-permute-start.1 = (bf16[32,768]{1,0:T(8,128)(2,1)S(1)}, bf16[32,768]{1,0:T(8,128)(2,1)S(1)}, u32[]{:S(2)}, u32[]{:S(2)}) collective-permute-start(bf16[32,768]{1,0:T(8,128)(2,1)S(1)} %get-tuple-element.33), channel_id=1, source_target_pairs={{0,1},{1,2},{2,3},{3,0},{4,5},{5,6},{6,7},{7,4},{8,9},{9,10},{10,1... | collective-permute-start | bytes 147464 | tf_op jit(solution)/shard_map/ppermute | solution.py:208
  13.3 2.1 %collective-permute-done.4.refs_2_ = bf16[512,384]{1,0:T(8,128)(2,1)S(1)} collective-permute-done((bf16[512,384]{1,0:T(8,128)(2,1)}, bf16[512,384]{1,0:T(8,128)(2,1)S(1)}, u32[]{:S(2)}, u32[]{:S(2)}) %collective-permute-start.4) | collective-permute-done | bytes 393248 | tf_op jit(solution)/shard_map/ppermute | solution.py:208
  15.4 5.3 %collective-permute-start.2 = (bf16[32,768]{1,0:T(8,128)(2,1)S(1)}, bf16[32,768]{1,0:T(8,128)(2,1)S(1)}, u32[]{:S(2)}, u32[]{:S(2)}) collective-permute-start(bf16[32,768]{1,0:T(8,128)(2,1)S(1)} %get-tuple-element.34), channel_id=1, source_target_pairs={{0,2},{1,3},{2,0},{3,1},{4,6},{5,7},{6,4},{7,5},{8,10},{9,11},{10,... | collective-permute-start | bytes 147464 | tf_op jit(solution)/shard_map/ppermute | solution.py:208
  20.8 1.8 %collective-permute-done.2.b = bf16[32,768]{1,0:T(8,128)(2,1)S(1)} collective-permute-done((bf16[32,768]{1,0:T(8,128)(2,1)S(1)}, bf16[32,768]{1,0:T(8,128)(2,1)S(1)}, u32[]{:S(2)}, u32[]{:S(2)}) %collective-permute-start.2) | collective-permute-done | bytes 49184 | tf_op jit(solution)/shard_map/ppermute | solution.py:208
  22.5 3.8 %collective-permute-done.3.c = bf16[32,768]{1,0:T(8,128)(2,1)S(1)} collective-permute-done((bf16[32,768]{1,0:T(8,128)(2,1)S(1)}, bf16[32,768]{1,0:T(8,128)(2,1)S(1)}, u32[]{:S(2)}, u32[]{:S(2)}) %collective-permute-start.3) | collective-permute-done | bytes 49184 | tf_op jit(solution)/shard_map/ppermute | solution.py:208
  26.3 2.7 %collective-permute-start.13 = (bf16[512,384]{1,0:T(8,128)(2,1)S(1)}, bf16[512,384]{1,0:T(8,128)(2,1)S(1)}, u32[]{:S(2)}, u32[]{:S(2)}) collective-permute-start(bf16[512,384]{1,0:T(8,128)(2,1)S(1)} %collective-permute-done.5.refs_5_), channel_id=1, source_target_pairs={{0,24},{8,0},{16,8},{24,16},{1,25},{9,1},{17,9},{25,17},{2,26},{10... | collective-permute-start | bytes 1179656 | tf_op jit(solution)/shard_map/ppermute | solution.py:208
  29.2 3.2 %collective-permute-done.6 = bf16[32,768]{1,0:T(8,128)(2,1)S(1)} collective-permute-done((bf16[32,768]{1,0:T(8,128)(2,1)S(1)}, bf16[32,768]{1,0:T(8,128)(2,1)S(1)}, u32[]{:S(2)}, u32[]{:S(2)}) %collective-permute-start.6) | collective-permute-done | bytes 49184 | tf_op jit(solution)/shard_map/ppermute | solution.py:208
  32.4 2.6 %collective-permute-start.10 = (bf16[64,768]{1,0:T(8,128)(2,1)S(1)}, bf16[64,768]{1,0:T(8,128)(2,1)S(1)}, u32[]{:S(2)}, u32[]{:S(2)}) collective-permute-start(bf16[64,768]{1,0:T(8,128)(2,1)S(1)} %pad_maximum_fusion), channel_id=1, source_target_pairs={{0,192},{64,0},{128,64},{192,128},{1,193},{65,1},{129,65},{193,129... | collective-permute-start | bytes 294920 | tf_op jit(solution)/shard_map/ppermute | solution.py:208
  35.5 0.6 collective-permute-start.9
  36.6 3.4 %collective-permute-done.11 = bf16[64,768]{1,0:T(8,128)(2,1)S(1)} collective-permute-done((bf16[64,768]{1,0:T(8,128)(2,1)S(1)}, bf16[64,768]{1,0:T(8,128)(2,1)S(1)}, u32[]{:S(2)}, u32[]{:S(2)}) %collective-permute-start.11) | collective-permute-done | bytes 98336 | tf_op jit(solution)/shard_map/ppermute | solution.py:208
  40.1 1.0 %collective-permute-done.9 = bf16[64,768]{1,0:T(8,128)(2,1)S(1)} collective-permute-done((bf16[64,768]{1,0:T(8,128)(2,1)S(1)}, bf16[64,768]{1,0:T(8,128)(2,1)S(1)}, u32[]{:S(2)}, u32[]{:S(2)}) %collective-permute-start.9) | collective-permute-done | bytes 98336 | tf_op jit(solution)/shard_map/ppermute | solution.py:208
  41.2 2.7 %collective-permute-start.15 = (bf16[256,768]{1,0:T(8,128)(2,1)S(1)}, bf16[256,768]{1,0:T(8,128)(2,1)S(1)}, u32[]{:S(2)}, u32[]{:S(2)}) collective-permute-start(bf16[256,768]{1,0:T(8,128)(2,1)S(1)} %constant_dynamic-update-slice_fusion.refs_0_), channel_id=1, source_target_pairs={{0,24},{8,0},{16,8},{24,16},{1,25},{9,1},{17,9},{25,17},{2,26},{10... | collective-permute-start | bytes 1179656 | tf_op jit(solution)/shard_map/ppermute | solution.py:208
  43.9 5.3 %attend_view.3.refs_4_ = f32[512,512]{1,0:T(8,128)S(1)} custom-call(bf16[512,384]{1,0:T(8,128)(2,1)S(1)} %copy-done, bf16[512,384]{1,0:T(8,128)(2,1)S(1)} %copy-done.3, bf16[512,384]{1,0:T(8,128)(2,1)S(1)} %copy-done.4, bf16[512,384]{1,0:T(8,128)(2,1)S(1)} %collective-permute-done.4.refs_2_, bf16[512,384]{1,0:T(8,128)(2,1)S(1)} %collective-permute-done.8.refs_3_, ...), custom_call_target="tpu_custom_call" | custom-call | flops 1610612736 | bytes 4718592 | tf_op jit(solution)/shard_map/attend_view/pallas_call | solution.py:166
  49.2 5.3 %attend_view.2.refs_4_ = f32[512,512]{1,0:T(8,128)S(1)} custom-call(bf16[512,384]{1,0:T(8,128)(2,1)S(1)} %collective-permute-done.q, bf16[512,384]{1,0:T(8,128)(2,1)S(1)} %copy-done.3, bf16[512,384]{1,0:T(8,128)(2,1)S(1)} %copy-done.4, bf16[512,384]{1,0:T(8,128)(2,1)S(1)} %collective-permute-done.4.refs_2_, ...), custom_call_target="tpu_custom_call" | custom-call | flops 1610612736 | bytes 4718592 | tf_op jit(solution)/shard_map/attend_view/pallas_call | solution.py:166
  54.5 2.3 %collective-permute-done.16.refs_3_ = bf16[256,768]{1,0:T(8,128)(2,1)S(1)} collective-permute-done((bf16[256,768]{1,0:T(8,128)(2,1)S(1)}, bf16[256,768]{1,0:T(8,128)(2,1)S(1)}, u32[]{:S(2)}, u32[]{:S(2)}) %collective-permute-start.16) | collective-permute-done | bytes 393248 | tf_op jit(solution)/shard_map/ppermute | solution.py:208
  56.8 3.9 %attend_more.3 = f32[512,512]{1,0:T(8,128)S(1)} custom-call(bf16[512,384]{1,0:T(8,128)(2,1)S(1)} %collective-permute-done.q, bf16[256,768]{1,0:T(8,128)(2,1)S(1)} %constant_dynamic-update-slice_fusion.refs_0_, bf16[256,768]{1,0:T(8,128)(2,1)S(1)} %collective-permute-done.14.refs_1_, bf16[256,768]{1,0:T(8,128)(2,1)S(1)} %collective-permute-done.15.refs_2_, ...), custom_call_target="tpu_custom_call" | custom-call | flops 805306368 | bytes 3145728 | tf_op jit(solution)/shard_map/attend_more/pallas_call | solution.py:166
  60.7 5.7 %collective-permute-start.17 = (f32[512,512]{1,0:T(8,128)S(1)}, f32[512,512]{1,0:T(8,128)S(1)}, u32[]{:S(2)}, u32[]{:S(2)}) collective-permute-start(f32[512,512]{1,0:T(8,128)S(1)} %attend_more.3), channel_id=1, source_target_pairs={{0,4},{4,0},{1,5},{5,1},{2,6},{6,2},{3,7},{7,3},{8,12},{12,8},{9,1... | collective-permute-start | bytes 3145736 | tf_op jit(solution)/shard_map/ppermute | solution.py:208
  66.3 3.7 %attend_more.2.a = f32[512,512]{1,0:T(8,128)S(1)} custom-call(bf16[512,384]{1,0:T(8,128)(2,1)S(1)} %copy-done, bf16[256,768]{1,0:T(8,128)(2,1)S(1)} %constant_dynamic-update-slice_fusion.refs_0_, bf16[256,768]{1,0:T(8,128)(2,1)S(1)} %collective-permute-done.14.refs_1_, bf16[256,768]{1,0:T(8,128)(2,1)S(1)} %collective-permute-done.15.refs_2_, ...), custom_call_target="tpu_custom_call" | custom-call | flops 805306368 | bytes 3145728 | tf_op jit(solution)/shard_map/attend_more/pallas_call | solution.py:166
  70.0 2.0 %join.1 = bf16[512,384]{1,0:T(8,128)(2,1)} custom-call(f32[512,512]{1,0:T(8,128)S(1)} %attend_more.2.a, f32[512,512]{1,0:T(8,128)S(1)} %collective-permute-done.17.b), custom_call_target="tpu_custom_call" | custom-call | flops 1572864 | bytes 2621440 | tf_op jit(solution)/shard_map/join/pallas_call | solution.py:198
  (34 shorter events, 1.5 us)
Async XLA Ops:
  0.0 7.4 %collective-permute-start = (bf16[512,384]{1,0:T(8,128)(2,1)}, bf16[512,384]{1,0:T(8,128)(2,1)S(1)}, u32[]{:S(2)}, u32[]{:S(2)}) collective-permute-start(bf16[512,384]{1,0:T(8,128)(2,1)} %q.3), channel_id=1, source_target_pairs={{0,4},{4,0},{1,5},{5,1},{2,6},{6,2},{3,7},{7,3},{8,12},{12,8},{9,1... | collective-permute-start | bytes 1179656 | tf_op jit(solution)/shard_map/ppermute | solution.py:208
  3.2 12.2 %collective-permute-start.4 = (bf16[512,384]{1,0:T(8,128)(2,1)}, bf16[512,384]{1,0:T(8,128)(2,1)S(1)}, u32[]{:S(2)}, u32[]{:S(2)}) collective-permute-start(bf16[512,384]{1,0:T(8,128)(2,1)} %refs_0_.3), channel_id=1, source_target_pairs={{0,8},{8,16},{16,24},{24,0},{1,9},{9,17},{17,25},{25,1},{2,10},{10... | collective-permute-start | bytes 1179656 | tf_op jit(solution)/shard_map/ppermute | solution.py:208
  3.2 17.5 %collective-permute-start.5 = (bf16[512,384]{1,0:T(8,128)(2,1)}, bf16[512,384]{1,0:T(8,128)(2,1)S(1)}, u32[]{:S(2)}, u32[]{:S(2)}) collective-permute-start(bf16[512,384]{1,0:T(8,128)(2,1)} %refs_1_.3), channel_id=1, source_target_pairs={{0,24},{8,0},{16,8},{24,16},{1,25},{9,1},{17,9},{25,17},{2,26},{10... | collective-permute-start | bytes 1179656 | tf_op jit(solution)/shard_map/ppermute | solution.py:208
  5.9 23.3 %collective-permute-start.7 = (bf16[512,384]{1,0:T(8,128)(2,1)}, bf16[512,384]{1,0:T(8,128)(2,1)S(1)}, u32[]{:S(2)}, u32[]{:S(2)}) collective-permute-start(bf16[512,384]{1,0:T(8,128)(2,1)} %refs_0_.3), channel_id=1, source_target_pairs={{0,24},{8,0},{16,8},{24,16},{1,25},{9,1},{17,9},{25,17},{2,26},{10... | collective-permute-start | bytes 1179656 | tf_op jit(solution)/shard_map/ppermute | solution.py:208
  6.0 23.3 %collective-permute-start.8 = (bf16[512,384]{1,0:T(8,128)(2,1)}, bf16[512,384]{1,0:T(8,128)(2,1)S(1)}, u32[]{:S(2)}, u32[]{:S(2)}) collective-permute-start(bf16[512,384]{1,0:T(8,128)(2,1)} %refs_1_.3), channel_id=1, source_target_pairs={{0,8},{8,16},{16,24},{24,0},{1,9},{9,17},{17,25},{25,1},{2,10},{10... | collective-permute-start | bytes 1179656 | tf_op jit(solution)/shard_map/ppermute | solution.py:208
  7.4 0.8 %copy-start.1 = (bf16[32,768]{1,0:T(8,128)(2,1)S(1)}, bf16[32,768]{1,0:T(8,128)(2,1)}, u32[]{:S(2)}) copy-start(bf16[32,768]{1,0:T(8,128)(2,1)} %hidden) | copy-start | bytes 147460
  8.2 20.8 %copy-start.2 = (f32[128]{0:T(128)S(1)}, f32[128]{0:T(128)}, u32[]{:S(2)}) copy-start(f32[128]{0:T(128)} %param.13) | copy-start | bytes 1540
  8.2 35.7 %copy-start = (bf16[512,384]{1,0:T(8,128)(2,1)S(1)}, bf16[512,384]{1,0:T(8,128)(2,1)}, u32[]{:S(2)}) copy-start(bf16[512,384]{1,0:T(8,128)(2,1)} %q.3) | copy-start | bytes 1179652
  8.2 35.7 %copy-start.3 = (bf16[512,384]{1,0:T(8,128)(2,1)S(1)}, bf16[512,384]{1,0:T(8,128)(2,1)}, u32[]{:S(2)}) copy-start(bf16[512,384]{1,0:T(8,128)(2,1)} %refs_0_.3) | copy-start | bytes 1179652
  8.2 35.7 %copy-start.4 = (bf16[512,384]{1,0:T(8,128)(2,1)S(1)}, bf16[512,384]{1,0:T(8,128)(2,1)}, u32[]{:S(2)}) copy-start(bf16[512,384]{1,0:T(8,128)(2,1)} %refs_1_.3) | copy-start | bytes 1179652
  11.9 8.9 %collective-permute-start.1 = (bf16[32,768]{1,0:T(8,128)(2,1)S(1)}, bf16[32,768]{1,0:T(8,128)(2,1)S(1)}, u32[]{:S(2)}, u32[]{:S(2)}) collective-permute-start(bf16[32,768]{1,0:T(8,128)(2,1)S(1)} %get-tuple-element.33), channel_id=1, source_target_pairs={{0,1},{1,2},{2,3},{3,0},{4,5},{5,6},{6,7},{7,4},{8,9},{9,10},{10,1... | collective-permute-start | bytes 147464 | tf_op jit(solution)/shard_map/ppermute | solution.py:208
  15.4 7.1 %collective-permute-start.2 = (bf16[32,768]{1,0:T(8,128)(2,1)S(1)}, bf16[32,768]{1,0:T(8,128)(2,1)S(1)}, u32[]{:S(2)}, u32[]{:S(2)}) collective-permute-start(bf16[32,768]{1,0:T(8,128)(2,1)S(1)} %get-tuple-element.34), channel_id=1, source_target_pairs={{0,2},{1,3},{2,0},{3,1},{4,6},{5,7},{6,4},{7,5},{8,10},{9,11},{10,... | collective-permute-start | bytes 147464 | tf_op jit(solution)/shard_map/ppermute | solution.py:208
  20.7 5.6 %collective-permute-start.3 = (bf16[32,768]{1,0:T(8,128)(2,1)S(1)}, bf16[32,768]{1,0:T(8,128)(2,1)S(1)}, u32[]{:S(2)}, u32[]{:S(2)}) collective-permute-start(bf16[32,768]{1,0:T(8,128)(2,1)S(1)} %get-tuple-element.35), channel_id=1, source_target_pairs={{0,3},{1,0},{2,1},{3,2},{4,7},{5,4},{6,5},{7,6},{8,11},{9,8},{10,9... | collective-permute-start | bytes 147464 | tf_op jit(solution)/shard_map/ppermute | solution.py:208
  26.3 14.7 %collective-permute-start.12 = (bf16[512,384]{1,0:T(8,128)(2,1)S(1)}, bf16[512,384]{1,0:T(8,128)(2,1)S(1)}, u32[]{:S(2)}, u32[]{:S(2)}) collective-permute-start(bf16[512,384]{1,0:T(8,128)(2,1)S(1)} %collective-permute-done.4.refs_2_), channel_id=1, source_target_pairs={{0,8},{8,16},{16,24},{24,0},{1,9},{9,17},{17,25},{25,1},{2,10},{10... | collective-permute-start | bytes 1179656 | tf_op jit(solution)/shard_map/ppermute | solution.py:208
  26.3 14.7 %collective-permute-start.13 = (bf16[512,384]{1,0:T(8,128)(2,1)S(1)}, bf16[512,384]{1,0:T(8,128)(2,1)S(1)}, u32[]{:S(2)}, u32[]{:S(2)}) collective-permute-start(bf16[512,384]{1,0:T(8,128)(2,1)S(1)} %collective-permute-done.5.refs_5_), channel_id=1, source_target_pairs={{0,24},{8,0},{16,8},{24,16},{1,25},{9,1},{17,9},{25,17},{2,26},{10... | collective-permute-start | bytes 1179656 | tf_op jit(solution)/shard_map/ppermute | solution.py:208
  29.1 3.3 %collective-permute-start.6 = (bf16[32,768]{1,0:T(8,128)(2,1)S(1)}, bf16[32,768]{1,0:T(8,128)(2,1)S(1)}, u32[]{:S(2)}, u32[]{:S(2)}) collective-permute-start(bf16[32,768]{1,0:T(8,128)(2,1)S(1)} %norm.1), channel_id=1, source_target_pairs={{0,32},{32,0},{1,33},{33,1},{2,34},{34,2},{3,35},{35,3},{4,36},{36... | collective-permute-start | bytes 147464 | tf_op jit(solution)/shard_map/ppermute | solution.py:208
  32.4 4.2 %collective-permute-start.10 = (bf16[64,768]{1,0:T(8,128)(2,1)S(1)}, bf16[64,768]{1,0:T(8,128)(2,1)S(1)}, u32[]{:S(2)}, u32[]{:S(2)}) collective-permute-start(bf16[64,768]{1,0:T(8,128)(2,1)S(1)} %pad_maximum_fusion), channel_id=1, source_target_pairs={{0,192},{64,0},{128,64},{192,128},{1,193},{65,1},{129,65},{193,129... | collective-permute-start | bytes 294920 | tf_op jit(solution)/shard_map/ppermute | solution.py:208
  35.0 5.1 %collective-permute-start.11 = (bf16[64,768]{1,0:T(8,128)(2,1)S(1)}, bf16[64,768]{1,0:T(8,128)(2,1)S(1)}, u32[]{:S(2)}, u32[]{:S(2)}) collective-permute-start(bf16[64,768]{1,0:T(8,128)(2,1)S(1)} %pad_maximum_fusion), channel_id=1, source_target_pairs={{0,128},{64,192},{128,0},{192,64},{1,129},{65,193},{129,1},{193,65... | collective-permute-start | bytes 294920 | tf_op jit(solution)/shard_map/ppermute | solution.py:208
  35.5 5.5 %collective-permute-start.9 = (bf16[64,768]{1,0:T(8,128)(2,1)S(1)}, bf16[64,768]{1,0:T(8,128)(2,1)S(1)}, u32[]{:S(2)}, u32[]{:S(2)}) collective-permute-start(bf16[64,768]{1,0:T(8,128)(2,1)S(1)} %pad_maximum_fusion), channel_id=1, source_target_pairs={{0,64},{64,128},{128,192},{192,0},{1,65},{65,129},{129,193},{193,1... | collective-permute-start | bytes 294920 | tf_op jit(solution)/shard_map/ppermute | solution.py:208
  41.1 13.4 %collective-permute-start.14 = (bf16[256,768]{1,0:T(8,128)(2,1)S(1)}, bf16[256,768]{1,0:T(8,128)(2,1)S(1)}, u32[]{:S(2)}, u32[]{:S(2)}) collective-permute-start(bf16[256,768]{1,0:T(8,128)(2,1)S(1)} %constant_dynamic-update-slice_fusion.refs_0_), channel_id=1, source_target_pairs={{0,8},{8,16},{16,24},{24,0},{1,9},{9,17},{17,25},{25,1},{2,10},{10... | collective-permute-start | bytes 1179656 | tf_op jit(solution)/shard_map/ppermute | solution.py:208
  41.2 13.3 %collective-permute-start.15 = (bf16[256,768]{1,0:T(8,128)(2,1)S(1)}, bf16[256,768]{1,0:T(8,128)(2,1)S(1)}, u32[]{:S(2)}, u32[]{:S(2)}) collective-permute-start(bf16[256,768]{1,0:T(8,128)(2,1)S(1)} %constant_dynamic-update-slice_fusion.refs_0_), channel_id=1, source_target_pairs={{0,24},{8,0},{16,8},{24,16},{1,25},{9,1},{17,9},{25,17},{2,26},{10... | collective-permute-start | bytes 1179656 | tf_op jit(solution)/shard_map/ppermute | solution.py:208
  43.8 12.9 %collective-permute-start.16 = (bf16[256,768]{1,0:T(8,128)(2,1)S(1)}, bf16[256,768]{1,0:T(8,128)(2,1)S(1)}, u32[]{:S(2)}, u32[]{:S(2)}) collective-permute-start(bf16[256,768]{1,0:T(8,128)(2,1)S(1)} %constant_dynamic-update-slice_fusion.refs_0_), channel_id=1, source_target_pairs={{0,16},{8,24},{16,0},{24,8},{1,17},{9,25},{17,1},{25,9},{2,18},{10... | collective-permute-start | bytes 1179656 | tf_op jit(solution)/shard_map/ppermute | solution.py:208
  60.7 9.4 %collective-permute-start.17 = (f32[512,512]{1,0:T(8,128)S(1)}, f32[512,512]{1,0:T(8,128)S(1)}, u32[]{:S(2)}, u32[]{:S(2)}) collective-permute-start(f32[512,512]{1,0:T(8,128)S(1)} %attend_more.3), channel_id=1, source_target_pairs={{0,4},{4,0},{1,5},{5,1},{2,6},{6,2},{3,7},{7,3},{8,12},{12,8},{9,1... | collective-permute-start | bytes 3145736 | tf_op jit(solution)/shard_map/ppermute | solution.py:208

commit v3 on v2

v3 whole, which is shorter than its diff:
```python
import functools

import jax
import jax.numpy as jnp
from jax import lax
from jax.experimental import pallas as pl
from jax.experimental.pallas import tpu as pltpu
from jax.sharding import Mesh
from jax.sharding import PartitionSpec as P

HD = 128
HEADS_HERE = 3
WIDTH = HEADS_HERE * HD
EPSILON = 1e-06
FACTOR = HD**-0.5 * 1.4426950408889634
SEQ = ("x", "w", "y", "core")
SMALL, BULK = "y", "x"


def ring(count, shift):
    return [(i, (i + shift) % count) for i in range(count)]


def project_kernel(hidden, wk, wv, k_tok, v_tok, own, near, far, next_to, beside, rows, weights, sems):
    me = lax.axis_index("tensor")
    first = pltpu.make_async_copy(hidden, rows, sems.at[8])
    first.start()
    copies = []
    for place, ahead in enumerate((1, 2, 3, 0)):
        peer = lax.rem(me + ahead, 4)
        cols = pl.ds(pl.multiple_of(peer * WIDTH, WIDTH), WIDTH)
        for half, source in enumerate((wk, wv)):
            slot = 2 * place + half
            copy = pltpu.make_async_copy(source.at[:, cols], weights.at[slot], sems.at[slot])
            copy.start()
            copies.append(copy)
    sides = []
    for half, source in enumerate((k_tok, v_tok)):
        copy = pltpu.make_async_copy(source, beside.at[:, pl.ds(half * WIDTH, WIDTH)], sems.at[9 + half])
        copy.start()
        sides.append(copy)
    first.wait()
    for place, out in enumerate((near, far, next_to, own)):
        for half in range(2):
            slot = 2 * place + half
            copies[slot].wait()
            part = jnp.dot(rows[...], weights[slot], preferred_element_type=jnp.float32)
            out[:, half * WIDTH : (half + 1) * WIDTH] = part.astype(out.dtype)
    for copy in sides:
        copy.wait()


def project(hidden, wk, wv, k_tok, v_tok):
    rows, depth = hidden.shape
    sent = jax.ShapeDtypeStruct((rows, 2 * WIDTH), jnp.bfloat16)
    vmem, anywhere = pl.BlockSpec(memory_space=pltpu.VMEM), pl.BlockSpec(memory_space=pl.ANY)
    return pl.pallas_call(
        project_kernel,
        out_shape=(
            jax.ShapeDtypeStruct((rows, 2 * WIDTH), jnp.float32),
            sent,
            sent,
            sent,
            jax.ShapeDtypeStruct((k_tok.shape[0], 2 * WIDTH), jnp.bfloat16),
        ),
        in_specs=[anywhere] * 5,
        out_specs=(vmem,) * 4 + (anywhere,),
        scratch_shapes=[
            pltpu.VMEM((rows, depth), jnp.bfloat16),
            pltpu.VMEM((8, depth, WIDTH), jnp.bfloat16),
            pltpu.SemaphoreType.DMA((11,)),
        ],
        compiler_params=pltpu.CompilerParams(vmem_limit_bytes=8 << 20),
        cost_estimate=pl.CostEstimate(
            flops=2 * rows * depth * 8 * WIDTH, bytes_accessed=2 * depth * 8 * WIDTH, transcendentals=0
        ),
        name="project",
    )(hidden, wk, wv, k_tok, v_tok)


def norm_kernel(own, a, b, c, gain, out):
    total = (
        own[...]
        + a[...].astype(jnp.float32)
        + b[...].astype(jnp.float32)
        + c[...].astype(jnp.float32)
    )
    for head in range(HEADS_HERE):
        cols = slice(head * HD, (head + 1) * HD)
        raw = total[:, cols]
        scale = lax.rsqrt(jnp.mean(raw * raw, axis=1, keepdims=True) + EPSILON)
        out[:, cols] = (raw * scale * gain[...]).astype(jnp.bfloat16)
    out[:, WIDTH:] = total[:, WIDTH:].astype(jnp.bfloat16)


def norm(own, a, b, c, gain):
    rows = own.shape[0]
    return pl.pallas_call(
        norm_kernel,
        out_shape=jax.ShapeDtypeStruct((rows, 2 * WIDTH), jnp.bfloat16),
        compiler_params=pltpu.CompilerParams(vmem_limit_bytes=2 << 20),
        cost_estimate=pl.CostEstimate(flops=10 * own.size, bytes_accessed=12 * own.size, transcendentals=128),
        name="norm",
    )(own, a, b, c, gain)


def attend_kernel(moves, keys, chunk, block, count_q, *refs):
    operands = 1 + max(move[0] for move in moves)
    queries, refs = refs[:count_q], refs[count_q:]
    pieces, refs = refs[:operands], refs[operands:]
    outs, (held, sems) = refs[:count_q], refs[count_q:]
    copies = []
    for index, (operand, source, count, row, col, width) in enumerate(moves):
        copy = pltpu.make_async_copy(
            pieces[operand].at[pl.ds(source, count), :],
            held.at[pl.ds(row, count), pl.ds(col, width)],
            sems.at[index],
        )
        copy.start()
        copies.append((row, copy))
    ones = jnp.ones((chunk, HD), jnp.bfloat16)
    rows = queries[0].shape[0]
    state = {}
    for base in range(0, keys, chunk):
        for begin, copy in copies:
            if base <= begin < base + chunk:
                copy.wait()
        for which, low in [(which, low) for which in range(count_q) for low in range(0, rows, block)]:
            q, out = queries[which], outs[which]
            here = slice(low, low + block)
            for head in range(HEADS_HERE):
                cols = slice(head * HD, (head + 1) * HD)
                vals = slice(WIDTH + head * HD, WIDTH + (head + 1) * HD)
                old = state.get((which, low, head))
                scores = lax.dot_general(
                    q[here, cols],
                    held[base : base + chunk, cols],
                    (((1,), (1,)), ((), ())),
                    preferred_element_type=jnp.float32,
                )
                raised = jnp.max(scores, axis=1, keepdims=True) * FACTOR
                if old is not None:
                    raised = jnp.maximum(raised, old[0])
                weights = jnp.exp2(scores * FACTOR - raised).astype(jnp.bfloat16)
                mixed = jnp.dot(
                    weights,
                    jnp.concatenate((held[base : base + chunk, vals], ones), axis=1),
                    preferred_element_type=jnp.float32,
                )
                acc, total = mixed[:, :HD], mixed[:, HD:]
                if old is not None:
                    rescale = jnp.exp2(old[0] - raised)
                    acc = old[2] * rescale + acc
                    total = old[1] * rescale + total
                state[which, low, head] = (raised, total, acc)
                if base + chunk >= keys:
                    if head == 0:
                        out[here, WIDTH:] = jnp.zeros((block, HD), jnp.float32)
                    out[here, cols] = acc
                    out[here, WIDTH + head : WIDTH + head + 1] = raised
                    out[here, WIDTH + HEADS_HERE + head : WIDTH + HEADS_HERE + head + 1] = total[:, :1]


def attend(queries, pieces, moves, chunk=1024, block=256):
    rows = queries[0].shape[0]
    keys = max(move[2] + move[3] for move in moves)
    chunk = min(chunk, keys)
    vmem, anywhere = pl.BlockSpec(memory_space=pltpu.VMEM), pl.BlockSpec(memory_space=pl.ANY)
    return pl.pallas_call(
        functools.partial(attend_kernel, moves, keys, chunk, block, len(queries)),
        out_shape=(jax.ShapeDtypeStruct((rows, WIDTH + HD), jnp.float32),) * len(queries),
        in_specs=[vmem] * len(queries) + [anywhere] * len(pieces),
        out_specs=(vmem,) * len(queries),
        scratch_shapes=[
            pltpu.VMEM((keys, 2 * WIDTH), jnp.bfloat16),
            pltpu.SemaphoreType.DMA((len(moves),)),
        ],
        compiler_params=pltpu.CompilerParams(vmem_limit_bytes=20 << 20),
        name="attend",
    )(*queries, *pieces)


def join_kernel(last, *refs):
    *parts, out = refs
    stats = [part[:, WIDTH:] for part in parts]
    top = functools.reduce(jnp.maximum, stats)
    scales = [jnp.exp2(stat - top) for stat in stats]
    total = sum(pltpu.roll(stat, HD - HEADS_HERE, axis=1) * scale for stat, scale in zip(stats, scales))
    if last:
        scales = [scale / total for scale in scales]
    else:
        out[:, WIDTH:] = jnp.zeros((top.shape[0], HD), jnp.float32)
        out[:, WIDTH : WIDTH + HEADS_HERE] = top[:, :HEADS_HERE]
        out[:, WIDTH + HEADS_HERE : WIDTH + 2 * HEADS_HERE] = total[:, :HEADS_HERE]
    for head in range(HEADS_HERE):
        cols = slice(head * HD, (head + 1) * HD)
        out[:, cols] = sum(
            part[:, cols] * scale[:, head : head + 1] for part, scale in zip(parts, scales)
        ).astype(out.dtype)


def join(parts, last):
    rows = parts[0].shape[0]
    size = parts[0].size
    return pl.pallas_call(
        functools.partial(join_kernel, last),
        out_shape=jax.ShapeDtypeStruct((rows, WIDTH), jnp.bfloat16)
        if last
        else jax.ShapeDtypeStruct(parts[0].shape, jnp.float32),
        compiler_params=pltpu.CompilerParams(vmem_limit_bytes=8 << 20),
        cost_estimate=pl.CostEstimate(
            flops=3 * len(parts) * size, bytes_accessed=4 * len(parts) * size, transcendentals=HD * rows
        ),
        name="join_last" if last else "join",
    )(*parts)


def hop(block, axis, shift):
    return lax.ppermute(block, axis, ring(2 if axis in ("w", "core") else 4, shift))


def per_device(q_tok, k_tok, v_tok, ref_hidden, ref_wk, ref_wv, key_gain):
    rows = q_tok.shape[0]
    barrier = lax.optimization_barrier
    inputs = [pltpu.with_memory_space_constraint(a, pltpu.HBM) for a in (ref_hidden, ref_wk, ref_wv, k_tok, v_tok)]
    own, *sent, beside = project(*inputs)
    arrived = [hop(block, "tensor", shift) for shift, block in zip((1, 2, 3), sent)]
    back, ahead = hop(beside, "y", 1), hop(beside, "y", 3)

    block = norm(own, *arrived, key_gain.reshape(1, HD))
    paired, q_peer = barrier((hop(block, "w", 1), hop(q_tok, "core", 1)))
    block = jnp.concatenate((block, paired), axis=0)
    pieces = [block] + [hop(block, SMALL, s) for s in (1, 3, 2)]
    pieces, back, ahead = barrier((pieces, back, ahead))
    block = jnp.concatenate(pieces, axis=0)
    late = [hop(block, BULK, s) for s in (1, 3, 2)]
    half = rows // 2
    opposite = [hop(back[:half], "y", 1), hop(ahead[half:], "y", 3)]

    moves = [(i, 0, rows, i * rows, 0, 2 * WIDTH) for i in range(2)]
    peer_a, own_a = attend((q_peer, q_tok), (beside, back), moves)
    opposite, peer_a, own_a = barrier((opposite, peer_a, own_a))
    moves = [(0, 0, rows, 0, 0, 2 * WIDTH)]
    moves += [(1 + i, 0, half, rows + i * half, 0, 2 * WIDTH) for i in range(2)]
    peer_b, own_b = attend((q_peer, q_tok), [ahead] + opposite, moves)
    late, peer_b, own_b = barrier((late, peer_b, own_b))
    size = block.shape[0]
    moves = [(i, 0, size, i * size, 0, 2 * WIDTH) for i in range(4)]
    (peer_c,) = attend((q_peer,), [block] + late, moves)
    from_peer = hop(join((peer_a, peer_b, peer_c), False), "core", 1)
    (own_c,) = attend((q_tok,), [block] + late, moves)
    return join((own_a, own_b, own_c, from_peer), True)


def solution(mesh):
    fine = Mesh(
        mesh.devices.reshape(4, 2, 4, 2, 4),
        ("x", "w", "y", "core", "tensor"),
    )
    placed = (
        P(SEQ, "tensor"),
        P(SEQ, "tensor"),
        P(SEQ, "tensor"),
        P(SEQ, "tensor"),
        P("tensor", None),
        P("tensor", None),
        P(),
    )
    return jax.shard_map(
        per_device, mesh=fine, in_specs=placed, out_specs=P(SEQ, "tensor"), check_vma=False
    )
```

time: 72.2 us -> 66.7 us (0.924)
  waiting for transfers between devices: 18 us -> 15.4 us
  starting transfers between devices: 29 us -> 28 us
  Pallas kernels: 23.9 us -> 23.1 us
  local copies, waits for them, and re-layouts: 0.85 us -> 0.09 us
    ppermute x18 -> x16, waiting for transfers between devices: 18 us -> 15.4 us  [hop(): lax.ppermute(block, axis, ring(2 if axis in ('w', 'core') else 4, shift))]
    pallas_call x4, Pallas kernels: 18.2 us -> 16.5 us  [attend(): pl.pallas_call(functools.partial(attend_kernel, moves, keys, chunk, block...]
    pallas_call x1 -> x2, Pallas kernels: 1.96 us -> 3.47 us  [join(): pl.pallas_call(functools.partial(join_kernel, last), out_shape=jax.ShapeD...]
    ppermute x18 -> x16, starting transfers between devices: 29 us -> 28 us  [hop(): lax.ppermute(block, axis, ring(2 if axis in ('w', 'core') else 4, shift))]
    unnamed x13 -> x7, local copies, waits for them, and re-layouts: 0.84 us -> 0.03 us
  transfers between devices with their start and end apart: 18 -> 16, of which waited for: 8 -> 7; matrix products, arithmetic and copies ran while one was open for 0% -> 0% of each run, Pallas kernels for 25% -> 20%
where the time goes in v3:
time: 66.7 us
  starting transfers between devices  28 us (42%)
  Pallas kernels  23.1 us (35%)
  waiting for transfers between devices  15.4 us (23%)
    ppermute x16, starting transfers between devices, hop(): lax.ppermute(block, axis, ring(2 if axis in ('w', 'core') else 4, shift))  28 us
    pallas_call x4, Pallas kernels, attend(): pl.pallas_call(functools.partial(attend_kernel, moves, keys, chunk, block...  16.5 us
    ppermute x16, waiting for transfers between devices, hop(): lax.ppermute(block, axis, ring(2 if axis in ('w', 'core') else 4, shift))  15.4 us
    pallas_call x2, Pallas kernels, join(): pl.pallas_call(functools.partial(join_kernel, last), out_shape=jax.ShapeD...  3.47 us
    pallas_call x1, Pallas kernels, project(): pl.pallas_call(project_kernel, out_shape=(jax.ShapeDtypeStruct((rows, 2 *...  3.03 us
  transfers between devices with their start and end apart: 16, of which 7 were waited for; matrix products, arithmetic and copies ran while one was open for 0% of the time, Pallas kernels for 20%

profile of v3, /device:TPU:1, one launch (start us, length us, event | category | flops | bytes accessed | tf_op | source)
XLA Modules:
  0.0 66.7 jit_solution(6650272040404306992)
XLA Ops:
  0.0 3.0 %project.1 = (f32[32,768]{1,0:T(8,128)S(1)}, bf16[32,768]{1,0:T(8,128)(2,1)S(1)}, bf16[32,768]{1,0:T(8,128)(2,1)S(1)}, bf16[32,768]{1,0:T(8,128)(2,1)S(1)}, bf16[512,768]{1,0:T(8,128)(2,1)S(1)}) custom-call(bf16[32,768]{1,0:T(8,128)(2,1)} %hidden.1, bf16[768,1536]{1,0:T(8,128)(2,1)} %wk.1, bf16[768,1536]{1,0:T(8,128)(2,1)} %wv.1, bf16[512,384]{1,0:T(8,128)(2,1)} %k_tok.1, ...), custom_call_target="tpu_custom_call" | custom-call | flops 150994944 | bytes 4718592 | tf_op jit(solution)/shard_map/project/pallas_call | solution.py:57
  3.0 3.6 %collective-permute-start.9 = (bf16[512,768]{1,0:T(8,128)(2,1)S(1)}, bf16[512,768]{1,0:T(8,128)(2,1)S(1)}, u32[]{:S(2)}, u32[]{:S(2)}) collective-permute-start(bf16[512,768]{1,0:T(8,128)(2,1)S(1)} %get-tuple-element.36.refs_2_), channel_id=1, source_target_pairs={{0,24},{8,0},{16,8},{24,16},{1,25},{9,1},{17,9},{25,17},{2,26},{10... | collective-permute-start | bytes 2359304 | tf_op jit(solution)/shard_map/ppermute | solution.py:219
  6.7 1.7 %collective-permute-start.4 = (bf16[512,384]{1,0:T(8,128)(2,1)S(1)}, bf16[512,384]{1,0:T(8,128)(2,1)S(1)}, u32[]{:S(2)}, u32[]{:S(2)}) collective-permute-start(bf16[512,384]{1,0:T(8,128)(2,1)S(1)} %copy-done), channel_id=1, source_target_pairs={{0,4},{4,0},{1,5},{5,1},{2,6},{6,2},{3,7},{7,3},{8,12},{12,8},{9,1... | collective-permute-start | bytes 1179656 | tf_op jit(solution)/shard_map/ppermute | solution.py:219
  8.4 2.3 %collective-permute-start = (bf16[32,768]{1,0:T(8,128)(2,1)S(1)}, bf16[32,768]{1,0:T(8,128)(2,1)S(1)}, u32[]{:S(2)}, u32[]{:S(2)}) collective-permute-start(bf16[32,768]{1,0:T(8,128)(2,1)S(1)} %get-tuple-element.32), channel_id=1, source_target_pairs={{0,1},{1,2},{2,3},{3,0},{4,5},{5,6},{6,7},{7,4},{8,9},{9,10},{10,1... | collective-permute-start | bytes 147464 | tf_op jit(solution)/shard_map/ppermute | solution.py:219
  10.6 5.1 %collective-permute-start.1 = (bf16[32,768]{1,0:T(8,128)(2,1)S(1)}, bf16[32,768]{1,0:T(8,128)(2,1)S(1)}, u32[]{:S(2)}, u32[]{:S(2)}) collective-permute-start(bf16[32,768]{1,0:T(8,128)(2,1)S(1)} %get-tuple-element.33), channel_id=1, source_target_pairs={{0,2},{1,3},{2,0},{3,1},{4,6},{5,7},{6,4},{7,5},{8,10},{9,11},{10,... | collective-permute-start | bytes 147464 | tf_op jit(solution)/shard_map/ppermute | solution.py:219
  15.8 2.4 %collective-permute-start.2 = (bf16[32,768]{1,0:T(8,128)(2,1)S(1)}, bf16[32,768]{1,0:T(8,128)(2,1)S(1)}, u32[]{:S(2)}, u32[]{:S(2)}) collective-permute-start(bf16[32,768]{1,0:T(8,128)(2,1)S(1)} %get-tuple-element.34), channel_id=1, source_target_pairs={{0,3},{1,0},{2,1},{3,2},{4,7},{5,4},{6,5},{7,6},{8,11},{9,8},{10,9... | collective-permute-start | bytes 147464 | tf_op jit(solution)/shard_map/ppermute | solution.py:219
  18.7 1.7 %collective-permute-done.2.c = bf16[32,768]{1,0:T(8,128)(2,1)S(1)} collective-permute-done((bf16[32,768]{1,0:T(8,128)(2,1)S(1)}, bf16[32,768]{1,0:T(8,128)(2,1)S(1)}, u32[]{:S(2)}, u32[]{:S(2)}) %collective-permute-start.2) | collective-permute-done | bytes 49184 | tf_op jit(solution)/shard_map/ppermute | solution.py:219
  20.5 1.8 %collective-permute-start.3 = (bf16[32,768]{1,0:T(8,128)(2,1)S(1)}, bf16[32,768]{1,0:T(8,128)(2,1)S(1)}, u32[]{:S(2)}, u32[]{:S(2)}) collective-permute-start(bf16[32,768]{1,0:T(8,128)(2,1)S(1)} %norm.1), channel_id=1, source_target_pairs={{0,32},{32,0},{1,33},{33,1},{2,34},{34,2},{3,35},{35,3},{4,36},{36... | collective-permute-start | bytes 147464 | tf_op jit(solution)/shard_map/ppermute | solution.py:219
  22.3 1.8 %collective-permute-done.3 = bf16[32,768]{1,0:T(8,128)(2,1)S(1)} collective-permute-done((bf16[32,768]{1,0:T(8,128)(2,1)S(1)}, bf16[32,768]{1,0:T(8,128)(2,1)S(1)}, u32[]{:S(2)}, u32[]{:S(2)}) %collective-permute-start.3) | collective-permute-done | bytes 49184 | tf_op jit(solution)/shard_map/ppermute | solution.py:219
  24.1 1.8 %collective-permute-start.7 = (bf16[64,768]{1,0:T(8,128)(2,1)S(1)}, bf16[64,768]{1,0:T(8,128)(2,1)S(1)}, u32[]{:S(2)}, u32[]{:S(2)}) collective-permute-start(bf16[64,768]{1,0:T(8,128)(2,1)S(1)} %pad_maximum_fusion), channel_id=1, source_target_pairs={{0,16},{8,24},{16,0},{24,8},{1,17},{9,25},{17,1},{25,9},{2,18},{10... | collective-permute-start | bytes 294920 | tf_op jit(solution)/shard_map/ppermute | solution.py:219
  26.0 1.3 %collective-permute-start.6 = (bf16[64,768]{1,0:T(8,128)(2,1)S(1)}, bf16[64,768]{1,0:T(8,128)(2,1)S(1)}, u32[]{:S(2)}, u32[]{:S(2)}) collective-permute-start(bf16[64,768]{1,0:T(8,128)(2,1)S(1)} %pad_maximum_fusion), channel_id=1, source_target_pairs={{0,24},{8,0},{16,8},{24,16},{1,25},{9,1},{17,9},{25,17},{2,26},{10... | collective-permute-start | bytes 294920 | tf_op jit(solution)/shard_map/ppermute | solution.py:219
  27.8 1.4 %collective-permute-done.7 = bf16[64,768]{1,0:T(8,128)(2,1)S(1)} collective-permute-done((bf16[64,768]{1,0:T(8,128)(2,1)S(1)}, bf16[64,768]{1,0:T(8,128)(2,1)S(1)}, u32[]{:S(2)}, u32[]{:S(2)}) %collective-permute-start.7) | collective-permute-done | bytes 98336 | tf_op jit(solution)/shard_map/ppermute | solution.py:219
  29.2 2.0 %collective-permute-done.6 = bf16[64,768]{1,0:T(8,128)(2,1)S(1)} collective-permute-done((bf16[64,768]{1,0:T(8,128)(2,1)S(1)}, bf16[64,768]{1,0:T(8,128)(2,1)S(1)}, u32[]{:S(2)}, u32[]{:S(2)}) %collective-permute-start.6) | collective-permute-done | bytes 98336 | tf_op jit(solution)/shard_map/ppermute | solution.py:219
  31.1 1.7 %collective-permute-done.5 = bf16[64,768]{1,0:T(8,128)(2,1)S(1)} collective-permute-done((bf16[64,768]{1,0:T(8,128)(2,1)S(1)}, bf16[64,768]{1,0:T(8,128)(2,1)S(1)}, u32[]{:S(2)}, u32[]{:S(2)}) %collective-permute-start.5) | collective-permute-done | bytes 98336 | tf_op jit(solution)/shard_map/ppermute | solution.py:219
  33.2 1.3 %collective-permute-start.10 = (bf16[256,768]{1,0:T(8,128)(2,1)S(1)}, bf16[256,768]{1,0:T(8,128)(2,1)S(1)}, u32[]{:S(2)}, u32[]{:S(2)}) collective-permute-start(bf16[256,768]{1,0:T(8,128)(2,1)S(1)} %slice.6), channel_id=1, source_target_pairs={{0,8},{8,16},{16,24},{24,0},{1,9},{9,17},{17,25},{25,1},{2,10},{10... | collective-permute-start | bytes 1179656 | tf_op jit(solution)/shard_map/ppermute | solution.py:219
  34.5 2.8 %collective-permute-start.14 = (bf16[256,768]{1,0:T(8,128)(2,1)S(1)}, bf16[256,768]{1,0:T(8,128)(2,1)S(1)}, u32[]{:S(2)}, u32[]{:S(2)}) collective-permute-start(bf16[256,768]{1,0:T(8,128)(2,1)S(1)} %constant_dynamic-update-slice_fusion.refs_1_), channel_id=1, source_target_pairs={{0,128},{64,192},{128,0},{192,64},{1,129},{65,193},{129,1},{193,65... | collective-permute-start | bytes 1179656 | tf_op jit(solution)/shard_map/ppermute | solution.py:219
  38.8 4.6 %attend.4 = (f32[512,512]{1,0:T(8,128)S(1)}, f32[512,512]{1,0:T(8,128)S(1)}) custom-call(bf16[512,384]{1,0:T(8,128)(2,1)S(1)} %collective-permute-done.4.refs_0_, bf16[512,384]{1,0:T(8,128)(2,1)S(1)} %copy-done, bf16[512,768]{1,0:T(8,128)(2,1)S(1)} %get-tuple-element.36.refs_2_, bf16[512,768]{1,0:T(8,128)(2,1)S(1)} %collective-permute-done.8.refs_3_), custom_call_target="tpu_custom_call" | custom-call | tf_op jit(solution)/shard_map/attend/pallas_call | solution.py:169
  43.5 5.0 %attend.5 = (f32[512,512]{1,0:T(8,128)S(1)}, f32[512,512]{1,0:T(8,128)S(1)}) custom-call(bf16[512,384]{1,0:T(8,128)(2,1)S(1)} %collective-permute-done.4.refs_0_, bf16[512,384]{1,0:T(8,128)(2,1)S(1)} %copy-done, bf16[512,768]{1,0:T(8,128)(2,1)S(1)} %collective-permute-done.9.refs_2_, bf16[256,768]{1,0:T(8,128)(2,1)S(1)} %collective-permute-done.10.refs_3_, ...), custom_call_target="tpu_custom_call" | custom-call | tf_op jit(solution)/shard_map/attend/pallas_call | solution.py:169
  48.5 6.2 %collective-permute-done.13.refs_3_ = bf16[256,768]{1,0:T(8,128)(2,1)S(1)} collective-permute-done((bf16[256,768]{1,0:T(8,128)(2,1)S(1)}, bf16[256,768]{1,0:T(8,128)(2,1)S(1)}, u32[]{:S(2)}, u32[]{:S(2)}) %collective-permute-start.13) | collective-permute-done | bytes 393248 | tf_op jit(solution)/shard_map/ppermute | solution.py:219
  54.7 3.5 %attend.7.refs_2_ = f32[512,512]{1,0:T(8,128)S(1)} custom-call(bf16[512,384]{1,0:T(8,128)(2,1)S(1)} %collective-permute-done.4.refs_0_, bf16[256,768]{1,0:T(8,128)(2,1)S(1)} %constant_dynamic-update-slice_fusion.refs_1_, bf16[256,768]{1,0:T(8,128)(2,1)S(1)} %collective-permute-done.12.refs_2_, bf16[256,768]{1,0:T(8,128)(2,1)S(1)} %collective-permute-done.13.refs_3_, ...), custom_call_target="tpu_custom_call" | custom-call | tf_op jit(solution)/shard_map/attend/pallas_call | solution.py:169
  58.2 1.2 %join.1 = f32[512,512]{1,0:T(8,128)S(1)} custom-call(f32[512,512]{1,0:T(8,128)S(1)} %get-tuple-element.55.refs_0_, f32[512,512]{1,0:T(8,128)S(1)} %get-tuple-element.56.refs_1_, f32[512,512]{1,0:T(8,128)S(1)} %attend.7.refs_2_), custom_call_target="tpu_custom_call" | custom-call | flops 2359296 | bytes 3145728 | tf_op jit(solution)/shard_map/join/pallas_call | solution.py:205
  59.4 1.6 %collective-permute-start.15 = (f32[512,512]{1,0:T(8,128)S(1)}, f32[512,512]{1,0:T(8,128)S(1)}, u32[]{:S(2)}, u32[]{:S(2)}) collective-permute-start(f32[512,512]{1,0:T(8,128)S(1)} %join.1), channel_id=1, source_target_pairs={{0,4},{4,0},{1,5},{5,1},{2,6},{6,2},{3,7},{7,3},{8,12},{12,8},{9,1... | collective-permute-start | bytes 3145736 | tf_op jit(solution)/shard_map/ppermute | solution.py:219
  61.0 3.3 %attend.6.refs_2_ = f32[512,512]{1,0:T(8,128)S(1)} custom-call(bf16[512,384]{1,0:T(8,128)(2,1)S(1)} %copy-done, bf16[256,768]{1,0:T(8,128)(2,1)S(1)} %constant_dynamic-update-slice_fusion.refs_1_, bf16[256,768]{1,0:T(8,128)(2,1)S(1)} %collective-permute-done.12.refs_2_, bf16[256,768]{1,0:T(8,128)(2,1)S(1)} %collective-permute-done.13.refs_3_, ...), custom_call_target="tpu_custom_call" | custom-call | tf_op jit(solution)/shard_map/attend/pallas_call | solution.py:169
  64.4 2.3 %join_last.1 = bf16[512,384]{1,0:T(8,128)(2,1)} custom-call(f32[512,512]{1,0:T(8,128)S(1)} %get-tuple-element.42.refs_0_, f32[512,512]{1,0:T(8,128)S(1)} %get-tuple-element.51.refs_1_, f32[512,512]{1,0:T(8,128)S(1)} %attend.6.refs_2_, f32[512,512]{1,0:T(8,128)S(1)} %collective-permute-done.15.refs_3_), custom_call_target="tpu_custom_call" | custom-call | flops 3145728 | bytes 4194304 | tf_op jit(solution)/shard_map/join_last/pallas_call | solution.py:205
  (27 shorter events, 3.0 us)
Async XLA Ops:
  0.0 6.7 %copy-start = (bf16[512,384]{1,0:T(8,128)(2,1)S(1)}, bf16[512,384]{1,0:T(8,128)(2,1)}, u32[]{:S(2)}) copy-start(bf16[512,384]{1,0:T(8,128)(2,1)} %refs_0_.1) | copy-start | bytes 1179652
  0.0 20.4 %copy-start.1 = (f32[128]{0:T(128)S(1)}, f32[128]{0:T(128)}, u32[]{:S(2)}) copy-start(f32[128]{0:T(128)} %param.13) | copy-start | bytes 1540
  3.0 29.8 %collective-permute-start.9 = (bf16[512,768]{1,0:T(8,128)(2,1)S(1)}, bf16[512,768]{1,0:T(8,128)(2,1)S(1)}, u32[]{:S(2)}, u32[]{:S(2)}) collective-permute-start(bf16[512,768]{1,0:T(8,128)(2,1)S(1)} %get-tuple-element.36.refs_2_), channel_id=1, source_target_pairs={{0,24},{8,0},{16,8},{24,16},{1,25},{9,1},{17,9},{25,17},{2,26},{10... | collective-permute-start | bytes 2359304 | tf_op jit(solution)/shard_map/ppermute | solution.py:219
  6.7 26.2 %collective-permute-start.8 = (bf16[512,768]{1,0:T(8,128)(2,1)S(1)}, bf16[512,768]{1,0:T(8,128)(2,1)S(1)}, u32[]{:S(2)}, u32[]{:S(2)}) collective-permute-start(bf16[512,768]{1,0:T(8,128)(2,1)S(1)} %get-tuple-element.36.refs_2_), channel_id=1, source_target_pairs={{0,8},{8,16},{16,24},{24,0},{1,9},{9,17},{17,25},{25,1},{2,10},{10... | collective-permute-start | bytes 2359304 | tf_op jit(solution)/shard_map/ppermute | solution.py:219
  6.7 17.4 %collective-permute-start.4 = (bf16[512,384]{1,0:T(8,128)(2,1)S(1)}, bf16[512,384]{1,0:T(8,128)(2,1)S(1)}, u32[]{:S(2)}, u32[]{:S(2)}) collective-permute-start(bf16[512,384]{1,0:T(8,128)(2,1)S(1)} %copy-done), channel_id=1, source_target_pairs={{0,4},{4,0},{1,5},{5,1},{2,6},{6,2},{3,7},{7,3},{8,12},{12,8},{9,1... | collective-permute-start | bytes 1179656 | tf_op jit(solution)/shard_map/ppermute | solution.py:219
  8.4 7.4 %collective-permute-start = (bf16[32,768]{1,0:T(8,128)(2,1)S(1)}, bf16[32,768]{1,0:T(8,128)(2,1)S(1)}, u32[]{:S(2)}, u32[]{:S(2)}) collective-permute-start(bf16[32,768]{1,0:T(8,128)(2,1)S(1)} %get-tuple-element.32), channel_id=1, source_target_pairs={{0,1},{1,2},{2,3},{3,0},{4,5},{5,6},{6,7},{7,4},{8,9},{9,10},{10,1... | collective-permute-start | bytes 147464 | tf_op jit(solution)/shard_map/ppermute | solution.py:219
  10.6 8.1 %collective-permute-start.1 = (bf16[32,768]{1,0:T(8,128)(2,1)S(1)}, bf16[32,768]{1,0:T(8,128)(2,1)S(1)}, u32[]{:S(2)}, u32[]{:S(2)}) collective-permute-start(bf16[32,768]{1,0:T(8,128)(2,1)S(1)} %get-tuple-element.33), channel_id=1, source_target_pairs={{0,2},{1,3},{2,0},{3,1},{4,6},{5,7},{6,4},{7,5},{8,10},{9,11},{10,... | collective-permute-start | bytes 147464 | tf_op jit(solution)/shard_map/ppermute | solution.py:219
  15.8 4.7 %collective-permute-start.2 = (bf16[32,768]{1,0:T(8,128)(2,1)S(1)}, bf16[32,768]{1,0:T(8,128)(2,1)S(1)}, u32[]{:S(2)}, u32[]{:S(2)}) collective-permute-start(bf16[32,768]{1,0:T(8,128)(2,1)S(1)} %get-tuple-element.34), channel_id=1, source_target_pairs={{0,3},{1,0},{2,1},{3,2},{4,7},{5,4},{6,5},{7,6},{8,11},{9,8},{10,9... | collective-permute-start | bytes 147464 | tf_op jit(solution)/shard_map/ppermute | solution.py:219
  20.5 3.6 %collective-permute-start.3 = (bf16[32,768]{1,0:T(8,128)(2,1)S(1)}, bf16[32,768]{1,0:T(8,128)(2,1)S(1)}, u32[]{:S(2)}, u32[]{:S(2)}) collective-permute-start(bf16[32,768]{1,0:T(8,128)(2,1)S(1)} %norm.1), channel_id=1, source_target_pairs={{0,32},{32,0},{1,33},{33,1},{2,34},{34,2},{3,35},{35,3},{4,36},{36... | collective-permute-start | bytes 147464 | tf_op jit(solution)/shard_map/ppermute | solution.py:219
  24.1 5.1 %collective-permute-start.7 = (bf16[64,768]{1,0:T(8,128)(2,1)S(1)}, bf16[64,768]{1,0:T(8,128)(2,1)S(1)}, u32[]{:S(2)}, u32[]{:S(2)}) collective-permute-start(bf16[64,768]{1,0:T(8,128)(2,1)S(1)} %pad_maximum_fusion), channel_id=1, source_target_pairs={{0,16},{8,24},{16,0},{24,8},{1,17},{9,25},{17,1},{25,9},{2,18},{10... | collective-permute-start | bytes 294920 | tf_op jit(solution)/shard_map/ppermute | solution.py:219
  26.0 5.2 %collective-permute-start.6 = (bf16[64,768]{1,0:T(8,128)(2,1)S(1)}, bf16[64,768]{1,0:T(8,128)(2,1)S(1)}, u32[]{:S(2)}, u32[]{:S(2)}) collective-permute-start(bf16[64,768]{1,0:T(8,128)(2,1)S(1)} %pad_maximum_fusion), channel_id=1, source_target_pairs={{0,24},{8,0},{16,8},{24,16},{1,25},{9,1},{17,9},{25,17},{2,26},{10... | collective-permute-start | bytes 294920 | tf_op jit(solution)/shard_map/ppermute | solution.py:219
  27.3 5.6 %collective-permute-start.5 = (bf16[64,768]{1,0:T(8,128)(2,1)S(1)}, bf16[64,768]{1,0:T(8,128)(2,1)S(1)}, u32[]{:S(2)}, u32[]{:S(2)}) collective-permute-start(bf16[64,768]{1,0:T(8,128)(2,1)S(1)} %pad_maximum_fusion), channel_id=1, source_target_pairs={{0,8},{8,16},{16,24},{24,0},{1,9},{9,17},{17,25},{25,1},{2,10},{10... | collective-permute-start | bytes 294920 | tf_op jit(solution)/shard_map/ppermute | solution.py:219
  33.0 10.5 %collective-permute-start.11 = (bf16[256,768]{1,0:T(8,128)(2,1)S(1)}, bf16[256,768]{1,0:T(8,128)(2,1)S(1)}, u32[]{:S(2)}, u32[]{:S(2)}) collective-permute-start(bf16[256,768]{1,0:T(8,128)(2,1)S(1)} %slice.7), channel_id=1, source_target_pairs={{0,24},{8,0},{16,8},{24,16},{1,25},{9,1},{17,9},{25,17},{2,26},{10... | collective-permute-start | bytes 1179656 | tf_op jit(solution)/shard_map/ppermute | solution.py:219
  33.2 10.3 %collective-permute-start.10 = (bf16[256,768]{1,0:T(8,128)(2,1)S(1)}, bf16[256,768]{1,0:T(8,128)(2,1)S(1)}, u32[]{:S(2)}, u32[]{:S(2)}) collective-permute-start(bf16[256,768]{1,0:T(8,128)(2,1)S(1)} %slice.6), channel_id=1, source_target_pairs={{0,8},{8,16},{16,24},{24,0},{1,9},{9,17},{17,25},{25,1},{2,10},{10... | collective-permute-start | bytes 1179656 | tf_op jit(solution)/shard_map/ppermute | solution.py:219
  34.5 13.9 %collective-permute-start.14 = (bf16[256,768]{1,0:T(8,128)(2,1)S(1)}, bf16[256,768]{1,0:T(8,128)(2,1)S(1)}, u32[]{:S(2)}, u32[]{:S(2)}) collective-permute-start(bf16[256,768]{1,0:T(8,128)(2,1)S(1)} %constant_dynamic-update-slice_fusion.refs_1_), channel_id=1, source_target_pairs={{0,128},{64,192},{128,0},{192,64},{1,129},{65,193},{129,1},{193,65... | collective-permute-start | bytes 1179656 | tf_op jit(solution)/shard_map/ppermute | solution.py:219
  37.4 17.3 %collective-permute-start.13 = (bf16[256,768]{1,0:T(8,128)(2,1)S(1)}, bf16[256,768]{1,0:T(8,128)(2,1)S(1)}, u32[]{:S(2)}, u32[]{:S(2)}) collective-permute-start(bf16[256,768]{1,0:T(8,128)(2,1)S(1)} %constant_dynamic-update-slice_fusion.refs_1_), channel_id=1, source_target_pairs={{0,192},{64,0},{128,64},{192,128},{1,193},{65,1},{129,65},{193,129... | collective-permute-start | bytes 1179656 | tf_op jit(solution)/shard_map/ppermute | solution.py:219
  38.2 16.4 %collective-permute-start.12 = (bf16[256,768]{1,0:T(8,128)(2,1)S(1)}, bf16[256,768]{1,0:T(8,128)(2,1)S(1)}, u32[]{:S(2)}, u32[]{:S(2)}) collective-permute-start(bf16[256,768]{1,0:T(8,128)(2,1)S(1)} %constant_dynamic-update-slice_fusion.refs_1_), channel_id=1, source_target_pairs={{0,64},{64,128},{128,192},{192,0},{1,65},{65,129},{129,193},{193,1... | collective-permute-start | bytes 1179656 | tf_op jit(solution)/shard_map/ppermute | solution.py:219
  59.4 5.0 %collective-permute-start.15 = (f32[512,512]{1,0:T(8,128)S(1)}, f32[512,512]{1,0:T(8,128)S(1)}, u32[]{:S(2)}, u32[]{:S(2)}) collective-permute-start(f32[512,512]{1,0:T(8,128)S(1)} %join.1), channel_id=1, source_target_pairs={{0,4},{4,0},{1,5},{5,1},{2,6},{6,2},{3,7},{7,3},{8,12},{12,8},{9,1... | collective-permute-start | bytes 3145736 | tf_op jit(solution)/shard_map/ppermute | solution.py:219

commit v4 on v3

--- a/solution.py
+++ b/solution.py
@@ -180,8 +180,14 @@
     )(*queries, *pieces)
 
 
-def join_kernel(last, *refs):
-    *parts, out = refs
+def join_kernel(count, last, *refs):
+    outs = refs[-count:]
+    each = (len(refs) - count) // count
+    for index, out in enumerate(outs):
+        join_one(last, refs[index * each : (index + 1) * each], out)
+
+
+def join_one(last, parts, out):
     stats = [part[:, WIDTH:] for part in parts]
     top = functools.reduce(jnp.maximum, stats)
     scales = [jnp.exp2(stat - top) for stat in stats]
@@ -199,20 +205,18 @@
         ).astype(out.dtype)
 
 
-def join(parts, last):
-    rows = parts[0].shape[0]
-    size = parts[0].size
-    return pl.pallas_call(
-        functools.partial(join_kernel, last),
-        out_shape=jax.ShapeDtypeStruct((rows, WIDTH), jnp.bfloat16)
-        if last
-        else jax.ShapeDtypeStruct(parts[0].shape, jnp.float32),
-        compiler_params=pltpu.CompilerParams(vmem_limit_bytes=8 << 20),
-        cost_estimate=pl.CostEstimate(
-            flops=3 * len(parts) * size, bytes_accessed=4 * len(parts) * size, transcendentals=HD * rows
-        ),
+def join(groups, last):
+    first = groups[0][0]
+    rows = first.shape[0]
+    size = sum(part.size for parts in groups for part in parts)
+    shape = jax.ShapeDtypeStruct((rows, WIDTH), jnp.bfloat16) if last else jax.ShapeDtypeStruct(first.shape, jnp.float32)
+    return pl.pallas_call(
+        functools.partial(join_kernel, len(groups), last),
+        out_shape=(shape,) * len(groups),
+        compiler_params=pltpu.CompilerParams(vmem_limit_bytes=12 << 20),
+        cost_estimate=pl.CostEstimate(flops=3 * size, bytes_accessed=4 * size, transcendentals=HD * rows),
         name="join_last" if last else "join",
-    )(*parts)
+    )(*[part for parts in groups for part in parts])
 
 
 def hop(block, axis, shift):
@@ -228,10 +232,11 @@
     back, ahead = hop(beside, "y", 1), hop(beside, "y", 3)
 
     block = norm(own, *arrived, key_gain.reshape(1, HD))
-    paired, q_peer = barrier((hop(block, "w", 1), hop(q_tok, "core", 1)))
+    block, q_late = barrier((block, q_tok))
+    paired, q_peer = barrier((hop(block, "w", 1), hop(q_late, "core", 1)))
     block = jnp.concatenate((block, paired), axis=0)
     pieces = [block] + [hop(block, SMALL, s) for s in (1, 3, 2)]
-    pieces, back, ahead = barrier((pieces, back, ahead))
+    pieces[1], back, ahead = barrier((pieces[1], back, ahead))
     block = jnp.concatenate(pieces, axis=0)
     late = [hop(block, BULK, s) for s in (1, 3, 2)]
     half = rows // 2
@@ -240,16 +245,17 @@
     moves = [(i, 0, rows, i * rows, 0, 2 * WIDTH) for i in range(2)]
     peer_a, own_a = attend((q_peer, q_tok), (beside, back), moves)
     opposite, peer_a, own_a = barrier((opposite, peer_a, own_a))
-    moves = [(0, 0, rows, 0, 0, 2 * WIDTH)]
-    moves += [(1 + i, 0, half, rows + i * half, 0, 2 * WIDTH) for i in range(2)]
-    peer_b, own_b = attend((q_peer, q_tok), [ahead] + opposite, moves)
-    late, peer_b, own_b = barrier((late, peer_b, own_b))
     size = block.shape[0]
-    moves = [(i, 0, size, i * size, 0, 2 * WIDTH) for i in range(4)]
-    (peer_c,) = attend((q_peer,), [block] + late, moves)
-    from_peer = hop(join((peer_a, peer_b, peer_c), False), "core", 1)
-    (own_c,) = attend((q_tok,), [block] + late, moves)
-    return join((own_a, own_b, own_c, from_peer), True)
+    moves = [(0, 0, rows, 0, 0, 2 * WIDTH), (1, 0, size, 2 * rows, 0, 2 * WIDTH)]
+    moves += [(2 + i, 0, half, rows + i * half, 0, 2 * WIDTH) for i in range(2)]
+    peer_b, own_b = attend((q_peer, q_tok), [ahead, block] + opposite, moves, chunk=2 * rows + size)
+    peer_ab, own_ab = join(((peer_a, peer_b), (own_a, own_b)), False)
+    late, peer_ab, own_ab = barrier((late, peer_ab, own_ab))
+    moves = [(i, 0, size, i * size, 0, 2 * WIDTH) for i in range(3)]
+    (peer_c,) = attend((q_peer,), late, moves)
+    from_peer = hop(*join(((peer_ab, peer_c),), False), "core", 1)
+    (own_c,) = attend((q_tok,), late, moves)
+    return join(((own_ab, own_c, from_peer),), True)[0]
 
 
 def solution(mesh):

time: 66.7 us -> 63 us (0.945)
  waiting for transfers between devices: 15.4 us -> 7.26 us
  starting transfers between devices: 28 us -> 32.1 us
    ppermute x16, waiting for transfers between devices: 15.4 us -> 7.26 us  [hop(): lax.ppermute(block, axis, ring(2 if axis in ('w', 'core') else 4, shift))]
    ppermute x16, starting transfers between devices: 28 us -> 32.1 us  [hop(): lax.ppermute(block, axis, ring(2 if axis in ('w', 'core') else 4, shift))]
    pallas_call x2 -> x3, Pallas kernels: 3.47 us -> 4.03 us  [join(): pl.pallas_call(functools.partial(join_kernel, len(groups), last), out_sha...]
  transfers between devices with their start and end apart: 16 -> 16, of which waited for: 7 -> 4; matrix products, arithmetic and copies ran while one was open for 0% -> 0% of each run, Pallas kernels for 20% -> 24%
where the time goes in v4:
time: 63 us; the launch traced here: 62.9 us
  starting transfers between devices  32.1 us (51%)
  Pallas kernels  23.3 us (37%)
  waiting for transfers between devices  7.26 us (12%)
    ppermute x16, starting transfers between devices, hop(): lax.ppermute(block, axis, ring(2 if axis in ('w', 'core') else 4, shift))  32.1 us
    pallas_call x4, Pallas kernels, attend(): pl.pallas_call(functools.partial(attend_kernel, moves, keys, chunk, block...  16.1 us
    ppermute x16, waiting for transfers between devices, hop(): lax.ppermute(block, axis, ring(2 if axis in ('w', 'core') else 4, shift))  7.26 us
    pallas_call x3, Pallas kernels, join(): pl.pallas_call(functools.partial(join_kernel, len(groups), last), out_sha...  4.03 us
    pallas_call x1, Pallas kernels, project(): pl.pallas_call(project_kernel, out_shape=(jax.ShapeDtypeStruct((rows, 2 *...  3.03 us
  transfers between devices with their start and end apart: 16, of which 4 were waited for; matrix products, arithmetic and copies ran while one was open for 0% of the time, Pallas kernels for 24%

profile of v4, /device:TPU:1, one launch (start us, length us, event | category | flops | bytes accessed | tf_op | source)
XLA Modules:
  0.0 62.9 jit_solution(15792627749665955960)
XLA Ops:
  0.0 3.0 %project.1 = (f32[32,768]{1,0:T(8,128)S(1)}, bf16[32,768]{1,0:T(8,128)(2,1)S(1)}, bf16[32,768]{1,0:T(8,128)(2,1)S(1)}, bf16[32,768]{1,0:T(8,128)(2,1)S(1)}, bf16[512,768]{1,0:T(8,128)(2,1)S(1)}) custom-call(bf16[32,768]{1,0:T(8,128)(2,1)} %hidden.1, bf16[768,1536]{1,0:T(8,128)(2,1)} %wk.1, bf16[768,1536]{1,0:T(8,128)(2,1)} %wv.1, bf16[512,384]{1,0:T(8,128)(2,1)} %k_tok.1, ...), custom_call_target="tpu_custom_call" | custom-call | flops 150994944 | bytes 4718592 | tf_op jit(solution)/shard_map/project/pallas_call | solution.py:57
  3.0 2.2 %collective-permute-start.6 = (bf16[512,768]{1,0:T(8,128)(2,1)S(1)}, bf16[512,768]{1,0:T(8,128)(2,1)S(1)}, u32[]{:S(2)}, u32[]{:S(2)}) collective-permute-start(bf16[512,768]{1,0:T(8,128)(2,1)S(1)} %get-tuple-element.39.refs_2_), channel_id=1, source_target_pairs={{0,8},{8,16},{16,24},{24,0},{1,9},{9,17},{17,25},{25,1},{2,10},{10... | collective-permute-start | bytes 2359304 | tf_op jit(solution)/shard_map/ppermute | solution.py:223
  5.2 1.5 %collective-permute-start.7 = (bf16[512,768]{1,0:T(8,128)(2,1)S(1)}, bf16[512,768]{1,0:T(8,128)(2,1)S(1)}, u32[]{:S(2)}, u32[]{:S(2)}) collective-permute-start(bf16[512,768]{1,0:T(8,128)(2,1)S(1)} %get-tuple-element.39.refs_2_), channel_id=1, source_target_pairs={{0,24},{8,0},{16,8},{24,16},{1,25},{9,1},{17,9},{25,17},{2,26},{10... | collective-permute-start | bytes 2359304 | tf_op jit(solution)/shard_map/ppermute | solution.py:223
  6.8 3.0 %collective-permute-start = (bf16[32,768]{1,0:T(8,128)(2,1)S(1)}, bf16[32,768]{1,0:T(8,128)(2,1)S(1)}, u32[]{:S(2)}, u32[]{:S(2)}) collective-permute-start(bf16[32,768]{1,0:T(8,128)(2,1)S(1)} %get-tuple-element.33), channel_id=1, source_target_pairs={{0,1},{1,2},{2,3},{3,0},{4,5},{5,6},{6,7},{7,4},{8,9},{9,10},{10,1... | collective-permute-start | bytes 147464 | tf_op jit(solution)/shard_map/ppermute | solution.py:223
  9.8 5.1 %collective-permute-start.1 = (bf16[32,768]{1,0:T(8,128)(2,1)S(1)}, bf16[32,768]{1,0:T(8,128)(2,1)S(1)}, u32[]{:S(2)}, u32[]{:S(2)}) collective-permute-start(bf16[32,768]{1,0:T(8,128)(2,1)S(1)} %get-tuple-element.34), channel_id=1, source_target_pairs={{0,2},{1,3},{2,0},{3,1},{4,6},{5,7},{6,4},{7,5},{8,10},{9,11},{10,... | collective-permute-start | bytes 147464 | tf_op jit(solution)/shard_map/ppermute | solution.py:223
  14.9 2.4 %collective-permute-start.2 = (bf16[32,768]{1,0:T(8,128)(2,1)S(1)}, bf16[32,768]{1,0:T(8,128)(2,1)S(1)}, u32[]{:S(2)}, u32[]{:S(2)}) collective-permute-start(bf16[32,768]{1,0:T(8,128)(2,1)S(1)} %get-tuple-element.35), channel_id=1, source_target_pairs={{0,3},{1,0},{2,1},{3,2},{4,7},{5,4},{6,5},{7,6},{8,11},{9,8},{10,9... | collective-permute-start | bytes 147464 | tf_op jit(solution)/shard_map/ppermute | solution.py:223
  17.3 3.0 %collective-permute-done.2.c = bf16[32,768]{1,0:T(8,128)(2,1)S(1)} collective-permute-done((bf16[32,768]{1,0:T(8,128)(2,1)S(1)}, bf16[32,768]{1,0:T(8,128)(2,1)S(1)}, u32[]{:S(2)}, u32[]{:S(2)}) %collective-permute-start.2) | collective-permute-done | bytes 49184 | tf_op jit(solution)/shard_map/ppermute | solution.py:223
  20.4 1.3 %collective-permute-start.4 = (bf16[512,384]{1,0:T(8,128)(2,1)S(1)}, bf16[512,384]{1,0:T(8,128)(2,1)S(1)}, u32[]{:S(2)}, u32[]{:S(2)}) collective-permute-start(bf16[512,384]{1,0:T(8,128)(2,1)S(1)} %copy-done), channel_id=1, source_target_pairs={{0,4},{4,0},{1,5},{5,1},{2,6},{6,2},{3,7},{7,3},{8,12},{12,8},{9,1... | collective-permute-start | bytes 1179656 | tf_op jit(solution)/shard_map/ppermute | solution.py:223
  21.7 0.8 %collective-permute-start.3 = (bf16[32,768]{1,0:T(8,128)(2,1)S(1)}, bf16[32,768]{1,0:T(8,128)(2,1)S(1)}, u32[]{:S(2)}, u32[]{:S(2)}) collective-permute-start(bf16[32,768]{1,0:T(8,128)(2,1)S(1)} %norm.1), channel_id=1, source_target_pairs={{0,32},{32,0},{1,33},{33,1},{2,34},{34,2},{3,35},{35,3},{4,36},{36... | collective-permute-start | bytes 147464 | tf_op jit(solution)/shard_map/ppermute | solution.py:223
  22.6 2.2 %collective-permute-done.3 = bf16[32,768]{1,0:T(8,128)(2,1)S(1)} collective-permute-done((bf16[32,768]{1,0:T(8,128)(2,1)S(1)}, bf16[32,768]{1,0:T(8,128)(2,1)S(1)}, u32[]{:S(2)}, u32[]{:S(2)}) %collective-permute-start.3) | collective-permute-done | bytes 49184 | tf_op jit(solution)/shard_map/ppermute | solution.py:223
  25.2 2.4 %collective-permute-start.8 = (bf16[64,768]{1,0:T(8,128)(2,1)S(1)}, bf16[64,768]{1,0:T(8,128)(2,1)S(1)}, u32[]{:S(2)}, u32[]{:S(2)}) collective-permute-start(bf16[64,768]{1,0:T(8,128)(2,1)S(1)} %get-tuple-element.59), channel_id=1, source_target_pairs={{0,24},{8,0},{16,8},{24,16},{1,25},{9,1},{17,9},{25,17},{2,26},{10... | collective-permute-start | bytes 294920 | tf_op jit(solution)/shard_map/ppermute | solution.py:223
  28.3 1.3 %collective-permute-done.5 = bf16[64,768]{1,0:T(8,128)(2,1)S(1)} collective-permute-done((bf16[64,768]{1,0:T(8,128)(2,1)S(1)}, bf16[64,768]{1,0:T(8,128)(2,1)S(1)}, u32[]{:S(2)}, u32[]{:S(2)}) %collective-permute-start.5) | collective-permute-done | bytes 98336 | tf_op jit(solution)/shard_map/ppermute | solution.py:223
  29.7 2.7 %collective-permute-start.14 = (bf16[256,768]{1,0:T(8,128)(2,1)S(1)}, bf16[256,768]{1,0:T(8,128)(2,1)S(1)}, u32[]{:S(2)}, u32[]{:S(2)}) collective-permute-start(bf16[256,768]{1,0:T(8,128)(2,1)S(1)} %slice.7), channel_id=1, source_target_pairs={{0,24},{8,0},{16,8},{24,16},{1,25},{9,1},{17,9},{25,17},{2,26},{10... | collective-permute-start | bytes 1179656 | tf_op jit(solution)/shard_map/ppermute | solution.py:223
  32.6 1.3 %collective-permute-start.10 = (bf16[256,768]{1,0:T(8,128)(2,1)S(1)}, bf16[256,768]{1,0:T(8,128)(2,1)S(1)}, u32[]{:S(2)}, u32[]{:S(2)}) collective-permute-start(bf16[256,768]{1,0:T(8,128)(2,1)S(1)} %constant_dynamic-update-slice_fusion.2.refs_3_), channel_id=1, source_target_pairs={{0,64},{64,128},{128,192},{192,0},{1,65},{65,129},{129,193},{193,1... | collective-permute-start | bytes 1179656 | tf_op jit(solution)/shard_map/ppermute | solution.py:223
  33.8 1.5 %collective-permute-start.11 = (bf16[256,768]{1,0:T(8,128)(2,1)S(1)}, bf16[256,768]{1,0:T(8,128)(2,1)S(1)}, u32[]{:S(2)}, u32[]{:S(2)}) collective-permute-start(bf16[256,768]{1,0:T(8,128)(2,1)S(1)} %constant_dynamic-update-slice_fusion.2.refs_3_), channel_id=1, source_target_pairs={{0,192},{64,0},{128,64},{192,128},{1,193},{65,1},{129,65},{193,129... | collective-permute-start | bytes 1179656 | tf_op jit(solution)/shard_map/ppermute | solution.py:223
  35.3 1.5 %collective-permute-start.12 = (bf16[256,768]{1,0:T(8,128)(2,1)S(1)}, bf16[256,768]{1,0:T(8,128)(2,1)S(1)}, u32[]{:S(2)}, u32[]{:S(2)}) collective-permute-start(bf16[256,768]{1,0:T(8,128)(2,1)S(1)} %constant_dynamic-update-slice_fusion.2.refs_3_), channel_id=1, source_target_pairs={{0,128},{64,192},{128,0},{192,64},{1,129},{65,193},{129,1},{193,65... | collective-permute-start | bytes 1179656 | tf_op jit(solution)/shard_map/ppermute | solution.py:223
  36.8 4.6 %attend.4 = (f32[512,512]{1,0:T(8,128)S(1)}, f32[512,512]{1,0:T(8,128)S(1)}) custom-call(bf16[512,384]{1,0:T(8,128)(2,1)S(1)} %collective-permute-done.4.refs_0_, bf16[512,384]{1,0:T(8,128)(2,1)S(1)} %copy-done, bf16[512,768]{1,0:T(8,128)(2,1)S(1)} %get-tuple-element.39.refs_2_, bf16[512,768]{1,0:T(8,128)(2,1)S(1)} %collective-permute-done.6.refs_3_), custom_call_target="tpu_custom_call" | custom-call | tf_op jit(solution)/shard_map/attend/pallas_call | solution.py:169
  41.5 6.1 %attend.5 = (f32[512,512]{1,0:T(8,128)S(1)}, f32[512,512]{1,0:T(8,128)S(1)}) custom-call(bf16[512,384]{1,0:T(8,128)(2,1)S(1)} %collective-permute-done.4.refs_0_, bf16[512,384]{1,0:T(8,128)(2,1)S(1)} %copy-done, bf16[512,768]{1,0:T(8,128)(2,1)S(1)} %collective-permute-done.7.refs_2_, bf16[256,768]{1,0:T(8,128)(2,1)S(1)} %constant_dynamic-update-slice_fusion.2.refs_3_, ...), custom_call_target="tpu_custom_call" | custom-call | tf_op jit(solution)/shard_map/attend/pallas_call | solution.py:169
  47.6 1.4 %join.2 = (f32[512,512]{1,0:T(8,128)S(1)}, f32[512,512]{1,0:T(8,128)S(1)}) custom-call(f32[512,512]{1,0:T(8,128)S(1)} %get-tuple-element.46.refs_0_, f32[512,512]{1,0:T(8,128)S(1)} %get-tuple-element.49.refs_1_, f32[512,512]{1,0:T(8,128)S(1)} %get-tuple-element.50.refs_2_, f32[512,512]{1,0:T(8,128)S(1)} %get-tuple-element.51.refs_3_), custom_call_target="tpu_custom_call" | custom-call | flops 3145728 | bytes 4194304 | tf_op jit(solution)/shard_map/join/pallas_call | solution.py:213
  49.6 2.8 %attend.7.refs_1_ = f32[512,512]{1,0:T(8,128)S(1)} custom-call(bf16[512,384]{1,0:T(8,128)(2,1)S(1)} %collective-permute-done.4.refs_0_, bf16[256,768]{1,0:T(8,128)(2,1)S(1)} %collective-permute-done.10.refs_1_, bf16[256,768]{1,0:T(8,128)(2,1)S(1)} %collective-permute-done.11.refs_2_, bf16[256,768]{1,0:T(8,128)(2,1)S(1)} %collective-permute-done.12.refs_3_), custom_call_target="tpu_custom_call" | custom-call | tf_op jit(solution)/shard_map/attend/pallas_call | solution.py:169
  52.4 0.8 %join.3 = f32[512,512]{1,0:T(8,128)S(1)} custom-call(f32[512,512]{1,0:T(8,128)S(1)} %get-tuple-element.58.refs_0_, f32[512,512]{1,0:T(8,128)S(1)} %attend.7.refs_1_), custom_call_target="tpu_custom_call" | custom-call | flops 1572864 | bytes 2097152 | tf_op jit(solution)/shard_map/join/pallas_call | solution.py:213
  53.2 5.2 %collective-permute-start.15 = (f32[512,512]{1,0:T(8,128)S(1)}, f32[512,512]{1,0:T(8,128)S(1)}, u32[]{:S(2)}, u32[]{:S(2)}) collective-permute-start(f32[512,512]{1,0:T(8,128)S(1)} %join.3), channel_id=1, source_target_pairs={{0,4},{4,0},{1,5},{5,1},{2,6},{6,2},{3,7},{7,3},{8,12},{12,8},{9,1... | collective-permute-start | bytes 3145736 | tf_op jit(solution)/shard_map/ppermute | solution.py:223
  58.5 2.6 %attend.6.refs_1_ = f32[512,512]{1,0:T(8,128)S(1)} custom-call(bf16[512,384]{1,0:T(8,128)(2,1)S(1)} %copy-done, bf16[256,768]{1,0:T(8,128)(2,1)S(1)} %collective-permute-done.10.refs_1_, bf16[256,768]{1,0:T(8,128)(2,1)S(1)} %collective-permute-done.11.refs_2_, bf16[256,768]{1,0:T(8,128)(2,1)S(1)} %collective-permute-done.12.refs_3_), custom_call_target="tpu_custom_call" | custom-call | tf_op jit(solution)/shard_map/attend/pallas_call | solution.py:169
  61.1 1.8 %join_last.1 = bf16[512,384]{1,0:T(8,128)(2,1)} custom-call(f32[512,512]{1,0:T(8,128)S(1)} %get-tuple-element.54.refs_0_, f32[512,512]{1,0:T(8,128)S(1)} %attend.6.refs_1_, f32[512,512]{1,0:T(8,128)S(1)} %collective-permute-done.15.refs_2_), custom_call_target="tpu_custom_call" | custom-call | flops 2359296 | bytes 3145728 | tf_op jit(solution)/shard_map/join_last/pallas_call | solution.py:213
  (28 shorter events, 2.0 us)
Async XLA Ops:
  0.0 20.3 %copy-start.1 = (f32[128]{0:T(128)S(1)}, f32[128]{0:T(128)}, u32[]{:S(2)}) copy-start(f32[128]{0:T(128)} %param.13) | copy-start | bytes 1540
  0.0 20.4 %copy-start = (bf16[512,384]{1,0:T(8,128)(2,1)S(1)}, bf16[512,384]{1,0:T(8,128)(2,1)}, u32[]{:S(2)}) copy-start(bf16[512,384]{1,0:T(8,128)(2,1)} %refs_0_.1) | copy-start | bytes 1179652
  3.0 26.5 %collective-permute-start.6 = (bf16[512,768]{1,0:T(8,128)(2,1)S(1)}, bf16[512,768]{1,0:T(8,128)(2,1)S(1)}, u32[]{:S(2)}, u32[]{:S(2)}) collective-permute-start(bf16[512,768]{1,0:T(8,128)(2,1)S(1)} %get-tuple-element.39.refs_2_), channel_id=1, source_target_pairs={{0,8},{8,16},{16,24},{24,0},{1,9},{9,17},{17,25},{25,1},{2,10},{10... | collective-permute-start | bytes 2359304 | tf_op jit(solution)/shard_map/ppermute | solution.py:223
  5.2 24.3 %collective-permute-start.7 = (bf16[512,768]{1,0:T(8,128)(2,1)S(1)}, bf16[512,768]{1,0:T(8,128)(2,1)S(1)}, u32[]{:S(2)}, u32[]{:S(2)}) collective-permute-start(bf16[512,768]{1,0:T(8,128)(2,1)S(1)} %get-tuple-element.39.refs_2_), channel_id=1, source_target_pairs={{0,24},{8,0},{16,8},{24,16},{1,25},{9,1},{17,9},{25,17},{2,26},{10... | collective-permute-start | bytes 2359304 | tf_op jit(solution)/shard_map/ppermute | solution.py:223
  6.8 10.5 %collective-permute-start = (bf16[32,768]{1,0:T(8,128)(2,1)S(1)}, bf16[32,768]{1,0:T(8,128)(2,1)S(1)}, u32[]{:S(2)}, u32[]{:S(2)}) collective-permute-start(bf16[32,768]{1,0:T(8,128)(2,1)S(1)} %get-tuple-element.33), channel_id=1, source_target_pairs={{0,1},{1,2},{2,3},{3,0},{4,5},{5,6},{6,7},{7,4},{8,9},{9,10},{10,1... | collective-permute-start | bytes 147464 | tf_op jit(solution)/shard_map/ppermute | solution.py:223
  9.8 7.5 %collective-permute-start.1 = (bf16[32,768]{1,0:T(8,128)(2,1)S(1)}, bf16[32,768]{1,0:T(8,128)(2,1)S(1)}, u32[]{:S(2)}, u32[]{:S(2)}) collective-permute-start(bf16[32,768]{1,0:T(8,128)(2,1)S(1)} %get-tuple-element.34), channel_id=1, source_target_pairs={{0,2},{1,3},{2,0},{3,1},{4,6},{5,7},{6,4},{7,5},{8,10},{9,11},{10,... | collective-permute-start | bytes 147464 | tf_op jit(solution)/shard_map/ppermute | solution.py:223
  14.9 5.4 %collective-permute-start.2 = (bf16[32,768]{1,0:T(8,128)(2,1)S(1)}, bf16[32,768]{1,0:T(8,128)(2,1)S(1)}, u32[]{:S(2)}, u32[]{:S(2)}) collective-permute-start(bf16[32,768]{1,0:T(8,128)(2,1)S(1)} %get-tuple-element.35), channel_id=1, source_target_pairs={{0,3},{1,0},{2,1},{3,2},{4,7},{5,4},{6,5},{7,6},{8,11},{9,8},{10,9... | collective-permute-start | bytes 147464 | tf_op jit(solution)/shard_map/ppermute | solution.py:223
  20.4 4.4 %collective-permute-start.4 = (bf16[512,384]{1,0:T(8,128)(2,1)S(1)}, bf16[512,384]{1,0:T(8,128)(2,1)S(1)}, u32[]{:S(2)}, u32[]{:S(2)}) collective-permute-start(bf16[512,384]{1,0:T(8,128)(2,1)S(1)} %copy-done), channel_id=1, source_target_pairs={{0,4},{4,0},{1,5},{5,1},{2,6},{6,2},{3,7},{7,3},{8,12},{12,8},{9,1... | collective-permute-start | bytes 1179656 | tf_op jit(solution)/shard_map/ppermute | solution.py:223
  21.7 3.1 %collective-permute-start.3 = (bf16[32,768]{1,0:T(8,128)(2,1)S(1)}, bf16[32,768]{1,0:T(8,128)(2,1)S(1)}, u32[]{:S(2)}, u32[]{:S(2)}) collective-permute-start(bf16[32,768]{1,0:T(8,128)(2,1)S(1)} %norm.1), channel_id=1, source_target_pairs={{0,32},{32,0},{1,33},{33,1},{2,34},{34,2},{3,35},{35,3},{4,36},{36... | collective-permute-start | bytes 147464 | tf_op jit(solution)/shard_map/ppermute | solution.py:223
  24.8 4.8 %collective-permute-start.5 = (bf16[64,768]{1,0:T(8,128)(2,1)S(1)}, bf16[64,768]{1,0:T(8,128)(2,1)S(1)}, u32[]{:S(2)}, u32[]{:S(2)}) collective-permute-start(bf16[64,768]{1,0:T(8,128)(2,1)S(1)} %get-tuple-element.59), channel_id=1, source_target_pairs={{0,8},{8,16},{16,24},{24,0},{1,9},{9,17},{17,25},{25,1},{2,10},{10... | collective-permute-start | bytes 294920 | tf_op jit(solution)/shard_map/ppermute | solution.py:223
  25.2 7.3 %collective-permute-start.8 = (bf16[64,768]{1,0:T(8,128)(2,1)S(1)}, bf16[64,768]{1,0:T(8,128)(2,1)S(1)}, u32[]{:S(2)}, u32[]{:S(2)}) collective-permute-start(bf16[64,768]{1,0:T(8,128)(2,1)S(1)} %get-tuple-element.59), channel_id=1, source_target_pairs={{0,24},{8,0},{16,8},{24,16},{1,25},{9,1},{17,9},{25,17},{2,26},{10... | collective-permute-start | bytes 294920 | tf_op jit(solution)/shard_map/ppermute | solution.py:223
  27.6 5.0 %collective-permute-start.9 = (bf16[64,768]{1,0:T(8,128)(2,1)S(1)}, bf16[64,768]{1,0:T(8,128)(2,1)S(1)}, u32[]{:S(2)}, u32[]{:S(2)}) collective-permute-start(bf16[64,768]{1,0:T(8,128)(2,1)S(1)} %get-tuple-element.59), channel_id=1, source_target_pairs={{0,16},{8,24},{16,0},{24,8},{1,17},{9,25},{17,1},{25,9},{2,18},{10... | collective-permute-start | bytes 294920 | tf_op jit(solution)/shard_map/ppermute | solution.py:223
  29.6 11.9 %collective-permute-start.13 = (bf16[256,768]{1,0:T(8,128)(2,1)S(1)}, bf16[256,768]{1,0:T(8,128)(2,1)S(1)}, u32[]{:S(2)}, u32[]{:S(2)}) collective-permute-start(bf16[256,768]{1,0:T(8,128)(2,1)S(1)} %slice.6), channel_id=1, source_target_pairs={{0,8},{8,16},{16,24},{24,0},{1,9},{9,17},{17,25},{25,1},{2,10},{10... | collective-permute-start | bytes 1179656 | tf_op jit(solution)/shard_map/ppermute | solution.py:223
  29.7 11.8 %collective-permute-start.14 = (bf16[256,768]{1,0:T(8,128)(2,1)S(1)}, bf16[256,768]{1,0:T(8,128)(2,1)S(1)}, u32[]{:S(2)}, u32[]{:S(2)}) collective-permute-start(bf16[256,768]{1,0:T(8,128)(2,1)S(1)} %slice.7), channel_id=1, source_target_pairs={{0,24},{8,0},{16,8},{24,16},{1,25},{9,1},{17,9},{25,17},{2,26},{10... | collective-permute-start | bytes 1179656 | tf_op jit(solution)/shard_map/ppermute | solution.py:223
  32.6 16.5 %collective-permute-start.10 = (bf16[256,768]{1,0:T(8,128)(2,1)S(1)}, bf16[256,768]{1,0:T(8,128)(2,1)S(1)}, u32[]{:S(2)}, u32[]{:S(2)}) collective-permute-start(bf16[256,768]{1,0:T(8,128)(2,1)S(1)} %constant_dynamic-update-slice_fusion.2.refs_3_), channel_id=1, source_target_pairs={{0,64},{64,128},{128,192},{192,0},{1,65},{65,129},{129,193},{193,1... | collective-permute-start | bytes 1179656 | tf_op jit(solution)/shard_map/ppermute | solution.py:223
  33.8 15.2 %collective-permute-start.11 = (bf16[256,768]{1,0:T(8,128)(2,1)S(1)}, bf16[256,768]{1,0:T(8,128)(2,1)S(1)}, u32[]{:S(2)}, u32[]{:S(2)}) collective-permute-start(bf16[256,768]{1,0:T(8,128)(2,1)S(1)} %constant_dynamic-update-slice_fusion.2.refs_3_), channel_id=1, source_target_pairs={{0,192},{64,0},{128,64},{192,128},{1,193},{65,1},{129,65},{193,129... | collective-permute-start | bytes 1179656 | tf_op jit(solution)/shard_map/ppermute | solution.py:223
  35.3 14.3 %collective-permute-start.12 = (bf16[256,768]{1,0:T(8,128)(2,1)S(1)}, bf16[256,768]{1,0:T(8,128)(2,1)S(1)}, u32[]{:S(2)}, u32[]{:S(2)}) collective-permute-start(bf16[256,768]{1,0:T(8,128)(2,1)S(1)} %constant_dynamic-update-slice_fusion.2.refs_3_), channel_id=1, source_target_pairs={{0,128},{64,192},{128,0},{192,64},{1,129},{65,193},{129,1},{193,65... | collective-permute-start | bytes 1179656 | tf_op jit(solution)/shard_map/ppermute | solution.py:223
  53.2 7.8 %collective-permute-start.15 = (f32[512,512]{1,0:T(8,128)S(1)}, f32[512,512]{1,0:T(8,128)S(1)}, u32[]{:S(2)}, u32[]{:S(2)}) collective-permute-start(f32[512,512]{1,0:T(8,128)S(1)} %join.3), channel_id=1, source_target_pairs={{0,4},{4,0},{1,5},{5,1},{2,6},{6,2},{3,7},{7,3},{8,12},{12,8},{9,1... | collective-permute-start | bytes 3145736 | tf_op jit(solution)/shard_map/ppermute | solution.py:223

commit v5 on v4

--- a/solution.py
+++ b/solution.py
@@ -180,11 +180,52 @@
     )(*queries, *pieces)
 
 
-def join_kernel(count, last, *refs):
+def attend_whole_kernel(block, q, *refs):
+    *pieces, out = refs
+    keys = sum(piece.shape[0] for piece in pieces)
+    ones = jnp.ones((keys, HD), jnp.bfloat16)
+    for low in range(0, q.shape[0], block):
+        here = slice(low, low + block)
+        out[here, WIDTH:] = jnp.zeros((block, HD), jnp.float32)
+        for head in range(HEADS_HERE):
+            cols = slice(head * HD, (head + 1) * HD)
+            vals = slice(WIDTH + head * HD, WIDTH + (head + 1) * HD)
+            scores = lax.dot_general(
+                q[here, cols],
+                jnp.concatenate([piece[:, cols] for piece in pieces], axis=0),
+                (((1,), (1,)), ((), ())),
+                preferred_element_type=jnp.float32,
+            )
+            raised = jnp.max(scores, axis=1, keepdims=True) * FACTOR
+            weights = jnp.exp2(scores * FACTOR - raised).astype(jnp.bfloat16)
+            values = jnp.concatenate([piece[:, vals] for piece in pieces], axis=0)
+            mixed = jnp.dot(
+                weights, jnp.concatenate((values, ones), axis=1), preferred_element_type=jnp.float32
+            )
+            out[here, cols] = mixed[:, :HD]
+            out[here, WIDTH + head : WIDTH + head + 1] = raised
+            out[here, WIDTH + HEADS_HERE + head : WIDTH + HEADS_HERE + head + 1] = mixed[:, HD : HD + 1]
+
+
+def attend_whole(q, pieces, block=256):
+    return pl.pallas_call(
+        functools.partial(attend_whole_kernel, block),
+        out_shape=jax.ShapeDtypeStruct((q.shape[0], WIDTH + HD), jnp.float32),
+        compiler_params=pltpu.CompilerParams(vmem_limit_bytes=20 << 20),
+        name="attend_whole",
+    )(q, *pieces)
+
+
+def join_kernel(count, *refs):
     outs = refs[-count:]
     each = (len(refs) - count) // count
     for index, out in enumerate(outs):
-        join_one(last, refs[index * each : (index + 1) * each], out)
+        join_one(False, refs[index * each : (index + 1) * each], out)
+
+
+def join_last_kernel(*refs):
+    *parts, out = refs
+    join_one(True, parts, out)
 
 
 def join_one(last, parts, out):
@@ -193,7 +234,8 @@
     scales = [jnp.exp2(stat - top) for stat in stats]
     total = sum(pltpu.roll(stat, HD - HEADS_HERE, axis=1) * scale for stat, scale in zip(stats, scales))
     if last:
-        scales = [scale / total for scale in scales]
+        inverse = 1.0 / total
+        scales = [scale * inverse for scale in scales]
     else:
         out[:, WIDTH:] = jnp.zeros((top.shape[0], HD), jnp.float32)
         out[:, WIDTH : WIDTH + HEADS_HERE] = top[:, :HEADS_HERE]
@@ -205,18 +247,27 @@
         ).astype(out.dtype)
 
 
-def join(groups, last):
+def join(*groups):
     first = groups[0][0]
-    rows = first.shape[0]
     size = sum(part.size for parts in groups for part in parts)
-    shape = jax.ShapeDtypeStruct((rows, WIDTH), jnp.bfloat16) if last else jax.ShapeDtypeStruct(first.shape, jnp.float32)
-    return pl.pallas_call(
-        functools.partial(join_kernel, len(groups), last),
-        out_shape=(shape,) * len(groups),
+    return pl.pallas_call(
+        functools.partial(join_kernel, len(groups)),
+        out_shape=(jax.ShapeDtypeStruct(first.shape, jnp.float32),) * len(groups),
         compiler_params=pltpu.CompilerParams(vmem_limit_bytes=12 << 20),
-        cost_estimate=pl.CostEstimate(flops=3 * size, bytes_accessed=4 * size, transcendentals=HD * rows),
-        name="join_last" if last else "join",
+        cost_estimate=pl.CostEstimate(
+            flops=3 * size, bytes_accessed=4 * size, transcendentals=HD * first.shape[0]
+        ),
+        name="join",
     )(*[part for parts in groups for part in parts])
+
+
+def join_last(parts):
+    return pl.pallas_call(
+        join_last_kernel,
+        out_shape=jax.ShapeDtypeStruct((parts[0].shape[0], WIDTH), jnp.bfloat16),
+        compiler_params=pltpu.CompilerParams(vmem_limit_bytes=12 << 20),
+        name="join_last",
+    )(*parts)
 
 
 def hop(block, axis, shift):
@@ -249,13 +300,11 @@
     moves = [(0, 0, rows, 0, 0, 2 * WIDTH), (1, 0, size, 2 * rows, 0, 2 * WIDTH)]
     moves += [(2 + i, 0, half, rows + i * half, 0, 2 * WIDTH) for i in range(2)]
     peer_b, own_b = attend((q_peer, q_tok), [ahead, block] + opposite, moves, chunk=2 * rows + size)
-    peer_ab, own_ab = join(((peer_a, peer_b), (own_a, own_b)), False)
+    peer_ab, own_ab = join((peer_a, peer_b), (own_a, own_b))
     late, peer_ab, own_ab = barrier((late, peer_ab, own_ab))
-    moves = [(i, 0, size, i * size, 0, 2 * WIDTH) for i in range(3)]
-    (peer_c,) = attend((q_peer,), late, moves)
-    from_peer = hop(*join(((peer_ab, peer_c),), False), "core", 1)
-    (own_c,) = attend((q_tok,), late, moves)
-    return join(((own_ab, own_c, from_peer),), True)[0]
+    peer_c = attend_whole(q_peer, late)
+    from_peer = hop(*join((peer_ab, peer_c)), "core", 1)
+    return join_last((own_ab, attend_whole(q_tok, late), from_peer))
 
 
 def solution(mesh):

time: 63 us -> 62.1 us (0.986)
  Pallas kernels: 23.3 us -> 21.9 us
    pallas_call x4 -> x2, Pallas kernels: 16.1 us -> 10.7 us  [attend(): pl.pallas_call(functools.partial(attend_kernel, moves, keys, chunk, block...]
    pallas_call x3 -> x5, Pallas kernels: 4.03 us -> 8.05 us  [the longest x2 4.02 us: attend_whole(): pl.pallas_call(functools.partial(attend_whole_kernel, block), out_shape=j...]
  transfers between devices with their start and end apart: 16 -> 16, of which waited for: 4 -> 5; matrix products, arithmetic and copies ran while one was open for 0% -> 0% of each run, Pallas kernels for 24% -> 23%
where the time goes in v5:
time: 62.1 us; the launch traced here: 62 us
  starting transfers between devices  32.3 us (52%)
  Pallas kernels  21.9 us (35%)
  waiting for transfers between devices  7.53 us (12%)
    ppermute x16, starting transfers between devices, hop(): lax.ppermute(block, axis, ring(2 if axis in ('w', 'core') else 4, shift))  32.3 us
    pallas_call x2, Pallas kernels, attend(): pl.pallas_call(functools.partial(attend_kernel, moves, keys, chunk, block...  10.7 us
    ppermute x16, waiting for transfers between devices, hop(): lax.ppermute(block, axis, ring(2 if axis in ('w', 'core') else 4, shift))  7.53 us
    pallas_call x2, Pallas kernels, attend_whole(): pl.pallas_call(functools.partial(attend_whole_kernel, block), out_shape=j...  4.02 us
    pallas_call x1, Pallas kernels, project(): pl.pallas_call(project_kernel, out_shape=(jax.ShapeDtypeStruct((rows, 2 *...  3.03 us
    pallas_call x2, Pallas kernels, join(): pl.pallas_call(functools.partial(join_kernel, len(groups)), out_shape=(ja...  2.21 us
    pallas_call x1, Pallas kernels, join_last(): pl.pallas_call(join_last_kernel, out_shape=jax.ShapeDtypeStruct((parts[0]...  1.82 us
  transfers between devices with their start and end apart: 16, of which 5 were waited for; matrix products, arithmetic and copies ran while one was open for 0% of the time, Pallas kernels for 23%

profile of v5, /device:TPU:1, one launch (start us, length us, event | category | flops | bytes accessed | tf_op | source)
XLA Modules:
  0.0 62.0 jit_solution(9025729162903067914)
XLA Ops:
  0.0 3.0 %project.1 = (f32[32,768]{1,0:T(8,128)S(1)}, bf16[32,768]{1,0:T(8,128)(2,1)S(1)}, bf16[32,768]{1,0:T(8,128)(2,1)S(1)}, bf16[32,768]{1,0:T(8,128)(2,1)S(1)}, bf16[512,768]{1,0:T(8,128)(2,1)S(1)}) custom-call(bf16[32,768]{1,0:T(8,128)(2,1)} %hidden.1, bf16[768,1536]{1,0:T(8,128)(2,1)} %wk.1, bf16[768,1536]{1,0:T(8,128)(2,1)} %wv.1, bf16[512,384]{1,0:T(8,128)(2,1)} %k_tok.1, ...), custom_call_target="tpu_custom_call" | custom-call | flops 150994944 | bytes 4718592 | tf_op jit(solution)/shard_map/project/pallas_call | solution.py:57
  3.0 2.2 %collective-permute-start.6 = (bf16[512,768]{1,0:T(8,128)(2,1)S(1)}, bf16[512,768]{1,0:T(8,128)(2,1)S(1)}, u32[]{:S(2)}, u32[]{:S(2)}) collective-permute-start(bf16[512,768]{1,0:T(8,128)(2,1)S(1)} %get-tuple-element.39.refs_2_), channel_id=1, source_target_pairs={{0,8},{8,16},{16,24},{24,0},{1,9},{9,17},{17,25},{25,1},{2,10},{10... | collective-permute-start | bytes 2359304 | tf_op jit(solution)/shard_map/ppermute | solution.py:274
  5.2 1.5 %collective-permute-start.7 = (bf16[512,768]{1,0:T(8,128)(2,1)S(1)}, bf16[512,768]{1,0:T(8,128)(2,1)S(1)}, u32[]{:S(2)}, u32[]{:S(2)}) collective-permute-start(bf16[512,768]{1,0:T(8,128)(2,1)S(1)} %get-tuple-element.39.refs_2_), channel_id=1, source_target_pairs={{0,24},{8,0},{16,8},{24,16},{1,25},{9,1},{17,9},{25,17},{2,26},{10... | collective-permute-start | bytes 2359304 | tf_op jit(solution)/shard_map/ppermute | solution.py:274
  6.8 3.0 %collective-permute-start = (bf16[32,768]{1,0:T(8,128)(2,1)S(1)}, bf16[32,768]{1,0:T(8,128)(2,1)S(1)}, u32[]{:S(2)}, u32[]{:S(2)}) collective-permute-start(bf16[32,768]{1,0:T(8,128)(2,1)S(1)} %get-tuple-element.33), channel_id=1, source_target_pairs={{0,1},{1,2},{2,3},{3,0},{4,5},{5,6},{6,7},{7,4},{8,9},{9,10},{10,1... | collective-permute-start | bytes 147464 | tf_op jit(solution)/shard_map/ppermute | solution.py:274
  9.8 5.1 %collective-permute-start.1 = (bf16[32,768]{1,0:T(8,128)(2,1)S(1)}, bf16[32,768]{1,0:T(8,128)(2,1)S(1)}, u32[]{:S(2)}, u32[]{:S(2)}) collective-permute-start(bf16[32,768]{1,0:T(8,128)(2,1)S(1)} %get-tuple-element.34), channel_id=1, source_target_pairs={{0,2},{1,3},{2,0},{3,1},{4,6},{5,7},{6,4},{7,5},{8,10},{9,11},{10,... | collective-permute-start | bytes 147464 | tf_op jit(solution)/shard_map/ppermute | solution.py:274
  14.9 2.4 %collective-permute-start.2 = (bf16[32,768]{1,0:T(8,128)(2,1)S(1)}, bf16[32,768]{1,0:T(8,128)(2,1)S(1)}, u32[]{:S(2)}, u32[]{:S(2)}) collective-permute-start(bf16[32,768]{1,0:T(8,128)(2,1)S(1)} %get-tuple-element.35), channel_id=1, source_target_pairs={{0,3},{1,0},{2,1},{3,2},{4,7},{5,4},{6,5},{7,6},{8,11},{9,8},{10,9... | collective-permute-start | bytes 147464 | tf_op jit(solution)/shard_map/ppermute | solution.py:274
  17.3 3.0 %collective-permute-done.2.c = bf16[32,768]{1,0:T(8,128)(2,1)S(1)} collective-permute-done((bf16[32,768]{1,0:T(8,128)(2,1)S(1)}, bf16[32,768]{1,0:T(8,128)(2,1)S(1)}, u32[]{:S(2)}, u32[]{:S(2)}) %collective-permute-start.2) | collective-permute-done | bytes 49184 | tf_op jit(solution)/shard_map/ppermute | solution.py:274
  20.4 1.3 %collective-permute-start.4 = (bf16[512,384]{1,0:T(8,128)(2,1)S(1)}, bf16[512,384]{1,0:T(8,128)(2,1)S(1)}, u32[]{:S(2)}, u32[]{:S(2)}) collective-permute-start(bf16[512,384]{1,0:T(8,128)(2,1)S(1)} %copy-done), channel_id=1, source_target_pairs={{0,4},{4,0},{1,5},{5,1},{2,6},{6,2},{3,7},{7,3},{8,12},{12,8},{9,1... | collective-permute-start | bytes 1179656 | tf_op jit(solution)/shard_map/ppermute | solution.py:274
  21.7 0.8 %collective-permute-start.3 = (bf16[32,768]{1,0:T(8,128)(2,1)S(1)}, bf16[32,768]{1,0:T(8,128)(2,1)S(1)}, u32[]{:S(2)}, u32[]{:S(2)}) collective-permute-start(bf16[32,768]{1,0:T(8,128)(2,1)S(1)} %norm.1), channel_id=1, source_target_pairs={{0,32},{32,0},{1,33},{33,1},{2,34},{34,2},{3,35},{35,3},{4,36},{36... | collective-permute-start | bytes 147464 | tf_op jit(solution)/shard_map/ppermute | solution.py:274
  22.6 2.2 %collective-permute-done.3 = bf16[32,768]{1,0:T(8,128)(2,1)S(1)} collective-permute-done((bf16[32,768]{1,0:T(8,128)(2,1)S(1)}, bf16[32,768]{1,0:T(8,128)(2,1)S(1)}, u32[]{:S(2)}, u32[]{:S(2)}) %collective-permute-start.3) | collective-permute-done | bytes 49184 | tf_op jit(solution)/shard_map/ppermute | solution.py:274
  25.2 2.4 %collective-permute-start.8 = (bf16[64,768]{1,0:T(8,128)(2,1)S(1)}, bf16[64,768]{1,0:T(8,128)(2,1)S(1)}, u32[]{:S(2)}, u32[]{:S(2)}) collective-permute-start(bf16[64,768]{1,0:T(8,128)(2,1)S(1)} %get-tuple-element.59), channel_id=1, source_target_pairs={{0,24},{8,0},{16,8},{24,16},{1,25},{9,1},{17,9},{25,17},{2,26},{10... | collective-permute-start | bytes 294920 | tf_op jit(solution)/shard_map/ppermute | solution.py:274
  28.3 1.3 %collective-permute-done.5 = bf16[64,768]{1,0:T(8,128)(2,1)S(1)} collective-permute-done((bf16[64,768]{1,0:T(8,128)(2,1)S(1)}, bf16[64,768]{1,0:T(8,128)(2,1)S(1)}, u32[]{:S(2)}, u32[]{:S(2)}) %collective-permute-start.5) | collective-permute-done | bytes 98336 | tf_op jit(solution)/shard_map/ppermute | solution.py:274
  29.7 2.7 %collective-permute-start.14 = (bf16[256,768]{1,0:T(8,128)(2,1)S(1)}, bf16[256,768]{1,0:T(8,128)(2,1)S(1)}, u32[]{:S(2)}, u32[]{:S(2)}) collective-permute-start(bf16[256,768]{1,0:T(8,128)(2,1)S(1)} %slice.7), channel_id=1, source_target_pairs={{0,24},{8,0},{16,8},{24,16},{1,25},{9,1},{17,9},{25,17},{2,26},{10... | collective-permute-start | bytes 1179656 | tf_op jit(solution)/shard_map/ppermute | solution.py:274
  32.6 1.3 %collective-permute-start.10 = (bf16[256,768]{1,0:T(8,128)(2,1)S(1)}, bf16[256,768]{1,0:T(8,128)(2,1)S(1)}, u32[]{:S(2)}, u32[]{:S(2)}) collective-permute-start(bf16[256,768]{1,0:T(8,128)(2,1)S(1)} %constant_dynamic-update-slice_fusion.2.refs_3_), channel_id=1, source_target_pairs={{0,64},{64,128},{128,192},{192,0},{1,65},{65,129},{129,193},{193,1... | collective-permute-start | bytes 1179656 | tf_op jit(solution)/shard_map/ppermute | solution.py:274
  33.8 1.5 %collective-permute-start.11 = (bf16[256,768]{1,0:T(8,128)(2,1)S(1)}, bf16[256,768]{1,0:T(8,128)(2,1)S(1)}, u32[]{:S(2)}, u32[]{:S(2)}) collective-permute-start(bf16[256,768]{1,0:T(8,128)(2,1)S(1)} %constant_dynamic-update-slice_fusion.2.refs_3_), channel_id=1, source_target_pairs={{0,192},{64,0},{128,64},{192,128},{1,193},{65,1},{129,65},{193,129... | collective-permute-start | bytes 1179656 | tf_op jit(solution)/shard_map/ppermute | solution.py:274
  35.3 1.5 %collective-permute-start.12 = (bf16[256,768]{1,0:T(8,128)(2,1)S(1)}, bf16[256,768]{1,0:T(8,128)(2,1)S(1)}, u32[]{:S(2)}, u32[]{:S(2)}) collective-permute-start(bf16[256,768]{1,0:T(8,128)(2,1)S(1)} %constant_dynamic-update-slice_fusion.2.refs_3_), channel_id=1, source_target_pairs={{0,128},{64,192},{128,0},{192,64},{1,129},{65,193},{129,1},{193,65... | collective-permute-start | bytes 1179656 | tf_op jit(solution)/shard_map/ppermute | solution.py:274
  36.8 4.6 %attend.2 = (f32[512,512]{1,0:T(8,128)S(1)}, f32[512,512]{1,0:T(8,128)S(1)}) custom-call(bf16[512,384]{1,0:T(8,128)(2,1)S(1)} %collective-permute-done.4.refs_0_.q, bf16[512,384]{1,0:T(8,128)(2,1)S(1)} %copy-done, bf16[512,768]{1,0:T(8,128)(2,1)S(1)} %get-tuple-element.39.refs_2_, bf16[512,768]{1,0:T(8,128)(2,1)S(1)} %collective-permute-done.6.refs_3_), custom_call_target="tpu_custom_call" | custom-call | tf_op jit(solution)/shard_map/attend/pallas_call | solution.py:169
  41.5 6.1 %attend.3 = (f32[512,512]{1,0:T(8,128)S(1)}, f32[512,512]{1,0:T(8,128)S(1)}) custom-call(bf16[512,384]{1,0:T(8,128)(2,1)S(1)} %collective-permute-done.4.refs_0_.q, bf16[512,384]{1,0:T(8,128)(2,1)S(1)} %copy-done, bf16[512,768]{1,0:T(8,128)(2,1)S(1)} %collective-permute-done.7.refs_2_, bf16[256,768]{1,0:T(8,128)(2,1)S(1)} %constant_dynamic-update-slice_fusion.2.refs_3_, ...), custom_call_target="tpu_custom_call" | custom-call | tf_op jit(solution)/shard_map/attend/pallas_call | solution.py:169
  47.6 1.4 %join.2 = (f32[512,512]{1,0:T(8,128)S(1)}, f32[512,512]{1,0:T(8,128)S(1)}) custom-call(f32[512,512]{1,0:T(8,128)S(1)} %get-tuple-element.46.refs_0_, f32[512,512]{1,0:T(8,128)S(1)} %get-tuple-element.49.refs_1_, f32[512,512]{1,0:T(8,128)S(1)} %get-tuple-element.50.refs_2_, f32[512,512]{1,0:T(8,128)S(1)} %get-tuple-element.51.refs_3_), custom_call_target="tpu_custom_call" | custom-call | flops 3145728 | bytes 4194304 | tf_op jit(solution)/shard_map/join/pallas_call | solution.py:253
  49.6 2.0 %attend_whole.3.refs_1_ = f32[512,512]{1,0:T(8,128)S(1)} custom-call(bf16[512,384]{1,0:T(8,128)(2,1)S(1)} %collective-permute-done.4.refs_0_.q, bf16[256,768]{1,0:T(8,128)(2,1)S(1)} %collective-permute-done.10.refs_0_, bf16[256,768]{1,0:T(8,128)(2,1)S(1)} %collective-permute-done.11.refs_1_, bf16[256,768]{1,0:T(8,128)(2,1)S(1)} %collective-permute-done.12.refs_2_), custom_call_target="tpu_custom_call" | custom-call | tf_op jit(solution)/shard_map/attend_whole/pallas_call | solution.py:211
  51.6 0.8 %join.3 = f32[512,512]{1,0:T(8,128)S(1)} custom-call(f32[512,512]{1,0:T(8,128)S(1)} %get-tuple-element.58.refs_0_, f32[512,512]{1,0:T(8,128)S(1)} %attend_whole.3.refs_1_), custom_call_target="tpu_custom_call" | custom-call | flops 1572864 | bytes 2097152 | tf_op jit(solution)/shard_map/join/pallas_call | solution.py:253
  52.4 5.5 %collective-permute-start.15 = (f32[512,512]{1,0:T(8,128)S(1)}, f32[512,512]{1,0:T(8,128)S(1)}, u32[]{:S(2)}, u32[]{:S(2)}) collective-permute-start(f32[512,512]{1,0:T(8,128)S(1)} %join.3), channel_id=1, source_target_pairs={{0,4},{4,0},{1,5},{5,1},{2,6},{6,2},{3,7},{7,3},{8,12},{12,8},{9,1... | collective-permute-start | bytes 3145736 | tf_op jit(solution)/shard_map/ppermute | solution.py:274
  57.9 2.0 %attend_whole.2.refs_1_ = f32[512,512]{1,0:T(8,128)S(1)} custom-call(bf16[512,384]{1,0:T(8,128)(2,1)S(1)} %copy-done, bf16[256,768]{1,0:T(8,128)(2,1)S(1)} %collective-permute-done.10.refs_0_, bf16[256,768]{1,0:T(8,128)(2,1)S(1)} %collective-permute-done.11.refs_1_, bf16[256,768]{1,0:T(8,128)(2,1)S(1)} %collective-permute-done.12.refs_2_), custom_call_target="tpu_custom_call" | custom-call | tf_op jit(solution)/shard_map/attend_whole/pallas_call | solution.py:211
  60.2 1.8 %join_last.1 = bf16[512,384]{1,0:T(8,128)(2,1)} custom-call(f32[512,512]{1,0:T(8,128)S(1)} %get-tuple-element.54.refs_0_, f32[512,512]{1,0:T(8,128)S(1)} %attend_whole.2.refs_1_, f32[512,512]{1,0:T(8,128)S(1)} %collective-permute-done.15.refs_2_), custom_call_target="tpu_custom_call" | custom-call | tf_op jit(solution)/shard_map/join_last/pallas_call | solution.py:265
  (28 shorter events, 2.2 us)
Async XLA Ops:
  0.0 20.3 %copy-start.1 = (f32[128]{0:T(128)S(1)}, f32[128]{0:T(128)}, u32[]{:S(2)}) copy-start(f32[128]{0:T(128)} %param.13) | copy-start | bytes 1540
  0.0 20.4 %copy-start = (bf16[512,384]{1,0:T(8,128)(2,1)S(1)}, bf16[512,384]{1,0:T(8,128)(2,1)}, u32[]{:S(2)}) copy-start(bf16[512,384]{1,0:T(8,128)(2,1)} %q.1) | copy-start | bytes 1179652
  3.0 26.5 %collective-permute-start.6 = (bf16[512,768]{1,0:T(8,128)(2,1)S(1)}, bf16[512,768]{1,0:T(8,128)(2,1)S(1)}, u32[]{:S(2)}, u32[]{:S(2)}) collective-permute-start(bf16[512,768]{1,0:T(8,128)(2,1)S(1)} %get-tuple-element.39.refs_2_), channel_id=1, source_target_pairs={{0,8},{8,16},{16,24},{24,0},{1,9},{9,17},{17,25},{25,1},{2,10},{10... | collective-permute-start | bytes 2359304 | tf_op jit(solution)/shard_map/ppermute | solution.py:274
  5.2 24.3 %collective-permute-start.7 = (bf16[512,768]{1,0:T(8,128)(2,1)S(1)}, bf16[512,768]{1,0:T(8,128)(2,1)S(1)}, u32[]{:S(2)}, u32[]{:S(2)}) collective-permute-start(bf16[512,768]{1,0:T(8,128)(2,1)S(1)} %get-tuple-element.39.refs_2_), channel_id=1, source_target_pairs={{0,24},{8,0},{16,8},{24,16},{1,25},{9,1},{17,9},{25,17},{2,26},{10... | collective-permute-start | bytes 2359304 | tf_op jit(solution)/shard_map/ppermute | solution.py:274
  6.8 10.5 %collective-permute-start = (bf16[32,768]{1,0:T(8,128)(2,1)S(1)}, bf16[32,768]{1,0:T(8,128)(2,1)S(1)}, u32[]{:S(2)}, u32[]{:S(2)}) collective-permute-start(bf16[32,768]{1,0:T(8,128)(2,1)S(1)} %get-tuple-element.33), channel_id=1, source_target_pairs={{0,1},{1,2},{2,3},{3,0},{4,5},{5,6},{6,7},{7,4},{8,9},{9,10},{10,1... | collective-permute-start | bytes 147464 | tf_op jit(solution)/shard_map/ppermute | solution.py:274
  9.8 7.5 %collective-permute-start.1 = (bf16[32,768]{1,0:T(8,128)(2,1)S(1)}, bf16[32,768]{1,0:T(8,128)(2,1)S(1)}, u32[]{:S(2)}, u32[]{:S(2)}) collective-permute-start(bf16[32,768]{1,0:T(8,128)(2,1)S(1)} %get-tuple-element.34), channel_id=1, source_target_pairs={{0,2},{1,3},{2,0},{3,1},{4,6},{5,7},{6,4},{7,5},{8,10},{9,11},{10,... | collective-permute-start | bytes 147464 | tf_op jit(solution)/shard_map/ppermute | solution.py:274
  14.9 5.4 %collective-permute-start.2 = (bf16[32,768]{1,0:T(8,128)(2,1)S(1)}, bf16[32,768]{1,0:T(8,128)(2,1)S(1)}, u32[]{:S(2)}, u32[]{:S(2)}) collective-permute-start(bf16[32,768]{1,0:T(8,128)(2,1)S(1)} %get-tuple-element.35), channel_id=1, source_target_pairs={{0,3},{1,0},{2,1},{3,2},{4,7},{5,4},{6,5},{7,6},{8,11},{9,8},{10,9... | collective-permute-start | bytes 147464 | tf_op jit(solution)/shard_map/ppermute | solution.py:274
  20.4 4.4 %collective-permute-start.4 = (bf16[512,384]{1,0:T(8,128)(2,1)S(1)}, bf16[512,384]{1,0:T(8,128)(2,1)S(1)}, u32[]{:S(2)}, u32[]{:S(2)}) collective-permute-start(bf16[512,384]{1,0:T(8,128)(2,1)S(1)} %copy-done), channel_id=1, source_target_pairs={{0,4},{4,0},{1,5},{5,1},{2,6},{6,2},{3,7},{7,3},{8,12},{12,8},{9,1... | collective-permute-start | bytes 1179656 | tf_op jit(solution)/shard_map/ppermute | solution.py:274
  21.7 3.1 %collective-permute-start.3 = (bf16[32,768]{1,0:T(8,128)(2,1)S(1)}, bf16[32,768]{1,0:T(8,128)(2,1)S(1)}, u32[]{:S(2)}, u32[]{:S(2)}) collective-permute-start(bf16[32,768]{1,0:T(8,128)(2,1)S(1)} %norm.1), channel_id=1, source_target_pairs={{0,32},{32,0},{1,33},{33,1},{2,34},{34,2},{3,35},{35,3},{4,36},{36... | collective-permute-start | bytes 147464 | tf_op jit(solution)/shard_map/ppermute | solution.py:274
  24.8 4.8 %collective-permute-start.5 = (bf16[64,768]{1,0:T(8,128)(2,1)S(1)}, bf16[64,768]{1,0:T(8,128)(2,1)S(1)}, u32[]{:S(2)}, u32[]{:S(2)}) collective-permute-start(bf16[64,768]{1,0:T(8,128)(2,1)S(1)} %get-tuple-element.59), channel_id=1, source_target_pairs={{0,8},{8,16},{16,24},{24,0},{1,9},{9,17},{17,25},{25,1},{2,10},{10... | collective-permute-start | bytes 294920 | tf_op jit(solution)/shard_map/ppermute | solution.py:274
  25.2 7.3 %collective-permute-start.8 = (bf16[64,768]{1,0:T(8,128)(2,1)S(1)}, bf16[64,768]{1,0:T(8,128)(2,1)S(1)}, u32[]{:S(2)}, u32[]{:S(2)}) collective-permute-start(bf16[64,768]{1,0:T(8,128)(2,1)S(1)} %get-tuple-element.59), channel_id=1, source_target_pairs={{0,24},{8,0},{16,8},{24,16},{1,25},{9,1},{17,9},{25,17},{2,26},{10... | collective-permute-start | bytes 294920 | tf_op jit(solution)/shard_map/ppermute | solution.py:274
  27.6 5.0 %collective-permute-start.9 = (bf16[64,768]{1,0:T(8,128)(2,1)S(1)}, bf16[64,768]{1,0:T(8,128)(2,1)S(1)}, u32[]{:S(2)}, u32[]{:S(2)}) collective-permute-start(bf16[64,768]{1,0:T(8,128)(2,1)S(1)} %get-tuple-element.59), channel_id=1, source_target_pairs={{0,16},{8,24},{16,0},{24,8},{1,17},{9,25},{17,1},{25,9},{2,18},{10... | collective-permute-start | bytes 294920 | tf_op jit(solution)/shard_map/ppermute | solution.py:274
  29.6 11.9 %collective-permute-start.13 = (bf16[256,768]{1,0:T(8,128)(2,1)S(1)}, bf16[256,768]{1,0:T(8,128)(2,1)S(1)}, u32[]{:S(2)}, u32[]{:S(2)}) collective-permute-start(bf16[256,768]{1,0:T(8,128)(2,1)S(1)} %slice.6), channel_id=1, source_target_pairs={{0,8},{8,16},{16,24},{24,0},{1,9},{9,17},{17,25},{25,1},{2,10},{10... | collective-permute-start | bytes 1179656 | tf_op jit(solution)/shard_map/ppermute | solution.py:274
  29.7 11.8 %collective-permute-start.14 = (bf16[256,768]{1,0:T(8,128)(2,1)S(1)}, bf16[256,768]{1,0:T(8,128)(2,1)S(1)}, u32[]{:S(2)}, u32[]{:S(2)}) collective-permute-start(bf16[256,768]{1,0:T(8,128)(2,1)S(1)} %slice.7), channel_id=1, source_target_pairs={{0,24},{8,0},{16,8},{24,16},{1,25},{9,1},{17,9},{25,17},{2,26},{10... | collective-permute-start | bytes 1179656 | tf_op jit(solution)/shard_map/ppermute | solution.py:274
  32.6 16.5 %collective-permute-start.10 = (bf16[256,768]{1,0:T(8,128)(2,1)S(1)}, bf16[256,768]{1,0:T(8,128)(2,1)S(1)}, u32[]{:S(2)}, u32[]{:S(2)}) collective-permute-start(bf16[256,768]{1,0:T(8,128)(2,1)S(1)} %constant_dynamic-update-slice_fusion.2.refs_3_), channel_id=1, source_target_pairs={{0,64},{64,128},{128,192},{192,0},{1,65},{65,129},{129,193},{193,1... | collective-permute-start | bytes 1179656 | tf_op jit(solution)/shard_map/ppermute | solution.py:274
  33.8 15.2 %collective-permute-start.11 = (bf16[256,768]{1,0:T(8,128)(2,1)S(1)}, bf16[256,768]{1,0:T(8,128)(2,1)S(1)}, u32[]{:S(2)}, u32[]{:S(2)}) collective-permute-start(bf16[256,768]{1,0:T(8,128)(2,1)S(1)} %constant_dynamic-update-slice_fusion.2.refs_3_), channel_id=1, source_target_pairs={{0,192},{64,0},{128,64},{192,128},{1,193},{65,1},{129,65},{193,129... | collective-permute-start | bytes 1179656 | tf_op jit(solution)/shard_map/ppermute | solution.py:274
  35.3 14.3 %collective-permute-start.12 = (bf16[256,768]{1,0:T(8,128)(2,1)S(1)}, bf16[256,768]{1,0:T(8,128)(2,1)S(1)}, u32[]{:S(2)}, u32[]{:S(2)}) collective-permute-start(bf16[256,768]{1,0:T(8,128)(2,1)S(1)} %constant_dynamic-update-slice_fusion.2.refs_3_), channel_id=1, source_target_pairs={{0,128},{64,192},{128,0},{192,64},{1,129},{65,193},{129,1},{193,65... | collective-permute-start | bytes 1179656 | tf_op jit(solution)/shard_map/ppermute | solution.py:274
  52.4 7.8 %collective-permute-start.15 = (f32[512,512]{1,0:T(8,128)S(1)}, f32[512,512]{1,0:T(8,128)S(1)}, u32[]{:S(2)}, u32[]{:S(2)}) collective-permute-start(f32[512,512]{1,0:T(8,128)S(1)} %join.3), channel_id=1, source_target_pairs={{0,4},{4,0},{1,5},{5,1},{2,6},{6,2},{3,7},{7,3},{8,12},{12,8},{9,1... | collective-permute-start | bytes 3145736 | tf_op jit(solution)/shard_map/ppermute | solution.py:274

commit v6 on v5

--- a/solution.py
+++ b/solution.py
@@ -104,87 +104,12 @@
     )(own, a, b, c, gain)
 
 
-def attend_kernel(moves, keys, chunk, block, count_q, *refs):
-    operands = 1 + max(move[0] for move in moves)
-    queries, refs = refs[:count_q], refs[count_q:]
-    pieces, refs = refs[:operands], refs[operands:]
-    outs, (held, sems) = refs[:count_q], refs[count_q:]
-    copies = []
-    for index, (operand, source, count, row, col, width) in enumerate(moves):
-        copy = pltpu.make_async_copy(
-            pieces[operand].at[pl.ds(source, count), :],
-            held.at[pl.ds(row, count), pl.ds(col, width)],
-            sems.at[index],
-        )
-        copy.start()
-        copies.append((row, copy))
-    ones = jnp.ones((chunk, HD), jnp.bfloat16)
-    rows = queries[0].shape[0]
-    state = {}
-    for base in range(0, keys, chunk):
-        for begin, copy in copies:
-            if base <= begin < base + chunk:
-                copy.wait()
-        for which, low in [(which, low) for which in range(count_q) for low in range(0, rows, block)]:
-            q, out = queries[which], outs[which]
-            here = slice(low, low + block)
-            for head in range(HEADS_HERE):
-                cols = slice(head * HD, (head + 1) * HD)
-                vals = slice(WIDTH + head * HD, WIDTH + (head + 1) * HD)
-                old = state.get((which, low, head))
-                scores = lax.dot_general(
-                    q[here, cols],
-                    held[base : base + chunk, cols],
-                    (((1,), (1,)), ((), ())),
-                    preferred_element_type=jnp.float32,
-                )
-                raised = jnp.max(scores, axis=1, keepdims=True) * FACTOR
-                if old is not None:
-                    raised = jnp.maximum(raised, old[0])
-                weights = jnp.exp2(scores * FACTOR - raised).astype(jnp.bfloat16)
-                mixed = jnp.dot(
-                    weights,
-                    jnp.concatenate((held[base : base + chunk, vals], ones), axis=1),
-                    preferred_element_type=jnp.float32,
-                )
-                acc, total = mixed[:, :HD], mixed[:, HD:]
-                if old is not None:
-                    rescale = jnp.exp2(old[0] - raised)
-                    acc = old[2] * rescale + acc
-                    total = old[1] * rescale + total
-                state[which, low, head] = (raised, total, acc)
-                if base + chunk >= keys:
-                    if head == 0:
-                        out[here, WIDTH:] = jnp.zeros((block, HD), jnp.float32)
-                    out[here, cols] = acc
-                    out[here, WIDTH + head : WIDTH + head + 1] = raised
-                    out[here, WIDTH + HEADS_HERE + head : WIDTH + HEADS_HERE + head + 1] = total[:, :1]
-
-
-def attend(queries, pieces, moves, chunk=1024, block=256):
-    rows = queries[0].shape[0]
-    keys = max(move[2] + move[3] for move in moves)
-    chunk = min(chunk, keys)
-    vmem, anywhere = pl.BlockSpec(memory_space=pltpu.VMEM), pl.BlockSpec(memory_space=pl.ANY)
-    return pl.pallas_call(
-        functools.partial(attend_kernel, moves, keys, chunk, block, len(queries)),
-        out_shape=(jax.ShapeDtypeStruct((rows, WIDTH + HD), jnp.float32),) * len(queries),
-        in_specs=[vmem] * len(queries) + [anywhere] * len(pieces),
-        out_specs=(vmem,) * len(queries),
-        scratch_shapes=[
-            pltpu.VMEM((keys, 2 * WIDTH), jnp.bfloat16),
-            pltpu.SemaphoreType.DMA((len(moves),)),
-        ],
-        compiler_params=pltpu.CompilerParams(vmem_limit_bytes=20 << 20),
-        name="attend",
-    )(*queries, *pieces)
-
-
-def attend_whole_kernel(block, q, *refs):
-    *pieces, out = refs
+def attend_whole_kernel(block, count_q, *refs):
+    queries, pieces, outs = refs[:count_q], refs[count_q:-count_q], refs[-count_q:]
     keys = sum(piece.shape[0] for piece in pieces)
     ones = jnp.ones((keys, HD), jnp.bfloat16)
-    for low in range(0, q.shape[0], block):
+    for which, low in [(which, low) for which in range(count_q) for low in range(0, queries[0].shape[0], block)]:
+        q, out = queries[which], outs[which]
         here = slice(low, low + block)
         out[here, WIDTH:] = jnp.zeros((block, HD), jnp.float32)
         for head in range(HEADS_HERE):
@@ -207,13 +132,14 @@
             out[here, WIDTH + HEADS_HERE + head : WIDTH + HEADS_HERE + head + 1] = mixed[:, HD : HD + 1]
 
 
-def attend_whole(q, pieces, block=256):
-    return pl.pallas_call(
-        functools.partial(attend_whole_kernel, block),
-        out_shape=jax.ShapeDtypeStruct((q.shape[0], WIDTH + HD), jnp.float32),
+def attend_whole(queries, pieces, block=256):
+    shape = jax.ShapeDtypeStruct((queries[0].shape[0], WIDTH + HD), jnp.float32)
+    return pl.pallas_call(
+        functools.partial(attend_whole_kernel, block, len(queries)),
+        out_shape=(shape,) * len(queries),
         compiler_params=pltpu.CompilerParams(vmem_limit_bytes=20 << 20),
         name="attend_whole",
-    )(q, *pieces)
+    )(*queries, *pieces)
 
 
 def join_kernel(count, *refs):
@@ -293,18 +219,15 @@
     half = rows // 2
     opposite = [hop(back[:half], "y", 1), hop(ahead[half:], "y", 3)]
 
-    moves = [(i, 0, rows, i * rows, 0, 2 * WIDTH) for i in range(2)]
-    peer_a, own_a = attend((q_peer, q_tok), (beside, back), moves)
+    peer_a, own_a = attend_whole((q_peer, q_tok), (beside, back))
     opposite, peer_a, own_a = barrier((opposite, peer_a, own_a))
-    size = block.shape[0]
-    moves = [(0, 0, rows, 0, 0, 2 * WIDTH), (1, 0, size, 2 * rows, 0, 2 * WIDTH)]
-    moves += [(2 + i, 0, half, rows + i * half, 0, 2 * WIDTH) for i in range(2)]
-    peer_b, own_b = attend((q_peer, q_tok), [ahead, block] + opposite, moves, chunk=2 * rows + size)
+    peer_b, own_b = attend_whole((q_peer, q_tok), [ahead, block] + opposite)
     peer_ab, own_ab = join((peer_a, peer_b), (own_a, own_b))
     late, peer_ab, own_ab = barrier((late, peer_ab, own_ab))
-    peer_c = attend_whole(q_peer, late)
+    (peer_c,) = attend_whole((q_peer,), late)
     from_peer = hop(*join((peer_ab, peer_c)), "core", 1)
-    return join_last((own_ab, attend_whole(q_tok, late), from_peer))
+    (own_c,) = attend_whole((q_tok,), late)
+    return join_last((own_ab, own_c, from_peer))
 
 
 def solution(mesh):

time: 62.1 us -> 62.1 us (level)
  waiting for transfers between devices: 7.53 us -> 8.24 us
    ppermute x16, waiting for transfers between devices: 7.53 us -> 8.24 us  [hop(): lax.ppermute(block, axis, ring(2 if axis in ('w', 'core') else 4, shift))]
  transfers between devices with their start and end apart: 16 -> 16, of which waited for: 5 -> 5; matrix products, arithmetic and copies ran while one was open for 0% -> 0% of each run, Pallas kernels for 23% -> 22%
where the time goes in v6:
time: 62.1 us; the launch traced here: 62 us
  starting transfers between devices  32.1 us (52%)
  Pallas kernels  21.4 us (34%)
  waiting for transfers between devices  8.24 us (13%)
    ppermute x16, starting transfers between devices, hop(): lax.ppermute(block, axis, ring(2 if axis in ('w', 'core') else 4, shift))  32.1 us
    pallas_call x4, Pallas kernels, attend_whole(): pl.pallas_call(functools.partial(attend_whole_kernel, block, len(queries)...  14.3 us
    ppermute x16, waiting for transfers between devices, hop(): lax.ppermute(block, axis, ring(2 if axis in ('w', 'core') else 4, shift))  8.24 us
    pallas_call x1, Pallas kernels, project(): pl.pallas_call(project_kernel, out_shape=(jax.ShapeDtypeStruct((rows, 2 *...  3.03 us
    pallas_call x2, Pallas kernels, join(): pl.pallas_call(functools.partial(join_kernel, len(groups)), out_shape=(ja...  2.21 us
    pallas_call x1, Pallas kernels, join_last(): pl.pallas_call(join_last_kernel, out_shape=jax.ShapeDtypeStruct((parts[0]...  1.82 us
  transfers between devices with their start and end apart: 16, of which 5 were waited for; matrix products, arithmetic and copies ran while one was open for 0% of the time, Pallas kernels for 22%

profile of v6, /device:TPU:1, one launch (start us, length us, event | category | flops | bytes accessed | tf_op | source)
XLA Modules:
  0.0 62.0 jit_solution(17376851536500572866)
XLA Ops:
  0.0 3.0 %project.1 = (f32[32,768]{1,0:T(8,128)S(1)}, bf16[32,768]{1,0:T(8,128)(2,1)S(1)}, bf16[32,768]{1,0:T(8,128)(2,1)S(1)}, bf16[32,768]{1,0:T(8,128)(2,1)S(1)}, bf16[512,768]{1,0:T(8,128)(2,1)S(1)}) custom-call(bf16[32,768]{1,0:T(8,128)(2,1)} %hidden.1, bf16[768,1536]{1,0:T(8,128)(2,1)} %wk.1, bf16[768,1536]{1,0:T(8,128)(2,1)} %wv.1, bf16[512,384]{1,0:T(8,128)(2,1)} %k_tok.1, ...), custom_call_target="tpu_custom_call" | custom-call | flops 150994944 | bytes 4718592 | tf_op jit(solution)/shard_map/project/pallas_call | solution.py:57
  3.0 2.2 %collective-permute-start.6 = (bf16[512,768]{1,0:T(8,128)(2,1)S(1)}, bf16[512,768]{1,0:T(8,128)(2,1)S(1)}, u32[]{:S(2)}, u32[]{:S(2)}) collective-permute-start(bf16[512,768]{1,0:T(8,128)(2,1)S(1)} %get-tuple-element.39.refs_2_), channel_id=1, source_target_pairs={{0,8},{8,16},{16,24},{24,0},{1,9},{9,17},{17,25},{25,1},{2,10},{10... | collective-permute-start | bytes 2359304 | tf_op jit(solution)/shard_map/ppermute | solution.py:200
  5.2 1.5 %collective-permute-start.7 = (bf16[512,768]{1,0:T(8,128)(2,1)S(1)}, bf16[512,768]{1,0:T(8,128)(2,1)S(1)}, u32[]{:S(2)}, u32[]{:S(2)}) collective-permute-start(bf16[512,768]{1,0:T(8,128)(2,1)S(1)} %get-tuple-element.39.refs_2_), channel_id=1, source_target_pairs={{0,24},{8,0},{16,8},{24,16},{1,25},{9,1},{17,9},{25,17},{2,26},{10... | collective-permute-start | bytes 2359304 | tf_op jit(solution)/shard_map/ppermute | solution.py:200
  6.8 3.0 %collective-permute-start = (bf16[32,768]{1,0:T(8,128)(2,1)S(1)}, bf16[32,768]{1,0:T(8,128)(2,1)S(1)}, u32[]{:S(2)}, u32[]{:S(2)}) collective-permute-start(bf16[32,768]{1,0:T(8,128)(2,1)S(1)} %get-tuple-element.33), channel_id=1, source_target_pairs={{0,1},{1,2},{2,3},{3,0},{4,5},{5,6},{6,7},{7,4},{8,9},{9,10},{10,1... | collective-permute-start | bytes 147464 | tf_op jit(solution)/shard_map/ppermute | solution.py:200
  9.8 5.1 %collective-permute-start.1 = (bf16[32,768]{1,0:T(8,128)(2,1)S(1)}, bf16[32,768]{1,0:T(8,128)(2,1)S(1)}, u32[]{:S(2)}, u32[]{:S(2)}) collective-permute-start(bf16[32,768]{1,0:T(8,128)(2,1)S(1)} %get-tuple-element.34), channel_id=1, source_target_pairs={{0,2},{1,3},{2,0},{3,1},{4,6},{5,7},{6,4},{7,5},{8,10},{9,11},{10,... | collective-permute-start | bytes 147464 | tf_op jit(solution)/shard_map/ppermute | solution.py:200
  14.9 2.4 %collective-permute-start.2 = (bf16[32,768]{1,0:T(8,128)(2,1)S(1)}, bf16[32,768]{1,0:T(8,128)(2,1)S(1)}, u32[]{:S(2)}, u32[]{:S(2)}) collective-permute-start(bf16[32,768]{1,0:T(8,128)(2,1)S(1)} %get-tuple-element.35), channel_id=1, source_target_pairs={{0,3},{1,0},{2,1},{3,2},{4,7},{5,4},{6,5},{7,6},{8,11},{9,8},{10,9... | collective-permute-start | bytes 147464 | tf_op jit(solution)/shard_map/ppermute | solution.py:200
  17.3 3.0 %collective-permute-done.2.c = bf16[32,768]{1,0:T(8,128)(2,1)S(1)} collective-permute-done((bf16[32,768]{1,0:T(8,128)(2,1)S(1)}, bf16[32,768]{1,0:T(8,128)(2,1)S(1)}, u32[]{:S(2)}, u32[]{:S(2)}) %collective-permute-start.2) | collective-permute-done | bytes 49184 | tf_op jit(solution)/shard_map/ppermute | solution.py:200
  20.4 1.3 %collective-permute-start.4 = (bf16[512,384]{1,0:T(8,128)(2,1)S(1)}, bf16[512,384]{1,0:T(8,128)(2,1)S(1)}, u32[]{:S(2)}, u32[]{:S(2)}) collective-permute-start(bf16[512,384]{1,0:T(8,128)(2,1)S(1)} %copy-done), channel_id=1, source_target_pairs={{0,4},{4,0},{1,5},{5,1},{2,6},{6,2},{3,7},{7,3},{8,12},{12,8},{9,1... | collective-permute-start | bytes 1179656 | tf_op jit(solution)/shard_map/ppermute | solution.py:200
  21.7 0.8 %collective-permute-start.3 = (bf16[32,768]{1,0:T(8,128)(2,1)S(1)}, bf16[32,768]{1,0:T(8,128)(2,1)S(1)}, u32[]{:S(2)}, u32[]{:S(2)}) collective-permute-start(bf16[32,768]{1,0:T(8,128)(2,1)S(1)} %norm.1), channel_id=1, source_target_pairs={{0,32},{32,0},{1,33},{33,1},{2,34},{34,2},{3,35},{35,3},{4,36},{36... | collective-permute-start | bytes 147464 | tf_op jit(solution)/shard_map/ppermute | solution.py:200
  22.6 2.2 %collective-permute-done.3 = bf16[32,768]{1,0:T(8,128)(2,1)S(1)} collective-permute-done((bf16[32,768]{1,0:T(8,128)(2,1)S(1)}, bf16[32,768]{1,0:T(8,128)(2,1)S(1)}, u32[]{:S(2)}, u32[]{:S(2)}) %collective-permute-start.3) | collective-permute-done | bytes 49184 | tf_op jit(solution)/shard_map/ppermute | solution.py:200
  25.2 2.4 %collective-permute-start.8 = (bf16[64,768]{1,0:T(8,128)(2,1)S(1)}, bf16[64,768]{1,0:T(8,128)(2,1)S(1)}, u32[]{:S(2)}, u32[]{:S(2)}) collective-permute-start(bf16[64,768]{1,0:T(8,128)(2,1)S(1)} %get-tuple-element.59), channel_id=1, source_target_pairs={{0,24},{8,0},{16,8},{24,16},{1,25},{9,1},{17,9},{25,17},{2,26},{10... | collective-permute-start | bytes 294920 | tf_op jit(solution)/shard_map/ppermute | solution.py:200
  28.3 1.3 %collective-permute-done.5 = bf16[64,768]{1,0:T(8,128)(2,1)S(1)} collective-permute-done((bf16[64,768]{1,0:T(8,128)(2,1)S(1)}, bf16[64,768]{1,0:T(8,128)(2,1)S(1)}, u32[]{:S(2)}, u32[]{:S(2)}) %collective-permute-start.5) | collective-permute-done | bytes 98336 | tf_op jit(solution)/shard_map/ppermute | solution.py:200
  29.7 2.7 %collective-permute-start.14 = (bf16[256,768]{1,0:T(8,128)(2,1)S(1)}, bf16[256,768]{1,0:T(8,128)(2,1)S(1)}, u32[]{:S(2)}, u32[]{:S(2)}) collective-permute-start(bf16[256,768]{1,0:T(8,128)(2,1)S(1)} %slice.7), channel_id=1, source_target_pairs={{0,24},{8,0},{16,8},{24,16},{1,25},{9,1},{17,9},{25,17},{2,26},{10... | collective-permute-start | bytes 1179656 | tf_op jit(solution)/shard_map/ppermute | solution.py:200
  32.6 1.3 %collective-permute-start.10 = (bf16[256,768]{1,0:T(8,128)(2,1)S(1)}, bf16[256,768]{1,0:T(8,128)(2,1)S(1)}, u32[]{:S(2)}, u32[]{:S(2)}) collective-permute-start(bf16[256,768]{1,0:T(8,128)(2,1)S(1)} %constant_dynamic-update-slice_fusion.2.refs_3_), channel_id=1, source_target_pairs={{0,64},{64,128},{128,192},{192,0},{1,65},{65,129},{129,193},{193,1... | collective-permute-start | bytes 1179656 | tf_op jit(solution)/shard_map/ppermute | solution.py:200
  33.8 1.5 %collective-permute-start.11 = (bf16[256,768]{1,0:T(8,128)(2,1)S(1)}, bf16[256,768]{1,0:T(8,128)(2,1)S(1)}, u32[]{:S(2)}, u32[]{:S(2)}) collective-permute-start(bf16[256,768]{1,0:T(8,128)(2,1)S(1)} %constant_dynamic-update-slice_fusion.2.refs_3_), channel_id=1, source_target_pairs={{0,192},{64,0},{128,64},{192,128},{1,193},{65,1},{129,65},{193,129... | collective-permute-start | bytes 1179656 | tf_op jit(solution)/shard_map/ppermute | solution.py:200
  35.3 1.5 %collective-permute-start.12 = (bf16[256,768]{1,0:T(8,128)(2,1)S(1)}, bf16[256,768]{1,0:T(8,128)(2,1)S(1)}, u32[]{:S(2)}, u32[]{:S(2)}) collective-permute-start(bf16[256,768]{1,0:T(8,128)(2,1)S(1)} %constant_dynamic-update-slice_fusion.2.refs_3_), channel_id=1, source_target_pairs={{0,128},{64,192},{128,0},{192,64},{1,129},{65,193},{129,1},{193,65... | collective-permute-start | bytes 1179656 | tf_op jit(solution)/shard_map/ppermute | solution.py:200
  36.8 4.5 %attend_whole.4 = (f32[512,512]{1,0:T(8,128)S(1)}, f32[512,512]{1,0:T(8,128)S(1)}) custom-call(bf16[512,384]{1,0:T(8,128)(2,1)S(1)} %collective-permute-done.4.refs_0_, bf16[512,384]{1,0:T(8,128)(2,1)S(1)} %copy-done, bf16[512,768]{1,0:T(8,128)(2,1)S(1)} %get-tuple-element.39.refs_2_, bf16[512,768]{1,0:T(8,128)(2,1)S(1)} %collective-permute-done.6.refs_3_), custom_call_target="tpu_custom_call" | custom-call | tf_op jit(solution)/shard_map/attend_whole/pallas_call | solution.py:137
  41.4 5.5 %attend_whole.5 = (f32[512,512]{1,0:T(8,128)S(1)}, f32[512,512]{1,0:T(8,128)S(1)}) custom-call(bf16[512,384]{1,0:T(8,128)(2,1)S(1)} %collective-permute-done.4.refs_0_, bf16[512,384]{1,0:T(8,128)(2,1)S(1)} %copy-done, bf16[512,768]{1,0:T(8,128)(2,1)S(1)} %collective-permute-done.7.refs_2_, bf16[256,768]{1,0:T(8,128)(2,1)S(1)} %constant_dynamic-update-slice_fusion.2.refs_3_, ...), custom_call_target="tpu_custom_call" | custom-call | tf_op jit(solution)/shard_map/attend_whole/pallas_call | solution.py:137
  46.9 1.4 %join.2 = (f32[512,512]{1,0:T(8,128)S(1)}, f32[512,512]{1,0:T(8,128)S(1)}) custom-call(f32[512,512]{1,0:T(8,128)S(1)} %get-tuple-element.46.refs_0_, f32[512,512]{1,0:T(8,128)S(1)} %get-tuple-element.49.refs_1_, f32[512,512]{1,0:T(8,128)S(1)} %get-tuple-element.50.refs_2_, f32[512,512]{1,0:T(8,128)S(1)} %get-tuple-element.51.refs_3_), custom_call_target="tpu_custom_call" | custom-call | flops 3145728 | bytes 4194304 | tf_op jit(solution)/shard_map/join/pallas_call | solution.py:179
  48.3 1.3 %collective-permute-done.12.refs_3_ = bf16[256,768]{1,0:T(8,128)(2,1)S(1)} collective-permute-done((bf16[256,768]{1,0:T(8,128)(2,1)S(1)}, bf16[256,768]{1,0:T(8,128)(2,1)S(1)}, u32[]{:S(2)}, u32[]{:S(2)}) %collective-permute-start.12) | collective-permute-done | bytes 393248 | tf_op jit(solution)/shard_map/ppermute | solution.py:200
  49.6 2.2 %attend_whole.7.refs_1_ = f32[512,512]{1,0:T(8,128)S(1)} custom-call(bf16[512,384]{1,0:T(8,128)(2,1)S(1)} %collective-permute-done.4.refs_0_, bf16[256,768]{1,0:T(8,128)(2,1)S(1)} %collective-permute-done.10.refs_1_, bf16[256,768]{1,0:T(8,128)(2,1)S(1)} %collective-permute-done.11.refs_2_, bf16[256,768]{1,0:T(8,128)(2,1)S(1)} %collective-permute-done.12.refs_3_), custom_call_target="tpu_custom_call" | custom-call | tf_op jit(solution)/shard_map/attend_whole/pallas_call | solution.py:137
  52.7 5.2 %collective-permute-start.15 = (f32[512,512]{1,0:T(8,128)S(1)}, f32[512,512]{1,0:T(8,128)S(1)}, u32[]{:S(2)}, u32[]{:S(2)}) collective-permute-start(f32[512,512]{1,0:T(8,128)S(1)} %join.3), channel_id=1, source_target_pairs={{0,4},{4,0},{1,5},{5,1},{2,6},{6,2},{3,7},{7,3},{8,12},{12,8},{9,1... | collective-permute-start | bytes 3145736 | tf_op jit(solution)/shard_map/ppermute | solution.py:200
  57.9 2.0 %attend_whole.6.refs_1_ = f32[512,512]{1,0:T(8,128)S(1)} custom-call(bf16[512,384]{1,0:T(8,128)(2,1)S(1)} %copy-done, bf16[256,768]{1,0:T(8,128)(2,1)S(1)} %collective-permute-done.10.refs_1_, bf16[256,768]{1,0:T(8,128)(2,1)S(1)} %collective-permute-done.11.refs_2_, bf16[256,768]{1,0:T(8,128)(2,1)S(1)} %collective-permute-done.12.refs_3_), custom_call_target="tpu_custom_call" | custom-call | tf_op jit(solution)/shard_map/attend_whole/pallas_call | solution.py:137
  60.2 1.8 %join_last.1 = bf16[512,384]{1,0:T(8,128)(2,1)} custom-call(f32[512,512]{1,0:T(8,128)S(1)} %get-tuple-element.54.refs_0_, f32[512,512]{1,0:T(8,128)S(1)} %attend_whole.6.refs_1_, f32[512,512]{1,0:T(8,128)S(1)} %collective-permute-done.15.refs_2_), custom_call_target="tpu_custom_call" | custom-call | tf_op jit(solution)/shard_map/join_last/pallas_call | solution.py:191
  (28 shorter events, 2.4 us)
Async XLA Ops:
  0.0 20.3 %copy-start.1 = (f32[128]{0:T(128)S(1)}, f32[128]{0:T(128)}, u32[]{:S(2)}) copy-start(f32[128]{0:T(128)} %param.13) | copy-start | bytes 1540
  0.0 20.4 %copy-start = (bf16[512,384]{1,0:T(8,128)(2,1)S(1)}, bf16[512,384]{1,0:T(8,128)(2,1)}, u32[]{:S(2)}) copy-start(bf16[512,384]{1,0:T(8,128)(2,1)} %refs_0_.1) | copy-start | bytes 1179652
  3.0 26.5 %collective-permute-start.6 = (bf16[512,768]{1,0:T(8,128)(2,1)S(1)}, bf16[512,768]{1,0:T(8,128)(2,1)S(1)}, u32[]{:S(2)}, u32[]{:S(2)}) collective-permute-start(bf16[512,768]{1,0:T(8,128)(2,1)S(1)} %get-tuple-element.39.refs_2_), channel_id=1, source_target_pairs={{0,8},{8,16},{16,24},{24,0},{1,9},{9,17},{17,25},{25,1},{2,10},{10... | collective-permute-start | bytes 2359304 | tf_op jit(solution)/shard_map/ppermute | solution.py:200
  5.2 24.3 %collective-permute-start.7 = (bf16[512,768]{1,0:T(8,128)(2,1)S(1)}, bf16[512,768]{1,0:T(8,128)(2,1)S(1)}, u32[]{:S(2)}, u32[]{:S(2)}) collective-permute-start(bf16[512,768]{1,0:T(8,128)(2,1)S(1)} %get-tuple-element.39.refs_2_), channel_id=1, source_target_pairs={{0,24},{8,0},{16,8},{24,16},{1,25},{9,1},{17,9},{25,17},{2,26},{10... | collective-permute-start | bytes 2359304 | tf_op jit(solution)/shard_map/ppermute | solution.py:200
  6.8 10.5 %collective-permute-start = (bf16[32,768]{1,0:T(8,128)(2,1)S(1)}, bf16[32,768]{1,0:T(8,128)(2,1)S(1)}, u32[]{:S(2)}, u32[]{:S(2)}) collective-permute-start(bf16[32,768]{1,0:T(8,128)(2,1)S(1)} %get-tuple-element.33), channel_id=1, source_target_pairs={{0,1},{1,2},{2,3},{3,0},{4,5},{5,6},{6,7},{7,4},{8,9},{9,10},{10,1... | collective-permute-start | bytes 147464 | tf_op jit(solution)/shard_map/ppermute | solution.py:200
  9.8 7.5 %collective-permute-start.1 = (bf16[32,768]{1,0:T(8,128)(2,1)S(1)}, bf16[32,768]{1,0:T(8,128)(2,1)S(1)}, u32[]{:S(2)}, u32[]{:S(2)}) collective-permute-start(bf16[32,768]{1,0:T(8,128)(2,1)S(1)} %get-tuple-element.34), channel_id=1, source_target_pairs={{0,2},{1,3},{2,0},{3,1},{4,6},{5,7},{6,4},{7,5},{8,10},{9,11},{10,... | collective-permute-start | bytes 147464 | tf_op jit(solution)/shard_map/ppermute | solution.py:200
  14.9 5.4 %collective-permute-start.2 = (bf16[32,768]{1,0:T(8,128)(2,1)S(1)}, bf16[32,768]{1,0:T(8,128)(2,1)S(1)}, u32[]{:S(2)}, u32[]{:S(2)}) collective-permute-start(bf16[32,768]{1,0:T(8,128)(2,1)S(1)} %get-tuple-element.35), channel_id=1, source_target_pairs={{0,3},{1,0},{2,1},{3,2},{4,7},{5,4},{6,5},{7,6},{8,11},{9,8},{10,9... | collective-permute-start | bytes 147464 | tf_op jit(solution)/shard_map/ppermute | solution.py:200
  20.4 4.4 %collective-permute-start.4 = (bf16[512,384]{1,0:T(8,128)(2,1)S(1)}, bf16[512,384]{1,0:T(8,128)(2,1)S(1)}, u32[]{:S(2)}, u32[]{:S(2)}) collective-permute-start(bf16[512,384]{1,0:T(8,128)(2,1)S(1)} %copy-done), channel_id=1, source_target_pairs={{0,4},{4,0},{1,5},{5,1},{2,6},{6,2},{3,7},{7,3},{8,12},{12,8},{9,1... | collective-permute-start | bytes 1179656 | tf_op jit(solution)/shard_map/ppermute | solution.py:200
  21.7 3.1 %collective-permute-start.3 = (bf16[32,768]{1,0:T(8,128)(2,1)S(1)}, bf16[32,768]{1,0:T(8,128)(2,1)S(1)}, u32[]{:S(2)}, u32[]{:S(2)}) collective-permute-start(bf16[32,768]{1,0:T(8,128)(2,1)S(1)} %norm.1), channel_id=1, source_target_pairs={{0,32},{32,0},{1,33},{33,1},{2,34},{34,2},{3,35},{35,3},{4,36},{36... | collective-permute-start | bytes 147464 | tf_op jit(solution)/shard_map/ppermute | solution.py:200
  24.8 4.8 %collective-permute-start.5 = (bf16[64,768]{1,0:T(8,128)(2,1)S(1)}, bf16[64,768]{1,0:T(8,128)(2,1)S(1)}, u32[]{:S(2)}, u32[]{:S(2)}) collective-permute-start(bf16[64,768]{1,0:T(8,128)(2,1)S(1)} %get-tuple-element.59), channel_id=1, source_target_pairs={{0,8},{8,16},{16,24},{24,0},{1,9},{9,17},{17,25},{25,1},{2,10},{10... | collective-permute-start | bytes 294920 | tf_op jit(solution)/shard_map/ppermute | solution.py:200
  25.2 7.3 %collective-permute-start.8 = (bf16[64,768]{1,0:T(8,128)(2,1)S(1)}, bf16[64,768]{1,0:T(8,128)(2,1)S(1)}, u32[]{:S(2)}, u32[]{:S(2)}) collective-permute-start(bf16[64,768]{1,0:T(8,128)(2,1)S(1)} %get-tuple-element.59), channel_id=1, source_target_pairs={{0,24},{8,0},{16,8},{24,16},{1,25},{9,1},{17,9},{25,17},{2,26},{10... | collective-permute-start | bytes 294920 | tf_op jit(solution)/shard_map/ppermute | solution.py:200
  27.6 5.0 %collective-permute-start.9 = (bf16[64,768]{1,0:T(8,128)(2,1)S(1)}, bf16[64,768]{1,0:T(8,128)(2,1)S(1)}, u32[]{:S(2)}, u32[]{:S(2)}) collective-permute-start(bf16[64,768]{1,0:T(8,128)(2,1)S(1)} %get-tuple-element.59), channel_id=1, source_target_pairs={{0,16},{8,24},{16,0},{24,8},{1,17},{9,25},{17,1},{25,9},{2,18},{10... | collective-permute-start | bytes 294920 | tf_op jit(solution)/shard_map/ppermute | solution.py:200
  29.6 11.8 %collective-permute-start.13 = (bf16[256,768]{1,0:T(8,128)(2,1)S(1)}, bf16[256,768]{1,0:T(8,128)(2,1)S(1)}, u32[]{:S(2)}, u32[]{:S(2)}) collective-permute-start(bf16[256,768]{1,0:T(8,128)(2,1)S(1)} %slice.6), channel_id=1, source_target_pairs={{0,8},{8,16},{16,24},{24,0},{1,9},{9,17},{17,25},{25,1},{2,10},{10... | collective-permute-start | bytes 1179656 | tf_op jit(solution)/shard_map/ppermute | solution.py:200
  29.7 11.7 %collective-permute-start.14 = (bf16[256,768]{1,0:T(8,128)(2,1)S(1)}, bf16[256,768]{1,0:T(8,128)(2,1)S(1)}, u32[]{:S(2)}, u32[]{:S(2)}) collective-permute-start(bf16[256,768]{1,0:T(8,128)(2,1)S(1)} %slice.7), channel_id=1, source_target_pairs={{0,24},{8,0},{16,8},{24,16},{1,25},{9,1},{17,9},{25,17},{2,26},{10... | collective-permute-start | bytes 1179656 | tf_op jit(solution)/shard_map/ppermute | solution.py:200
  32.6 15.8 %collective-permute-start.10 = (bf16[256,768]{1,0:T(8,128)(2,1)S(1)}, bf16[256,768]{1,0:T(8,128)(2,1)S(1)}, u32[]{:S(2)}, u32[]{:S(2)}) collective-permute-start(bf16[256,768]{1,0:T(8,128)(2,1)S(1)} %constant_dynamic-update-slice_fusion.2.refs_3_), channel_id=1, source_target_pairs={{0,64},{64,128},{128,192},{192,0},{1,65},{65,129},{129,193},{193,1... | collective-permute-start | bytes 1179656 | tf_op jit(solution)/shard_map/ppermute | solution.py:200
  33.8 14.5 %collective-permute-start.11 = (bf16[256,768]{1,0:T(8,128)(2,1)S(1)}, bf16[256,768]{1,0:T(8,128)(2,1)S(1)}, u32[]{:S(2)}, u32[]{:S(2)}) collective-permute-start(bf16[256,768]{1,0:T(8,128)(2,1)S(1)} %constant_dynamic-update-slice_fusion.2.refs_3_), channel_id=1, source_target_pairs={{0,192},{64,0},{128,64},{192,128},{1,193},{65,1},{129,65},{193,129... | collective-permute-start | bytes 1179656 | tf_op jit(solution)/shard_map/ppermute | solution.py:200
  35.3 14.3 %collective-permute-start.12 = (bf16[256,768]{1,0:T(8,128)(2,1)S(1)}, bf16[256,768]{1,0:T(8,128)(2,1)S(1)}, u32[]{:S(2)}, u32[]{:S(2)}) collective-permute-start(bf16[256,768]{1,0:T(8,128)(2,1)S(1)} %constant_dynamic-update-slice_fusion.2.refs_3_), channel_id=1, source_target_pairs={{0,128},{64,192},{128,0},{192,64},{1,129},{65,193},{129,1},{193,65... | collective-permute-start | bytes 1179656 | tf_op jit(solution)/shard_map/ppermute | solution.py:200
  52.7 7.5 %collective-permute-start.15 = (f32[512,512]{1,0:T(8,128)S(1)}, f32[512,512]{1,0:T(8,128)S(1)}, u32[]{:S(2)}, u32[]{:S(2)}) collective-permute-start(f32[512,512]{1,0:T(8,128)S(1)} %join.3), channel_id=1, source_target_pairs={{0,4},{4,0},{1,5},{5,1},{2,6},{6,2},{3,7},{7,3},{8,12},{12,8},{9,1... | collective-permute-start | bytes 3145736 | tf_op jit(solution)/shard_map/ppermute | solution.py:200
